TPU v7x, 128 devices: a whole 4x4x4 slice. The times are simulated.
128 devices in a mesh: gx: 8 (over y, core), gy: 16 (over z, x).
Axes of the slice: x: 4, y: 4, z: 4, core: 2. Of those that a mesh axis runs over, the one named last changes fastest.
Arguments:
- volume_sens: float32 [3, 256, 512, 128], P(None, 'gx', 'gy'), may hold values from -6 to 6
- stiffness: float32 [256, 512, 128], P('gx', 'gy'), may hold values from 0.25 to 4
- patch_of_row: int32 [128, 1024, 1], P(('gx', 'gy')), may hold values from 0 to 127; in each aligned block of 1024 rows (0 to 1023, 1024 to 2047, ..., all dimensions but the last counted through in order) at most 32 rows name the same one
- knot_spans: int32 [128, 1024, 2], P(('gx', 'gy')), may hold values from 0 to 60
- span_params: float32 [128, 1024, 2], P(('gx', 'gy')), may hold values from 0 to 1
Outputs:
- adjoint_field: float32 [3, 256, 512, 128], P(None, 'gx', 'gy')
- control_grad: float32 [128, 3, 64, 64], P(('gx', 'gy'))
Inputs may be any that keep to these rules, and one draw needn't show every extreme that they name: `patch_of_row`: the surface nodes of one device name any one patch at most 32 times; in every draw some device names some patch exactly 32 times.
All inputs are finite; a program needn't handle non-finite values.
Results may differ from a plain program's by a relative error of at most 0.000092.
Values sent between devices are 32-bit elements; how exact they have to be, the bound alone decides.
No kernel may reach another device: no remote copies, remote signals or barrier semaphores. Data moves between devices by JAX's collectives and lax.ppermute only.
A program may use at most 192 MiB of HBM per device.

v0:
```python
import jax
import jax.numpy as jnp
from jax import lax
from jax.sharding import PartitionSpec as P

SWEEPS = 3
NC = 64


omega_relax = 2.0 / 3.0


def with_halo(cells, sides, width):
    for axis, dim in sides:
        count = lax.axis_size(axis)
        ends = count - 1
        head = lax.slice_in_dim(cells, 0, width, axis=dim)
        tail = lax.slice_in_dim(cells, cells.shape[dim] - width, cells.shape[dim], axis=dim)
        cells = jnp.concatenate(
            [
                lax.ppermute(tail, axis, [(i, (i + 1) % count) for i in range(ends)]),
                cells,
                lax.ppermute(head, axis, [((i + 1) % count, i) for i in range(ends)]),
            ],
            axis=dim,
        )
    return cells


def six_sides(padded):
    return [
        padded[..., 2:, 1:-1, 1:-1],
        padded[..., :-2, 1:-1, 1:-1],
        padded[..., 1:-1, 2:, 1:-1],
        padded[..., 1:-1, :-2, 1:-1],
        padded[..., 1:-1, 1:-1, 2:],
        padded[..., 1:-1, 1:-1, :-2],
    ]


def pad_vertical(array):
    widths = [(0, 0)] * (array.ndim - 1) + [(1, 1)]
    return jnp.pad(array, widths)


def face_weights(center, stiff_pad):
    weights = [(center + side) * 0.5 for side in six_sides(stiff_pad)]
    diag = weights[0] + weights[1] + weights[2] + weights[3] + weights[4] + weights[5]
    return (weights, diag)


def neighbour_total(weights, scaled_pad):
    sides = six_sides(scaled_pad)
    total = weights[0][None] * sides[0]
    for index in range(1, 6):
        total = total + weights[index][None] * sides[index]
    return total


def pieces(param):
    other = 1.0 - param
    return [
        other * other * other / 6.0,
        (3.0 * param**3 - 6.0 * param * param + 4.0) / 6.0,
        (-3.0 * param**3 + 3.0 * param * param + 3.0 * param + 1.0) / 6.0,
        param**3 / 6.0,
    ]


def spline_rows(spans, param, width):
    offset = jnp.arange(width, dtype=jnp.float32)[None, None, :] - spans[:, :, None]
    basis = pieces(param)
    rows = jnp.zeros(offset.shape, jnp.float32)
    for index in range(4):
        rows = rows + jnp.where(offset == float(index), basis[index][:, :, None], 0.0)
    return rows


def contrib(floats, width):
    basis_u = spline_rows(floats[5], floats[3], width)
    basis_v = spline_rows(floats[6], floats[4], width)
    values = jnp.transpose(floats[:3], (1, 0, 2))
    left = values[:, :, :, None] * basis_u[:, None]
    return jnp.einsum(
        "pkrm,prn->pkmn",
        left,
        basis_v,
        precision=lax.Precision.HIGHEST,
        preferred_element_type=jnp.float32,
    )


def body(volume_sens, stiffness, patch_of_row, knot_spans, span_params):
    stiff_pad = pad_vertical(with_halo(stiffness, (("gx", 0), ("gy", 1)), 1))
    weights, diag = face_weights(stiffness, stiff_pad)
    field = volume_sens
    for sweep in range(SWEEPS):
        scaled = field / diag[None]
        scaled_pad = pad_vertical(with_halo(scaled, (("gx", 1), ("gy", 2)), 1))
        field = (
            volume_sens
            + (1.0 - omega_relax) * field
            + omega_relax * neighbour_total(weights, scaled_pad)
        )
    surface = omega_relax * field[:, :, :, 0] / diag[None, :, :, 0]
    row_count = surface.shape[1] * surface.shape[2]
    surface = surface.reshape(3, row_count)
    devices_all = lax.axis_size("gx") * lax.axis_size("gy")
    capacity = 4 * row_count // devices_all
    patch = patch_of_row[0, :, 0]
    one_hot = (patch[:, None] == jnp.arange(devices_all, dtype=jnp.int32)[None, :]).astype(
        jnp.int32
    )
    rank = jnp.sum(jnp.cumsum(one_hot, axis=0) * one_hot, axis=1) - 1
    slot = patch * capacity + rank
    packed = jnp.concatenate(
        [surface, span_params[0].T, knot_spans[0].T.astype(jnp.float32)], axis=0
    )
    buffer = jnp.zeros((7, devices_all * capacity), jnp.float32).at[:, slot].set(packed)
    grouped = buffer.reshape(7, devices_all, capacity)
    grads = lax.psum_scatter(contrib(grouped, NC), ("gx", "gy"), scatter_dimension=0, tiled=True)
    return (field, grads)


def solution(mesh):
    placed = (
        P(None, "gx", "gy", None),
        P("gx", "gy", None),
        P(("gx", "gy"), None, None),
        P(("gx", "gy"), None, None),
        P(("gx", "gy"), None, None),
    )
    return jax.shard_map(
        body,
        mesh=mesh,
        in_specs=placed,
        out_specs=(P(None, "gx", "gy", None), P(("gx", "gy"), None, None, None)),
        check_vma=False,
    )
```

profile of v0, /device:TPU:1, one launch (start us, length us, event | category | flops | bytes accessed | tf_op | source)
XLA Modules:
  0.0 375.5 jit_solution(5617851888141342408)
XLA Ops:
  7.2 0.7 fusion.117
  7.9 3.3 collective-permute-start
  11.3 3.2 collective-permute-start.1
  14.5 0.8 copy.16
  15.3 0.2 fusion.82
  15.5 1.3 constant_dynamic-update-slice_fusion.1
  16.8 3.1 collective-permute-start.3
  20.0 1.3 collective-permute-start.2
  21.3 3.6 collective-permute-done.2
  24.9 0.6 select_maximum_fusion.12
  25.5 0.6 add_add_fusion
  26.2 0.7 copy-done
  26.9 0.2 broadcast_divide_fusion.2
  27.2 5.0 %collective-permute-start.5 = (f32[3,1,32,128]{3,2,1,0:T(8,128)S(1)}, f32[3,1,32,128]{3,2,1,0:T(8,128)S(1)}, u32[]{:S(2)}, u32[]{:S(2)}) collective-permute-start(f32[3,1,32,128]{3,2,1,0:T(8,128)S(1)} %get-tuple-element.27), channel_id=1, source_target_pairs={{0,16},{16,32},{32,48},{48,64},{64,80},{80,96},{96,112},{1,17},{17... | collective-permute-start | bytes 147464 | tf_op jit(solution)/shard_map/ppermute | solution.py:21
  32.2 1.9 collective-permute-start.4
  34.2 3.4 collective-permute-done.4
  37.6 0.1 pad_maximum_fusion.34
  37.7 3.1 collective-permute-start.7
  40.8 1.3 collective-permute-start.6
  42.1 0.1 copy.17
  42.3 3.4 collective-permute-done.6
  45.7 3.6 select_maximum_fusion.8
  49.3 3.0 broadcast_divide_fusion.1
  52.3 3.5 collective-permute-start.9
  55.8 1.9 collective-permute-start.8
  57.7 0.4 fusion.81
  58.1 3.1 collective-permute-done.8
  61.2 0.1 pad_maximum_fusion.31
  61.3 4.6 %collective-permute-start.11 = (f32[3,34,1,128]{3,2,1,0:T(1,128)S(1)}, f32[3,34,1,128]{3,2,1,0:T(1,128)S(1)}, u32[]{:S(2)}, u32[]{:S(2)}) collective-permute-start(f32[3,34,1,128]{3,2,1,0:T(1,128)S(1)} %get-tuple-element.19), channel_id=1, source_target_pairs={{0,1},{1,2},{2,3},{3,4},{4,5},{5,6},{6,7},{7,8},{8,9},{9,10},{10,1... | collective-permute-start | bytes 156680 | tf_op jit(solution)/shard_map/ppermute | solution.py:21
  65.9 1.3 collective-permute-start.10
  67.2 4.0 %collective-permute-done.10 = f32[3,34,1,128]{3,2,1,0:T(1,128)S(1)} collective-permute-done((f32[3,34,1,128]{3,2,1,0:T(1,128)S(1)}, f32[3,34,1,128]{3,2,1,0:T(1,128)S(1)}, u32[]{:S(2)}, u32[]{:S(2)}) %collective-permute-start.10) | collective-permute-done | bytes 52256 | tf_op jit(solution)/shard_map/ppermute | solution.py:23
  71.2 3.6 select_maximum_fusion.4
  74.9 4.0 %broadcast_divide_fusion = (f32[3,32,32,128]{3,2,1,0:T(8,128)S(1)}, f32[3,32,32,128]{3,2,1,0:T(8,128)}) fusion(f32[32,32,128]{2,1,0:T(8,128)S(1)} %get-tuple-element.10, f32[3,34,34,130]{3,2,1,0:T(8,128)S(1)} %select_maximum_fusion.4, f32[32,32,128]{2,1,0:T(8,128)S(1)} %get-tuple-element.16, f32[32,32,128]{2,1,0:T(8,128)S(1)} %get-tuple-element.15, ...), kind=kLoop, calls=%fused_computation.125 | loop fusion | flops 9437184 | bytes 14882816 | tf_op jit(solution)/shard_map/div | solution.py:98
  78.8 3.0 collective-permute-start.13
  81.9 1.9 collective-permute-start.12
  83.8 3.5 collective-permute-done.12
  87.3 0.1 pad_maximum_fusion.28
  87.4 3.6 collective-permute-start.15
  91.0 1.5 collective-permute-start.14
  92.5 0.2 slice_reduce_fusion.4
  92.8 3.4 collective-permute-done.14
  96.3 3.6 select_maximum_fusion
  99.9 2.9 fusion.29
  102.8 1.1 copy-done.14
  104.0 0.5 fusion.26
  104.4 0.1 mul.354
  104.6 0.1 copy-done.21
  104.7 0.2 copy.18
  104.9 3.6 scatter_custom_fusion
  108.5 4.4 %slice_reduce_fusion.1 = (f32[4096]{0:T(1024)S(1)}, f32[4096]{0:T(1024)S(1)}, f32[4096]{0:T(1024)S(1)}, f32[4096]{0:T(1024)S(1)}) fusion(f32[7,4096]{0,1:T(8,128)S(1)} %scatter_custom_fusion), kind=kLoop, calls=%fused_computation.22 | loop fusion | bytes 131072 | tf_op jit(solution)/shard_map/slice | solution.py:81
  112.9 0.1 sub.77
  113.2 0.1 copy.33
  113.3 0.1 copy.39
  113.4 0.1 copy.43
  113.5 0.1 copy.42
  113.6 0.1 squeeze.13
  113.8 0.1 copy.21
  113.9 0.1 copy.27
  114.0 0.1 copy.31
  114.1 0.1 copy.30
  114.2 0.9 copy.19
  115.1 3.1 select_add_fusion
  118.2 27.5 %fusion = f32[128,3,64,64]{3,2,1,0:T(8,128)} fusion(f32[128,32,64]{2,1,0:T(8,128)S(1)} %select_add_fusion, f32[128,3,32]{2,1,0:T(4,128)S(1)} %copy.19, f32[128,32]{1,0:T(8,128)S(1)} %copy.43, f32[128,32]{1,0:T(8,128)S(1)} %copy.42, f32[128,32]{1,0:T(8,128)S(1)} %copy.39, f32[128,32]{1,0:T(8,128)S(1)} %copy.33, f32[128,32]{1,0:T(8,128)S(1)} %sub.77), kind=kOutput, calls=%fused_computation.1 | convolution fusion | flops 607911936 | bytes 7471104 | tf_op jit(solution)/shard_map/pkrm,prn->pkmn/dot_general | solution.py:84
  145.7 223.0 %reduce-scatter.2.cloned.1.call-done = f32[1,3,64,64]{3,2,1,0:T(8,128)} async-done(((f32[128,3,64,64]{3,2,1,0:T(8,128)}), f32[1,3,64,64]{3,2,1,0:T(8,128)}) %reduce-scatter.2.cloned.1.call-update) | async-done | bytes 49168 | tf_op jit(solution)/shard_map/reduce_scatter | solution.py:121
  (75 shorter events, 0.8 us)
Async XLA Ops:
  7.2 361.5 %reduce-scatter.2.cloned.1.call-start = ((), (), s32[]{:S(2)}) async-start(), calls=%async_computation.1 | async-start | bytes 12681216 | tf_op jit(solution)/shard_map/reduce_scatter | solution.py:121
  7.9 8.8 %collective-permute-start = (f32[1,32,128]{2,1,0:T(8,128)S(1)}, f32[1,32,128]{2,1,0:T(8,128)S(1)}, u32[]{:S(2)}, u32[]{:S(2)}) collective-permute-start(f32[1,32,128]{2,1,0:T(8,128)S(1)} %get-tuple-element.31), channel_id=1, source_target_pairs={{16,0},{32,16},{48,32},{64,48},{80,64},{96,80},{112,96},{17,1},{33... | collective-permute-start | bytes 49160 | tf_op jit(solution)/shard_map/ppermute | solution.py:23
  11.3 4.2 %collective-permute-start.1 = (f32[1,32,128]{2,1,0:T(8,128)S(1)}, f32[1,32,128]{2,1,0:T(8,128)S(1)}, u32[]{:S(2)}, u32[]{:S(2)}) collective-permute-start(f32[1,32,128]{2,1,0:T(8,128)S(1)} %get-tuple-element.32), channel_id=1, source_target_pairs={{0,16},{16,32},{32,48},{48,64},{64,80},{80,96},{96,112},{1,17},{17... | collective-permute-start | bytes 49160 | tf_op jit(solution)/shard_map/ppermute | solution.py:21
  15.5 5.8 %copy-start.16 = (s32[128,8,128]{0,1,2:T(8,128)}, s32[128,8,128]{0,1,2:T(8,128)S(1)}, u32[]{:S(2)}) copy-start(s32[128,8,128]{0,1,2:T(8,128)S(1)} %fusion.82) | copy-start | bytes 1572868
  15.5 10.0 %copy-start.15 = (f32[32,32,128]{2,1,0:T(8,128)S(1)}, f32[32,32,128]{2,1,0:T(8,128)}, u32[]{:S(2)}) copy-start(f32[32,32,128]{2,1,0:T(8,128)} %param.6) | copy-start | bytes 1572868
  16.8 4.5 %collective-permute-start.3 = (f32[34,1,128]{2,1,0:T(1,128)S(1)}, f32[34,1,128]{2,1,0:T(1,128)S(1)}, u32[]{:S(2)}, u32[]{:S(2)}) collective-permute-start(f32[34,1,128]{2,1,0:T(1,128)S(1)} %get-tuple-element.29), channel_id=1, source_target_pairs={{0,1},{1,2},{2,3},{3,4},{4,5},{5,6},{6,7},{7,8},{8,9},{9,10},{10,1... | collective-permute-start | bytes 52232 | tf_op jit(solution)/shard_map/ppermute | solution.py:21
  20.0 4.9 %collective-permute-start.2 = (f32[34,1,128]{2,1,0:T(1,128)S(1)}, f32[34,1,128]{2,1,0:T(1,128)S(1)}, u32[]{:S(2)}, u32[]{:S(2)}) collective-permute-start(f32[34,1,128]{2,1,0:T(1,128)S(1)} %get-tuple-element.30), channel_id=1, source_target_pairs={{1,0},{2,1},{3,2},{4,3},{5,4},{6,5},{7,6},{8,7},{9,8},{10,9},{11,1... | collective-permute-start | bytes 52232 | tf_op jit(solution)/shard_map/ppermute | solution.py:23
  21.3 4.8 %copy-start.19 = (s32[128,9]{0,1:T(8,128)}, s32[128,9]{0,1:T(8,128)S(1)}, u32[]{:S(2)}) copy-start(s32[128,9]{0,1:T(8,128)S(1)} %reduce-window.9) | copy-start | bytes 13828
  25.5 1.4 copy-start
  26.1 48.7 %copy-start.1 = (f32[32,32,128]{2,1,0:T(8,128)}, f32[32,32,128]{2,1,0:T(8,128)S(1)}, u32[]{:S(2)}) copy-start(f32[32,32,128]{2,1,0:T(8,128)S(1)} %get-tuple-element.11) | copy-start | bytes 1572868
  26.1 48.7 %copy-start.3 = (f32[32,32,128]{2,1,0:T(8,128)}, f32[32,32,128]{2,1,0:T(8,128)S(1)}, u32[]{:S(2)}) copy-start(f32[32,32,128]{2,1,0:T(8,128)S(1)} %get-tuple-element.12) | copy-start | bytes 1572868
  26.2 48.7 %copy-start.5 = (f32[32,32,128]{2,1,0:T(8,128)}, f32[32,32,128]{2,1,0:T(8,128)S(1)}, u32[]{:S(2)}) copy-start(f32[32,32,128]{2,1,0:T(8,128)S(1)} %get-tuple-element.13) | copy-start | bytes 1572868
  26.2 48.7 %copy-start.7 = (f32[32,32,128]{2,1,0:T(8,128)}, f32[32,32,128]{2,1,0:T(8,128)S(1)}, u32[]{:S(2)}) copy-start(f32[32,32,128]{2,1,0:T(8,128)S(1)} %get-tuple-element.14) | copy-start | bytes 1572868
  26.2 48.7 %copy-start.9 = (f32[32,32,128]{2,1,0:T(8,128)}, f32[32,32,128]{2,1,0:T(8,128)S(1)}, u32[]{:S(2)}) copy-start(f32[32,32,128]{2,1,0:T(8,128)S(1)} %get-tuple-element.15) | copy-start | bytes 1572868
  26.2 48.7 %copy-start.11 = (f32[32,32,128]{2,1,0:T(8,128)}, f32[32,32,128]{2,1,0:T(8,128)S(1)}, u32[]{:S(2)}) copy-start(f32[32,32,128]{2,1,0:T(8,128)S(1)} %get-tuple-element.16) | copy-start | bytes 1572868
  26.9 7.2 %copy-start.17 = (s32[128,8,128]{0,1,2:T(8,128)S(1)}, s32[128,8,128]{0,1,2:T(8,128)}, u32[]{:S(2)}) copy-start(s32[128,8,128]{0,1,2:T(8,128)} %copy-done.16) | copy-start | bytes 1572868
  26.9 7.2 %slice-start = ((s32[128,9]{0,1:T(8,128)}), s32[128,8]{0,1:T(8,128)S(1)}, s32[]{:S(2)}) async-start(s32[128,9]{0,1:T(8,128)} %copy-done.19), calls=%async_computation.2 | async-start | bytes 8192 | tf_op jit(solution)/shard_map/slice.1
  27.1 15.0 %copy-start.20 = (s32[1,1024,2]{1,2,0:T(2,128)S(1)}, s32[1,1024,2]{1,2,0:T(2,128)}, u32[]{:S(2)}) copy-start(s32[1,1024,2]{1,2,0:T(2,128)} %param.8) | copy-start | bytes 24580
  27.2 7.0 %collective-permute-start.5 = (f32[3,1,32,128]{3,2,1,0:T(8,128)S(1)}, f32[3,1,32,128]{3,2,1,0:T(8,128)S(1)}, u32[]{:S(2)}, u32[]{:S(2)}) collective-permute-start(f32[3,1,32,128]{3,2,1,0:T(8,128)S(1)} %get-tuple-element.27), channel_id=1, source_target_pairs={{0,16},{16,32},{32,48},{48,64},{64,80},{80,96},{96,112},{1,17},{17... | collective-permute-start | bytes 147464 | tf_op jit(solution)/shard_map/ppermute | solution.py:21
  32.2 5.4 %collective-permute-start.4 = (f32[3,1,32,128]{3,2,1,0:T(8,128)S(1)}, f32[3,1,32,128]{3,2,1,0:T(8,128)S(1)}, u32[]{:S(2)}, u32[]{:S(2)}) collective-permute-start(f32[3,1,32,128]{3,2,1,0:T(8,128)S(1)} %get-tuple-element.28), channel_id=1, source_target_pairs={{16,0},{32,16},{48,32},{64,48},{80,64},{96,80},{112,96},{17,1},{33... | collective-permute-start | bytes 147464 | tf_op jit(solution)/shard_map/ppermute | solution.py:23
  37.7 4.6 %collective-permute-start.7 = (f32[3,34,1,128]{3,2,1,0:T(1,128)S(1)}, f32[3,34,1,128]{3,2,1,0:T(1,128)S(1)}, u32[]{:S(2)}, u32[]{:S(2)}) collective-permute-start(f32[3,34,1,128]{3,2,1,0:T(1,128)S(1)} %get-tuple-element.21), channel_id=1, source_target_pairs={{0,1},{1,2},{2,3},{3,4},{4,5},{5,6},{6,7},{7,8},{8,9},{9,10},{10,1... | collective-permute-start | bytes 156680 | tf_op jit(solution)/shard_map/ppermute | solution.py:21
  40.8 4.9 %collective-permute-start.6 = (f32[3,34,1,128]{3,2,1,0:T(1,128)S(1)}, f32[3,34,1,128]{3,2,1,0:T(1,128)S(1)}, u32[]{:S(2)}, u32[]{:S(2)}) collective-permute-start(f32[3,34,1,128]{3,2,1,0:T(1,128)S(1)} %get-tuple-element.22), channel_id=1, source_target_pairs={{1,0},{2,1},{3,2},{4,3},{5,4},{6,5},{7,6},{8,7},{9,8},{10,9},{11,1... | collective-permute-start | bytes 156680 | tf_op jit(solution)/shard_map/ppermute | solution.py:23
  49.3 8.5 %copy-start.18 = (s32[1,1024,1]{1,2,0:T(1,128)S(1)}, s32[1,1024,1]{1,2,0:T(1,128)}, u32[]{:S(2)}) copy-start(s32[1,1024,1]{1,2,0:T(1,128)} %param.7) | copy-start | bytes 12292
  52.3 5.8 %collective-permute-start.9 = (f32[3,1,32,128]{3,2,1,0:T(8,128)S(1)}, f32[3,1,32,128]{3,2,1,0:T(8,128)S(1)}, u32[]{:S(2)}, u32[]{:S(2)}) collective-permute-start(f32[3,1,32,128]{3,2,1,0:T(8,128)S(1)} %get-tuple-element.25), channel_id=1, source_target_pairs={{0,16},{16,32},{32,48},{48,64},{64,80},{80,96},{96,112},{1,17},{17... | collective-permute-start | bytes 147464 | tf_op jit(solution)/shard_map/ppermute | solution.py:21
  55.8 5.4 %collective-permute-start.8 = (f32[3,1,32,128]{3,2,1,0:T(8,128)S(1)}, f32[3,1,32,128]{3,2,1,0:T(8,128)S(1)}, u32[]{:S(2)}, u32[]{:S(2)}) collective-permute-start(f32[3,1,32,128]{3,2,1,0:T(8,128)S(1)} %get-tuple-element.26), channel_id=1, source_target_pairs={{16,0},{32,16},{48,32},{64,48},{80,64},{96,80},{112,96},{17,1},{33... | collective-permute-start | bytes 147464 | tf_op jit(solution)/shard_map/ppermute | solution.py:23
  61.3 5.9 %collective-permute-start.11 = (f32[3,34,1,128]{3,2,1,0:T(1,128)S(1)}, f32[3,34,1,128]{3,2,1,0:T(1,128)S(1)}, u32[]{:S(2)}, u32[]{:S(2)}) collective-permute-start(f32[3,34,1,128]{3,2,1,0:T(1,128)S(1)} %get-tuple-element.19), channel_id=1, source_target_pairs={{0,1},{1,2},{2,3},{3,4},{4,5},{5,6},{6,7},{7,8},{8,9},{9,10},{10,1... | collective-permute-start | bytes 156680 | tf_op jit(solution)/shard_map/ppermute | solution.py:21
  65.9 5.3 %collective-permute-start.10 = (f32[3,34,1,128]{3,2,1,0:T(1,128)S(1)}, f32[3,34,1,128]{3,2,1,0:T(1,128)S(1)}, u32[]{:S(2)}, u32[]{:S(2)}) collective-permute-start(f32[3,34,1,128]{3,2,1,0:T(1,128)S(1)} %get-tuple-element.20), channel_id=1, source_target_pairs={{1,0},{2,1},{3,2},{4,3},{5,4},{6,5},{7,6},{8,7},{9,8},{10,9},{11,1... | collective-permute-start | bytes 156680 | tf_op jit(solution)/shard_map/ppermute | solution.py:23
  78.8 5.0 %collective-permute-start.13 = (f32[3,1,32,128]{3,2,1,0:T(8,128)S(1)}, f32[3,1,32,128]{3,2,1,0:T(8,128)S(1)}, u32[]{:S(2)}, u32[]{:S(2)}) collective-permute-start(f32[3,1,32,128]{3,2,1,0:T(8,128)S(1)} %get-tuple-element.23), channel_id=1, source_target_pairs={{0,16},{16,32},{32,48},{48,64},{64,80},{80,96},{96,112},{1,17},{17... | collective-permute-start | bytes 147464 | tf_op jit(solution)/shard_map/ppermute | solution.py:21
  81.9 5.4 %collective-permute-start.12 = (f32[3,1,32,128]{3,2,1,0:T(8,128)S(1)}, f32[3,1,32,128]{3,2,1,0:T(8,128)S(1)}, u32[]{:S(2)}, u32[]{:S(2)}) collective-permute-start(f32[3,1,32,128]{3,2,1,0:T(8,128)S(1)} %get-tuple-element.24), channel_id=1, source_target_pairs={{16,0},{32,16},{48,32},{64,48},{80,64},{96,80},{112,96},{17,1},{33... | collective-permute-start | bytes 147464 | tf_op jit(solution)/shard_map/ppermute | solution.py:23
  87.4 5.5 %collective-permute-start.15 = (f32[3,34,1,128]{3,2,1,0:T(1,128)S(1)}, f32[3,34,1,128]{3,2,1,0:T(1,128)S(1)}, u32[]{:S(2)}, u32[]{:S(2)}) collective-permute-start(f32[3,34,1,128]{3,2,1,0:T(1,128)S(1)} %get-tuple-element.17), channel_id=1, source_target_pairs={{0,1},{1,2},{2,3},{3,4},{4,5},{5,6},{6,7},{7,8},{8,9},{9,10},{10,1... | collective-permute-start | bytes 156680 | tf_op jit(solution)/shard_map/ppermute | solution.py:21
  91.0 5.3 %collective-permute-start.14 = (f32[3,34,1,128]{3,2,1,0:T(1,128)S(1)}, f32[3,34,1,128]{3,2,1,0:T(1,128)S(1)}, u32[]{:S(2)}, u32[]{:S(2)}) collective-permute-start(f32[3,34,1,128]{3,2,1,0:T(1,128)S(1)} %get-tuple-element.18), channel_id=1, source_target_pairs={{1,0},{2,1},{3,2},{4,3},{5,4},{6,5},{7,6},{8,7},{9,8},{10,9},{11,1... | collective-permute-start | bytes 156680 | tf_op jit(solution)/shard_map/ppermute | solution.py:23
  92.8 7.1 %copy-start.2 = (f32[32,32,128]{2,1,0:T(8,128)S(1)}, f32[32,32,128]{2,1,0:T(8,128)}, u32[]{:S(2)}) copy-start(f32[32,32,128]{2,1,0:T(8,128)} %copy-done.1) | copy-start | bytes 1572868
  92.8 7.1 %copy-start.4 = (f32[32,32,128]{2,1,0:T(8,128)S(1)}, f32[32,32,128]{2,1,0:T(8,128)}, u32[]{:S(2)}) copy-start(f32[32,32,128]{2,1,0:T(8,128)} %copy-done.3) | copy-start | bytes 1572868
  92.8 7.1 %copy-start.6 = (f32[32,32,128]{2,1,0:T(8,128)S(1)}, f32[32,32,128]{2,1,0:T(8,128)}, u32[]{:S(2)}) copy-start(f32[32,32,128]{2,1,0:T(8,128)} %copy-done.5) | copy-start | bytes 1572868
  92.8 7.1 %copy-start.8 = (f32[32,32,128]{2,1,0:T(8,128)S(1)}, f32[32,32,128]{2,1,0:T(8,128)}, u32[]{:S(2)}) copy-start(f32[32,32,128]{2,1,0:T(8,128)} %copy-done.7) | copy-start | bytes 1572868
  92.8 7.1 %copy-start.10 = (f32[32,32,128]{2,1,0:T(8,128)S(1)}, f32[32,32,128]{2,1,0:T(8,128)}, u32[]{:S(2)}) copy-start(f32[32,32,128]{2,1,0:T(8,128)} %copy-done.9) | copy-start | bytes 1572868
  92.8 7.1 %copy-start.12 = (f32[32,32,128]{2,1,0:T(8,128)S(1)}, f32[32,32,128]{2,1,0:T(8,128)}, u32[]{:S(2)}) copy-start(f32[32,32,128]{2,1,0:T(8,128)} %copy-done.11) | copy-start | bytes 1572868
  92.8 7.1 %copy-start.13 = (f32[3,32,32,128]{3,2,1,0:T(8,128)S(1)}, f32[3,32,32,128]{3,2,1,0:T(8,128)}, u32[]{:S(2)}) copy-start(f32[3,32,32,128]{3,2,1,0:T(8,128)} %get-tuple-element.7) | copy-start | bytes 4718596
  102.8 1.1 copy-start.14
  104.0 0.7 copy-start.21
Sparse Core Ops, SparseCore 0:
  145.8 222.8 reduce-scatter.1
where the time goes:
time: 377 us; the launch traced here: 375 us
  waiting for transfers between devices  247 us (66%)
  starting transfers between devices  43.7 us (12%)
  matrix products  27.5 us (7%)
  other arithmetic  26.6 us (7%)
  local copies, waits for them, and re-layouts  15.6 us (4%)
  between operations  14.8 us (4%)
    reduce_scatter x1, waiting for transfers between devices, body(): lax.psum_scatter(contrib(grouped, NC), ('gx', 'gy'), scatter_dimension=0,...  223 us
    ppermute x8, starting transfers between devices, with_halo(): lax.ppermute(tail, axis, [(i, (i + 1) % count) for i in range(ends)])  29.2 us
    dot_general x1, matrix products, contrib(): jnp.einsum('pkrm,prn->pkmn', left, basis_v, precision=lax.Precision.HIGHE...  27.5 us
    ppermute x8, waiting for transfers between devices, with_halo(): lax.ppermute(head, axis, [((i + 1) % count, i) for i in range(ends)])  24.4 us
    ppermute x8, starting transfers between devices, with_halo(): lax.ppermute(head, axis, [((i + 1) % count, i) for i in range(ends)])  14.4 us
    concatenate x7, other arithmetic, with_halo(): jnp.concatenate([lax.ppermute(tail, axis, [(i, (i + 1) % count) for i in...  11.6 us
  transfers between devices with their start and end apart: 17, of which 8 were waited for; matrix products, arithmetic and copies ran while one was open for 1% of the time, Pallas kernels for 0%

commit v1 on v0

v1 whole, which is shorter than its diff:
```python
import jax
import jax.numpy as jnp
from jax import lax
from jax.experimental import pallas as pl
from jax.experimental.pallas import tpu as pltpu
from jax.sharding import PartitionSpec as P

NC = 64
OMEGA = 2.0 / 3.0
KEEP = 1.0 - OMEGA
NX = 32
NY = 32
NZ = 128
ROWS = NX * NY
CAP = 32
DEV = 128
EX = NX + 8
EY = NY + 8
SLAB_V = 36 * 9
SLAB = SLAB_V + 38 * 4 + 4
F32 = jnp.float32
BF16 = jnp.bfloat16
VMEM_LIMIT = 40 * 1024 * 1024


def vmem():
    return pl.BlockSpec(memory_space=pltpu.VMEM)


def params():
    return pltpu.CompilerParams(vmem_limit_bytes=VMEM_LIMIT)


def is_even(axis):
    return lax.rem(lax.axis_index(axis), 2) == 0


def pairings(axis):
    count = lax.axis_size(axis)
    first = [(i, i ^ 1) for i in range(count)]
    second = [(i, ((i + 1) ^ 1) - 1) for i in range(1, count - 1)]
    return first, second


def swap(axis, one, two):
    first, second = pairings(axis)
    return lax.ppermute(one, axis, first), lax.ppermute(two, axis, second)


def two_pieces(x):
    high = x.astype(BF16)
    return high, (x - high.astype(F32)).astype(BF16)


def three_pieces(x):
    high = x.astype(BF16)
    rest = x - high.astype(F32)
    mid = rest.astype(BF16)
    return high, mid, (rest - mid.astype(F32)).astype(BF16)


def dot(a, b):
    return jnp.dot(a, b, preferred_element_type=F32)


def dot_nt(a, b):
    return lax.dot_general(a, b, (((1,), (1,)), ((), ())), preferred_element_type=F32)


def x_message_kernel(vs_lo, vs_hi, c_lo, c_hi, one, two):
    def fill(low, high):
        low[0:9] = vs_lo[:, 0:3].reshape(9, NY, NZ)
        low[9:13] = c_lo[...]
        high[0:9] = vs_hi[:, 1:4].reshape(9, NY, NZ)
        high[9:13] = c_hi[...]

    even = is_even("gx")

    @pl.when(even)
    def _():
        fill(two, one)

    @pl.when(jnp.logical_not(even))
    def _():
        fill(one, two)


def x_messages(vs, c):
    shape = jax.ShapeDtypeStruct((13, NY, NZ), F32)
    return pl.pallas_call(
        x_message_kernel,
        out_shape=(shape, shape),
        grid=(1,),
        in_specs=[
            pl.BlockSpec((3, 4, NY, NZ), lambda i: (0, 0, 0, 0)),
            pl.BlockSpec((3, 4, NY, NZ), lambda i: (0, 7, 0, 0)),
            pl.BlockSpec((4, NY, NZ), lambda i: (0, 0, 0)),
            pl.BlockSpec((4, NY, NZ), lambda i: (7, 0, 0)),
        ],
        out_specs=(
            pl.BlockSpec((13, NY, NZ), lambda i: (0, 0, 0)),
            pl.BlockSpec((13, NY, NZ), lambda i: (0, 0, 0)),
        ),
        name="x_messages",
    )(vs, vs, c, c)


def y_message_kernel(vs_lo, vs_hi, c_lo, c_hi, got_one, got_two, one, two):
    even_x = is_even("gx")
    even_y = is_even("gy")

    def slab(out, vs_ref, c_ref, low, start, x_low, x_high):
        v0 = 0 if low else 5
        c0 = 0 if low else 4
        for i in range(36):
            x = i - 2
            for k in range(3):
                if x < 0:
                    piece = x_low[3 * k + 3 + x, start + v0 : start + v0 + 3]
                elif x < NX:
                    piece = vs_ref[k, x, v0 : v0 + 3]
                else:
                    piece = x_high[3 * k + x - NX, start + v0 : start + v0 + 3]
                out[9 * i + 3 * k : 9 * i + 3 * k + 3] = piece
        for i in range(38):
            x = i - 3
            if x < 0:
                piece = x_low[9 + 4 + x, start + c0 : start + c0 + 4]
            elif x < NX:
                piece = c_ref[x, c0 : c0 + 4]
            else:
                piece = x_high[9 + x - NX, start + c0 : start + c0 + 4]
            out[SLAB_V + 4 * i : SLAB_V + 4 * i + 4] = piece

    def fill(low_out, high_out, x_low, x_high):
        slab(low_out, vs_lo, c_lo, True, 0, x_low, x_high)
        slab(high_out, vs_hi, c_hi, False, 24, x_low, x_high)

    for want_x in (True, False):
        for want_y in (True, False):

            @pl.when(jnp.logical_and(even_x == want_x, even_y == want_y))
            def _():
                x_low, x_high = (got_two, got_one) if want_x else (got_one, got_two)
                low_out, high_out = (two, one) if want_y else (one, two)
                fill(low_out, high_out, x_low, x_high)


def y_messages(vs, c, got_one, got_two):
    shape = jax.ShapeDtypeStruct((SLAB, NZ), F32)
    whole = pl.BlockSpec((13, NY, NZ), lambda i: (0, 0, 0))
    return pl.pallas_call(
        y_message_kernel,
        out_shape=(shape, shape),
        grid=(1,),
        in_specs=[
            pl.BlockSpec((3, NX, 8, NZ), lambda i: (0, 0, 0, 0)),
            pl.BlockSpec((3, NX, 8, NZ), lambda i: (0, 0, 3, 0)),
            pl.BlockSpec((NX, 8, NZ), lambda i: (0, 0, 0)),
            pl.BlockSpec((NX, 8, NZ), lambda i: (0, 3, 0)),
            whole,
            whole,
        ],
        out_specs=(
            pl.BlockSpec((SLAB, NZ), lambda i: (0, 0)),
            pl.BlockSpec((SLAB, NZ), lambda i: (0, 0)),
        ),
        name="y_messages",
    )(vs, vs, c, c, got_one, got_two)


def route_kernel(patch, spans, par, to_patch, to_slot, meta):
    patch_row = patch[...]
    hot = (lax.broadcasted_iota(jnp.int32, (DEV, ROWS), 0) == patch_row).astype(F32)
    hot16 = hot.astype(BF16)
    to_patch[...] = hot16
    upper = (
        lax.broadcasted_iota(jnp.int32, (128, 128), 0)
        <= lax.broadcasted_iota(jnp.int32, (128, 128), 1)
    ).astype(BF16)
    before = jnp.zeros((DEV, 1), F32)
    ranks = []
    for block in range(ROWS // 128):
        part = slice(128 * block, 128 * block + 128)
        count = dot(hot16[:, part], upper) + before
        ranks.append(jnp.sum(count * hot[:, part], axis=0, keepdims=True) - 1.0)
        before = count[:, 127:128]
    rank = jnp.concatenate(ranks, axis=1)
    lane_slot = lax.rem(lax.broadcasted_iota(jnp.int32, (128, ROWS), 0), CAP).astype(F32)
    slot_hot = (lane_slot == rank).astype(F32)
    to_slot[...] = slot_hot.T
    fields = [
        spans[0:1].astype(F32),
        spans[1:2].astype(F32),
        par[0:1],
        par[1:2],
    ]
    spread = jnp.concatenate(
        [slot_hot[CAP * f : CAP * f + CAP] * fields[f] for f in range(4)], axis=0
    )
    high, mid, low = three_pieces(spread)
    meta[...] = dot_nt(hot16, high) + dot_nt(hot16, mid) + dot_nt(hot16, low)


def route(patch, spans, par):
    return pl.pallas_call(
        route_kernel,
        out_shape=(
            jax.ShapeDtypeStruct((DEV, ROWS), BF16),
            jax.ShapeDtypeStruct((ROWS, 128), F32),
            jax.ShapeDtypeStruct((DEV, 128), F32),
        ),
        in_specs=[vmem()] * 3,
        out_specs=(vmem(),) * 3,
        compiler_params=params(),
        cost_estimate=pl.CostEstimate(flops=400_000_000, bytes_accessed=2_000_000, transcendentals=0),
        name="route",
    )(patch, spans, par)


def up(x):
    return pltpu.roll(x, x.shape[0] - 1, 0)


def down(x):
    return pltpu.roll(x, 1, 0)


def sweep_kernel(
    vs, c, xa, xb, ya, yb, to_patch, to_slot, meta, field, send,
    stiff, ratio, wx, wy, wz, y0, y1, y2, spread,
):
    even_x = is_even("gx")
    even_y = is_even("gy")
    for k in range(3):
        y0[k, 4:36, 0:NY] = vs[k]
    stiff[4:36, 0:NY] = c[...]

    def put_x(low, high):
        for k in range(3):
            y0[k, 1:4, 0:NY] = low[3 * k : 3 * k + 3]
            y0[k, 36:39, 0:NY] = high[3 * k : 3 * k + 3]
        stiff[0:4, 0:NY] = low[9:13]
        stiff[36:40, 0:NY] = high[9:13]

    def put_y(low, high):
        for i in range(36):
            for k in range(3):
                row = 9 * i + 3 * k
                y0[k, i + 2, 32:35] = high[row : row + 3]
                y0[k, i + 2, 37:40] = low[row : row + 3]
        for i in range(38):
            row = SLAB_V + 4 * i
            stiff[i + 1, 32:36] = high[row : row + 4]
            stiff[i + 1, 36:40] = low[row : row + 4]

    @pl.when(even_x)
    def _():
        put_x(xb, xa)

    @pl.when(jnp.logical_not(even_x))
    def _():
        put_x(xa, xb)

    @pl.when(even_y)
    def _():
        put_y(yb, ya)

    @pl.when(jnp.logical_not(even_y))
    def _():
        put_y(ya, yb)

    lane = lax.broadcasted_iota(jnp.int32, (EY, NZ), 1)
    not_last = lane < NZ - 1
    not_first = lane > 0

    def prepare(x, carry):
        here = stiff[x]
        after = stiff[x + 1]
        y_next = up(here)
        z_next = jnp.where(not_last, pltpu.roll(here, NZ - 1, 1), 0.0)
        z_prev = jnp.where(not_first, pltpu.roll(here, 1, 1), 0.0)
        sides = (stiff[x - 1] + after) + (y_next + down(here)) + (z_next + z_prev)
        diag = 3.0 * here + 0.5 * sides
        inverse = jnp.where(here > 0.0, 1.0 / diag, 0.0)
        ratio[x] = OMEGA * inverse
        wx[x] = 0.5 * (here + after)
        wy[x] = 0.5 * (here + y_next)
        wz[x] = jnp.where(not_last, 0.5 * (here + z_next), 0.0)
        for k in range(3):
            y0[k, x] = y0[k, x] * inverse
        return carry

    lax.fori_loop(1, 39, prepare, 0)

    def update(source, k, x):
        here = source[k, x]
        face_y = wy[x]
        face_z = wz[x]
        total = wx[x] * source[k, x + 1] + wx[x - 1] * source[k, x - 1]
        total = total + (face_y * up(here) + down(face_y * here))
        total = total + (
            face_z * pltpu.roll(here, NZ - 1, 1) + pltpu.roll(face_z * here, 1, 1)
        )
        return y0[k, x] + KEEP * here + ratio[x] * total

    def sweep(source, target, first, last):
        def step(x, carry):
            for k in range(3):
                target[k, x] = update(source, k, x)
            return carry

        lax.fori_loop(first, last, step, 0)

    sweep(y0, y1, 2, 38)
    sweep(y1, y2, 3, 37)

    lane_field = lax.broadcasted_iota(jnp.int32, (NY, NZ), 1)

    def last_step(x, carry):
        scale = stiff[x]
        sides = (stiff[x - 1] + stiff[x + 1]) + (up(scale) + down(scale))
        z_next = jnp.where(not_last, pltpu.roll(scale, NZ - 1, 1), 0.0)
        z_prev = jnp.where(not_first, pltpu.roll(scale, 1, 1), 0.0)
        diag = (3.0 * scale + 0.5 * (sides + (z_next + z_prev)))[0:NY]
        picked = jnp.zeros((NY, NZ), F32)
        for k in range(3):
            fresh = update(y2, k, x)[0:NY]
            field[k, x - 4] = fresh * diag
            wide = jnp.broadcast_to(fresh[:, 0:1], (NY, NZ))
            picked = jnp.where(lane_field // CAP == k, wide, picked)
        rows = pl.ds(pl.multiple_of((x - 4) * NY, NY), NY)
        spread[rows] = (OMEGA * picked) * to_slot[rows]
        return carry

    lax.fori_loop(4, 36, last_step, 0)
    high, mid, low = three_pieces(spread[...])
    hot = to_patch[...]
    send[:, 0:128] = meta[...]
    send[:, 128:256] = dot(hot, high) + dot(hot, mid) + dot(hot, low)


def sweeps(vs, c, xa, xb, ya, yb, to_patch, to_slot, meta):
    plane = pltpu.VMEM((EX, EY, NZ), F32)
    cube = pltpu.VMEM((3, EX, EY, NZ), F32)
    return pl.pallas_call(
        sweep_kernel,
        out_shape=(
            jax.ShapeDtypeStruct((3, NX, NY, NZ), F32),
            jax.ShapeDtypeStruct((DEV, 256), F32),
        ),
        in_specs=[vmem()] * 9,
        out_specs=(vmem(),) * 2,
        scratch_shapes=[plane] * 5 + [cube] * 3 + [pltpu.VMEM((ROWS, 128), F32)],
        compiler_params=params(),
        cost_estimate=pl.CostEstimate(flops=60_000_000, bytes_accessed=6_000_000, transcendentals=0),
        name="sweeps",
    )(vs, c, xa, xb, ya, yb, to_patch, to_slot, meta)


def pieces(param):
    other = 1.0 - param
    return [
        other * other * other / 6.0,
        (3.0 * param * param * param - 6.0 * param * param + 4.0) / 6.0,
        (-3.0 * param * param * param + 3.0 * param * param + 3.0 * param + 1.0) / 6.0,
        param * param * param / 6.0,
    ]


def gather_kernel(got, grads, table, left, right):
    table[0:128] = got[:, 0:128].T
    table[128:256] = got[:, 128:256].T
    basis_u = pieces(table[64:96])
    basis_v = pieces(table[96:128])
    knot = lax.broadcasted_iota(jnp.int32, (NC, DEV), 0).astype(F32)

    def spline(span, basis, slot):
        offset = knot - table[span + slot : span + slot + 1]
        rows = jnp.zeros((NC, DEV), F32)
        for index in range(4):
            rows = jnp.where(offset == float(index), basis[index][slot : slot + 1], rows)
        return rows

    for slot in range(CAP):
        part = slice(DEV * slot, DEV * slot + DEV)
        along_u = spline(0, basis_u, slot)
        for k in range(3):
            value = table[128 + CAP * k + slot : 128 + CAP * k + slot + 1]
            high, low = two_pieces(along_u * value)
            left[NC * k : NC * k + NC, part] = high
            left[3 * NC + NC * k : 3 * NC + NC * k + NC, part] = low
        high, low = two_pieces(spline(CAP, basis_v, slot))
        right[0:NC, part] = high
        right[NC : 2 * NC, part] = low
    product = dot_nt(left[...], right[...])
    total = product[0 : 3 * NC, 0:NC] + (
        product[0 : 3 * NC, NC : 2 * NC] + product[3 * NC : 6 * NC, 0:NC]
    )
    grads[0] = total.reshape(3, NC, NC)


def gather(got):
    return pl.pallas_call(
        gather_kernel,
        out_shape=jax.ShapeDtypeStruct((1, 3, NC, NC), F32),
        in_specs=[vmem()],
        out_specs=vmem(),
        scratch_shapes=[
            pltpu.VMEM((256, DEV), F32),
            pltpu.VMEM((6 * NC, DEV * CAP), BF16),
            pltpu.VMEM((2 * NC, DEV * CAP), BF16),
        ],
        compiler_params=params(),
        cost_estimate=pl.CostEstimate(flops=400_000_000, bytes_accessed=200_000, transcendentals=0),
        name="gather",
    )(got)


def body(volume_sens, stiffness, patch_of_row, knot_spans, span_params):
    one, two = x_messages(volume_sens, stiffness)
    xa, xb = swap("gx", one, two)
    to_patch, to_slot, meta = route(
        patch_of_row.reshape(1, ROWS), knot_spans[0].T, span_params[0].T
    )
    one, two = y_messages(volume_sens, stiffness, xa, xb)
    ya, yb = swap("gy", one, two)
    field, send = sweeps(volume_sens, stiffness, xa, xb, ya, yb, to_patch, to_slot, meta)
    got = lax.all_to_all(send, ("gx", "gy"), 0, 0, tiled=True)
    return field, gather(got)


def solution(mesh):
    placed = (
        P(None, "gx", "gy", None),
        P("gx", "gy", None),
        P(("gx", "gy"), None, None),
        P(("gx", "gy"), None, None),
        P(("gx", "gy"), None, None),
    )
    return jax.shard_map(
        body,
        mesh=mesh,
        in_specs=placed,
        out_specs=(P(None, "gx", "gy", None), P(("gx", "gy"), None, None, None)),
        check_vma=False,
    )
```

time: 377 us -> 69 us (0.18)
  waiting for transfers between devices: 247 us -> 6.4 us
  starting transfers between devices: 43.7 us -> 6.78 us
  blocking collectives: 0 us -> 27.7 us
  matrix products: 27.5 us -> 0 us
  other arithmetic: 26.6 us -> 0 us
  Pallas kernels: 0 us -> 26.3 us
  local copies, waits for them, and re-layouts: 15.6 us -> 0.86 us
  between operations: 14.8 us -> 0.73 us
    reduce_scatter x1 -> x0, waiting for transfers between devices: 223 us -> none  [body(): lax.psum_scatter(contrib(grouped, NC), ('gx', 'gy'), scatter_dimension=0,...]
    ppermute x16 -> x4, starting transfers between devices: 43.6 us -> 6.78 us  [swap(): return (lax.ppermute(one, axis, first), lax.ppermute(two, axis, second))]
    all_to_all x0 -> x1, blocking collectives: none -> 27.7 us  [body(): got = lax.all_to_all(send, ('gx', 'gy'), 0, 0, tiled=True)]
    dot_general x1 -> x0, matrix products: 27.5 us -> none  [contrib(): jnp.einsum('pkrm,prn->pkmn', left, basis_v, precision=lax.Precision.HIGHE...]
    pallas_call x0 -> x5, Pallas kernels: none -> 26.3 us  [the longest x1 17.9 us: sweeps(): pl.pallas_call(sweep_kernel, out_shape=(jax.ShapeDtypeStruct((3, NX, NY,...]
    ppermute x16 -> x4, waiting for transfers between devices: 24.4 us -> 6.4 us  [swap(): return (lax.ppermute(one, axis, first), lax.ppermute(two, axis, second))]
    concatenate x8 -> x0, other arithmetic: 11.6 us -> none  [the longest x7 11.6 us: with_halo(): jnp.concatenate([lax.ppermute(tail, axis, [(i, (i + 1) % count) for i in...]
    div x6 -> x0, other arithmetic: 7.26 us -> none  [the longest x3 7.16 us: body(): scaled = field / diag[None]]
  transfers between devices with their start and end apart: 17 -> 4, of which waited for: 8 -> 2; matrix products, arithmetic and copies ran while one was open for 1% -> 0% of each run, Pallas kernels for 0% -> 1%
where the time goes in v1:
time: 69 us; the launch traced here: 68.8 us
  blocking collectives  27.7 us (40%)
  Pallas kernels  26.3 us (38%)
  starting transfers between devices  6.78 us (10%)
  waiting for transfers between devices  6.4 us (9%)
  local copies, waits for them, and re-layouts  0.86 us (1%)
  between operations  0.73 us (1%)
    all_to_all x1, blocking collectives, body(): got = lax.all_to_all(send, ('gx', 'gy'), 0, 0, tiled=True)  27.7 us
    pallas_call x1, Pallas kernels, sweeps(): pl.pallas_call(sweep_kernel, out_shape=(jax.ShapeDtypeStruct((3, NX, NY,...  17.9 us
    ppermute x4, starting transfers between devices, swap(): return (lax.ppermute(one, axis, first), lax.ppermute(two, axis, second))  6.78 us
    ppermute x4, waiting for transfers between devices, swap(): return (lax.ppermute(one, axis, first), lax.ppermute(two, axis, second))  6.4 us
    pallas_call x1, Pallas kernels, gather(): pl.pallas_call(gather_kernel, out_shape=jax.ShapeDtypeStruct((1, 3, NC, N...  3.23 us
    pallas_call x1, Pallas kernels, y_messages(): pl.pallas_call(y_message_kernel, out_shape=(shape, shape), grid=(1,), in_...  2.35 us
    pallas_call x1, Pallas kernels, x_messages(): pl.pallas_call(x_message_kernel, out_shape=(shape, shape), grid=(1,), in_...  1.85 us
  transfers between devices with their start and end apart: 4, of which 2 were waited for; matrix products, arithmetic and copies ran while one was open for 0% of the time, Pallas kernels for 1%

profile of v1, /device:TPU:1, one launch (start us, length us, event | category | flops | bytes accessed | tf_op | source)
XLA Modules:
  0.0 68.8 jit_solution(8152858741740110484)
XLA Ops:
  0.6 1.8 %x_messages.1 = (f32[13,32,128]{2,1,0:T(8,128)}, f32[13,32,128]{2,1,0:T(8,128)}) custom-call(f32[3,32,32,128]{3,2,1,0:T(8,128)} %vs.1, f32[3,32,32,128]{3,2,1,0:T(8,128)} %vs.1, f32[32,32,128]{2,1,0:T(8,128)} %c.1, f32[32,32,128]{2,1,0:T(8,128)} %c.1), custom_call_target="tpu_custom_call" | custom-call | tf_op jit(solution)/shard_map/x_messages/pallas_call | solution.py:90
  2.5 1.4 %collective-permute-start = (f32[13,32,128]{2,1,0:T(8,128)}, f32[13,32,128]{2,1,0:T(8,128)S(1)}, u32[]{:S(2)}, u32[]{:S(2)}) collective-permute-start(f32[13,32,128]{2,1,0:T(8,128)} %get-tuple-element.11), channel_id=1, source_target_pairs={{0,16},{16,0},{32,48},{48,32},{64,80},{80,64},{96,112},{112,96},{1... | collective-permute-start | bytes 638984 | tf_op jit(solution)/shard_map/ppermute | solution.py:47
  3.9 0.0 copy-start.6
  3.9 0.0 copy-start.7
  3.9 0.0 copy-start.8
  3.9 3.3 %collective-permute-start.1 = (f32[13,32,128]{2,1,0:T(8,128)}, f32[13,32,128]{2,1,0:T(8,128)S(1)}, u32[]{:S(2)}, u32[]{:S(2)}) collective-permute-start(f32[13,32,128]{2,1,0:T(8,128)} %get-tuple-element.12), channel_id=1, source_target_pairs={{16,32},{32,16},{48,64},{64,48},{80,96},{96,80},{17,33},{33,17},{4... | collective-permute-start | bytes 638984 | tf_op jit(solution)/shard_map/ppermute | solution.py:47
  7.2 0.0 collective-permute-done.got_one.xa
  7.2 0.0 copy-start.2
  7.3 4.1 %collective-permute-done.1.got_two.xb = f32[13,32,128]{2,1,0:T(8,128)S(1)} collective-permute-done((f32[13,32,128]{2,1,0:T(8,128)}, f32[13,32,128]{2,1,0:T(8,128)S(1)}, u32[]{:S(2)}, u32[]{:S(2)}) %collective-permute-start.1) | collective-permute-done | bytes 213024 | tf_op jit(solution)/shard_map/ppermute | solution.py:47
  11.4 0.0 copy-done.2
  11.4 0.0 copy-start.4
  11.4 0.7 copy-done.4
  12.1 0.0 copy-start
  12.1 2.4 %y_messages.1 = (f32[480,128]{1,0:T(8,128)}, f32[480,128]{1,0:T(8,128)}) custom-call(f32[3,32,32,128]{3,2,1,0:T(8,128)} %vs.1, f32[3,32,32,128]{3,2,1,0:T(8,128)} %vs.1, f32[32,32,128]{2,1,0:T(8,128)} %c.1, f32[32,32,128]{2,1,0:T(8,128)} %c.1, f32[13,32,128]{2,1,0:T(8,128)} %copy-done.2, f32[13,32,128]{2,1,0:T(8,128)} %copy-done.4), custom_call_target="tpu_custom_call" | custom-call | tf_op jit(solution)/shard_map/y_messages/pallas_call | solution.py:152
  14.4 0.0 copy-start.1
  14.4 0.0 copy-start.3
  14.4 0.0 copy-start.5
  14.5 1.4 %collective-permute-start.2 = (f32[480,128]{1,0:T(8,128)}, f32[480,128]{1,0:T(8,128)S(1)}, u32[]{:S(2)}, u32[]{:S(2)}) collective-permute-start(f32[480,128]{1,0:T(8,128)} %get-tuple-element.13), channel_id=1, source_target_pairs={{0,1},{1,0},{2,3},{3,2},{4,5},{5,4},{6,7},{7,6},{8,9},{9,8},{10,11... | collective-permute-start | bytes 737288 | tf_op jit(solution)/shard_map/ppermute | solution.py:47
  15.8 0.7 collective-permute-start.3
  16.5 0.0 copy-done.6
  16.5 0.0 copy-done.7
  16.5 0.0 copy-done.8
  16.5 1.0 %route.1 = (bf16[128,1024]{1,0:T(8,128)(2,1)S(1)}, f32[1024,128]{1,0:T(8,128)S(1)}, f32[128,128]{1,0:T(8,128)S(1)}) custom-call(s32[1,1024]{1,0:T(1,128)S(1)} %bitcast.15, s32[2,1024]{1,0:T(2,128)S(1)} %bitcast.13, f32[2,1024]{1,0:T(2,128)S(1)} %bitcast.14), custom_call_target="tpu_custom_call" | custom-call | flops 400000000 | bytes 2000000 | tf_op jit(solution)/shard_map/route/pallas_call | solution.py:206
  17.5 2.3 %collective-permute-done.2.ya = f32[480,128]{1,0:T(8,128)S(1)} collective-permute-done((f32[480,128]{1,0:T(8,128)}, f32[480,128]{1,0:T(8,128)S(1)}, u32[]{:S(2)}, u32[]{:S(2)}) %collective-permute-start.2) | collective-permute-done | bytes 245792 | tf_op jit(solution)/shard_map/ppermute | solution.py:47
  19.8 0.0 collective-permute-done.3.yb
  19.8 0.0 copy-done
  19.8 0.0 copy-done.1
  19.8 0.0 copy-done.3
  19.8 0.0 copy-done.5
  19.8 17.9 %sweeps.1 = (f32[3,32,32,128]{3,2,1,0:T(8,128)}, f32[128,256]{1,0:T(8,128)S(1)}) custom-call(f32[3,32,32,128]{3,2,1,0:T(8,128)S(1)} %copy-done, f32[32,32,128]{2,1,0:T(8,128)S(1)} %copy-done.1, f32[13,32,128]{2,1,0:T(8,128)S(1)} %copy-done.3, f32[13,32,128]{2,1,0:T(8,128)S(1)} %copy-done.5, f32[480,128]{1,0:T(8,128)S(1)} %collective-permute-done.2.ya, ...), custom_call_target="tpu_custom_call" | custom-call | flops 60000000 | bytes 6000000 | tf_op jit(solution)/shard_map/sweeps/pallas_call | solution.py:346
  37.7 0.1 copy.7
  37.8 27.7 %all_to_all.11 = f32[128,1,256]{2,1,0:T(1,128)S(1)} all-to-all(f32[128,1,256]{2,1,0:T(1,128)S(1)} %copy.7), channel_id=1, replica_groups=mesh['gx'=8,'gy'=16] {'gx','gy'}, dimensions={0} | all-to-all | bytes 262144 | tf_op jit(solution)/shard_map/all_to_all | solution.py:429
  65.6 3.2 %gather.1 = f32[1,3,64,64]{3,2,1,0:T(8,128)} custom-call(f32[128,256]{1,0:T(8,128)S(1)} %bitcast.12), custom_call_target="tpu_custom_call" | custom-call | flops 400000000 | bytes 200000 | tf_op jit(solution)/shard_map/gather/pallas_call | solution.py:404
  (1 shorter events, 0.0 us)
Async XLA Ops:
  2.5 4.8 %collective-permute-start = (f32[13,32,128]{2,1,0:T(8,128)}, f32[13,32,128]{2,1,0:T(8,128)S(1)}, u32[]{:S(2)}, u32[]{:S(2)}) collective-permute-start(f32[13,32,128]{2,1,0:T(8,128)} %get-tuple-element.11), channel_id=1, source_target_pairs={{0,16},{16,0},{32,48},{48,32},{64,80},{80,64},{96,112},{112,96},{1... | collective-permute-start | bytes 638984 | tf_op jit(solution)/shard_map/ppermute | solution.py:47
  3.9 12.6 %copy-start.6 = (s32[1,1024,2]{1,2,0:T(2,128)S(1)}, s32[1,1024,2]{1,2,0:T(2,128)}, u32[]{:S(2)}) copy-start(s32[1,1024,2]{1,2,0:T(2,128)} %param.8) | copy-start | bytes 24580
  3.9 12.6 %copy-start.7 = (f32[1,1024,2]{1,2,0:T(2,128)S(1)}, f32[1,1024,2]{1,2,0:T(2,128)}, u32[]{:S(2)}) copy-start(f32[1,1024,2]{1,2,0:T(2,128)} %param.9) | copy-start | bytes 24580
  3.9 12.6 %copy-start.8 = (s32[1,1024,1]{1,2,0:T(1,128)S(1)}, s32[1,1024,1]{1,2,0:T(1,128)}, u32[]{:S(2)}) copy-start(s32[1,1024,1]{1,2,0:T(1,128)} %param.7) | copy-start | bytes 12292
  3.9 7.5 %collective-permute-start.1 = (f32[13,32,128]{2,1,0:T(8,128)}, f32[13,32,128]{2,1,0:T(8,128)S(1)}, u32[]{:S(2)}, u32[]{:S(2)}) collective-permute-start(f32[13,32,128]{2,1,0:T(8,128)} %get-tuple-element.12), channel_id=1, source_target_pairs={{16,32},{32,16},{48,64},{64,48},{80,96},{96,80},{17,33},{33,17},{4... | collective-permute-start | bytes 638984 | tf_op jit(solution)/shard_map/ppermute | solution.py:47
  7.2 4.2 %copy-start.2 = (f32[13,32,128]{2,1,0:T(8,128)}, f32[13,32,128]{2,1,0:T(8,128)S(1)}, u32[]{:S(2)}) copy-start(f32[13,32,128]{2,1,0:T(8,128)S(1)} %collective-permute-done.got_one.xa) | copy-start | bytes 638980
  11.4 0.7 copy-start.4
  12.1 7.7 %copy-start = (f32[3,32,32,128]{3,2,1,0:T(8,128)S(1)}, f32[3,32,32,128]{3,2,1,0:T(8,128)}, u32[]{:S(2)}) copy-start(f32[3,32,32,128]{3,2,1,0:T(8,128)} %vs.1) | copy-start | bytes 4718596
  14.4 5.4 %copy-start.1 = (f32[32,32,128]{2,1,0:T(8,128)S(1)}, f32[32,32,128]{2,1,0:T(8,128)}, u32[]{:S(2)}) copy-start(f32[32,32,128]{2,1,0:T(8,128)} %c.1) | copy-start | bytes 1572868
  14.4 5.4 %copy-start.3 = (f32[13,32,128]{2,1,0:T(8,128)S(1)}, f32[13,32,128]{2,1,0:T(8,128)}, u32[]{:S(2)}) copy-start(f32[13,32,128]{2,1,0:T(8,128)} %copy-done.2) | copy-start | bytes 638980
  14.4 5.4 %copy-start.5 = (f32[13,32,128]{2,1,0:T(8,128)S(1)}, f32[13,32,128]{2,1,0:T(8,128)}, u32[]{:S(2)}) copy-start(f32[13,32,128]{2,1,0:T(8,128)} %copy-done.4) | copy-start | bytes 638980
  14.5 5.3 %collective-permute-start.2 = (f32[480,128]{1,0:T(8,128)}, f32[480,128]{1,0:T(8,128)S(1)}, u32[]{:S(2)}, u32[]{:S(2)}) collective-permute-start(f32[480,128]{1,0:T(8,128)} %get-tuple-element.13), channel_id=1, source_target_pairs={{0,1},{1,0},{2,3},{3,2},{4,5},{5,4},{6,7},{7,6},{8,9},{9,8},{10,11... | collective-permute-start | bytes 737288 | tf_op jit(solution)/shard_map/ppermute | solution.py:47
  15.8 4.0 %collective-permute-start.3 = (f32[480,128]{1,0:T(8,128)}, f32[480,128]{1,0:T(8,128)S(1)}, u32[]{:S(2)}, u32[]{:S(2)}) collective-permute-start(f32[480,128]{1,0:T(8,128)} %get-tuple-element.14), channel_id=1, source_target_pairs={{1,2},{2,1},{3,4},{4,3},{5,6},{6,5},{7,8},{8,7},{9,10},{10,9},{11,... | collective-permute-start | bytes 737288 | tf_op jit(solution)/shard_map/ppermute | solution.py:47

commit v2 on v1

--- a/solution.py
+++ b/solution.py
@@ -68,21 +68,15 @@
 
 
 def x_message_kernel(vs_lo, vs_hi, c_lo, c_hi, one, two):
-    def fill(low, high):
-        low[0:9] = vs_lo[:, 0:3].reshape(9, NY, NZ)
-        low[9:13] = c_lo[...]
-        high[0:9] = vs_hi[:, 1:4].reshape(9, NY, NZ)
-        high[9:13] = c_hi[...]
-
     even = is_even("gx")
-
-    @pl.when(even)
-    def _():
-        fill(two, one)
-
-    @pl.when(jnp.logical_not(even))
-    def _():
-        fill(one, two)
+    for i in range(13):
+        if i < 9:
+            k, layer = divmod(i, 3)
+            low, high = vs_lo[k, layer], vs_hi[k, layer + 1]
+        else:
+            low, high = c_lo[i - 9], c_hi[i - 9]
+        one[i] = jnp.where(even, high, low)
+        two[i] = jnp.where(even, low, high)
 
 
 def x_messages(vs, c):
@@ -97,76 +91,54 @@
             pl.BlockSpec((4, NY, NZ), lambda i: (0, 0, 0)),
             pl.BlockSpec((4, NY, NZ), lambda i: (7, 0, 0)),
         ],
-        out_specs=(
-            pl.BlockSpec((13, NY, NZ), lambda i: (0, 0, 0)),
-            pl.BlockSpec((13, NY, NZ), lambda i: (0, 0, 0)),
-        ),
+        out_specs=(vmem(), vmem()),
         name="x_messages",
     )(vs, vs, c, c)
 
 
-def y_message_kernel(vs_lo, vs_hi, c_lo, c_hi, got_one, got_two, one, two):
+def y_message_kernel(vs, c, got_one, got_two, one, two):
     even_x = is_even("gx")
     even_y = is_even("gy")
 
-    def slab(out, vs_ref, c_ref, low, start, x_low, x_high):
-        v0 = 0 if low else 5
-        c0 = 0 if low else 4
-        for i in range(36):
-            x = i - 2
-            for k in range(3):
-                if x < 0:
-                    piece = x_low[3 * k + 3 + x, start + v0 : start + v0 + 3]
-                elif x < NX:
-                    piece = vs_ref[k, x, v0 : v0 + 3]
-                else:
-                    piece = x_high[3 * k + x - NX, start + v0 : start + v0 + 3]
-                out[9 * i + 3 * k : 9 * i + 3 * k + 3] = piece
-        for i in range(38):
-            x = i - 3
+    def put(row, size, low, high):
+        one[row : row + size] = jnp.where(even_y, high, low)
+        two[row : row + size] = jnp.where(even_y, low, high)
+
+    def halo(layer, before, part):
+        first, second = got_one[layer, part], got_two[layer, part]
+        return jnp.where(even_x == before, second, first)
+
+    for i in range(36):
+        x = i - 2
+        for k in range(3):
             if x < 0:
-                piece = x_low[9 + 4 + x, start + c0 : start + c0 + 4]
+                low, high = (halo(3 * k + 3 + x, True, p) for p in (slice(0, 3), slice(29, 32)))
             elif x < NX:
-                piece = c_ref[x, c0 : c0 + 4]
+                low, high = vs[k, x, 0:3], vs[k, x, 29:32]
             else:
-                piece = x_high[9 + x - NX, start + c0 : start + c0 + 4]
-            out[SLAB_V + 4 * i : SLAB_V + 4 * i + 4] = piece
-
-    def fill(low_out, high_out, x_low, x_high):
-        slab(low_out, vs_lo, c_lo, True, 0, x_low, x_high)
-        slab(high_out, vs_hi, c_hi, False, 24, x_low, x_high)
-
-    for want_x in (True, False):
-        for want_y in (True, False):
-
-            @pl.when(jnp.logical_and(even_x == want_x, even_y == want_y))
-            def _():
-                x_low, x_high = (got_two, got_one) if want_x else (got_one, got_two)
-                low_out, high_out = (two, one) if want_y else (one, two)
-                fill(low_out, high_out, x_low, x_high)
+                low, high = (halo(3 * k + x - NX, False, p) for p in (slice(0, 3), slice(29, 32)))
+            put(9 * i + 3 * k, 3, low, high)
+    for i in range(38):
+        x = i - 3
+        if x < 0:
+            low, high = (halo(13 + x, True, p) for p in (slice(0, 4), slice(28, 32)))
+        elif x < NX:
+            low, high = c[x, 0:4], c[x, 28:32]
+        else:
+            low, high = (halo(9 + x - NX, False, p) for p in (slice(0, 4), slice(28, 32)))
+        put(SLAB_V + 4 * i, 4, low, high)
 
 
 def y_messages(vs, c, got_one, got_two):
     shape = jax.ShapeDtypeStruct((SLAB, NZ), F32)
-    whole = pl.BlockSpec((13, NY, NZ), lambda i: (0, 0, 0))
     return pl.pallas_call(
         y_message_kernel,
         out_shape=(shape, shape),
-        grid=(1,),
-        in_specs=[
-            pl.BlockSpec((3, NX, 8, NZ), lambda i: (0, 0, 0, 0)),
-            pl.BlockSpec((3, NX, 8, NZ), lambda i: (0, 0, 3, 0)),
-            pl.BlockSpec((NX, 8, NZ), lambda i: (0, 0, 0)),
-            pl.BlockSpec((NX, 8, NZ), lambda i: (0, 3, 0)),
-            whole,
-            whole,
-        ],
-        out_specs=(
-            pl.BlockSpec((SLAB, NZ), lambda i: (0, 0)),
-            pl.BlockSpec((SLAB, NZ), lambda i: (0, 0)),
-        ),
+        in_specs=[vmem()] * 4,
+        out_specs=(vmem(), vmem()),
+        compiler_params=params(),
         name="y_messages",
-    )(vs, vs, c, c, got_one, got_two)
+    )(vs, c, got_one, got_two)
 
 
 def route_kernel(patch, spans, par, to_patch, to_slot, meta):
@@ -228,53 +200,40 @@
 
 def sweep_kernel(
     vs, c, xa, xb, ya, yb, to_patch, to_slot, meta, field, send,
-    stiff, ratio, wx, wy, wz, y0, y1, y2, spread,
+    stiff, ratio, wx, wy, wz, scale, halo, y0, y1, y2, spread, out, sem,
 ):
     even_x = is_even("gx")
     even_y = is_even("gy")
-    for k in range(3):
-        y0[k, 4:36, 0:NY] = vs[k]
-    stiff[4:36, 0:NY] = c[...]
-
-    def put_x(low, high):
-        for k in range(3):
-            y0[k, 1:4, 0:NY] = low[3 * k : 3 * k + 3]
-            y0[k, 36:39, 0:NY] = high[3 * k : 3 * k + 3]
-        stiff[0:4, 0:NY] = low[9:13]
-        stiff[36:40, 0:NY] = high[9:13]
-
-    def put_y(low, high):
-        for i in range(36):
+
+    def x_halo(layer, before):
+        return jnp.where(even_x == before, xb[layer], xa[layer])
+
+    def y_halo(first, size, before):
+        rows = slice(first, first + size)
+        return jnp.where(even_y == before, yb[rows], ya[rows])
+
+    for x in range(EX):
+        if x < 4:
+            stiff[x, 0:NY] = x_halo(9 + x, True)
+        elif x < 36:
+            stiff[x, 0:NY] = c[x - 4]
+        else:
+            stiff[x, 0:NY] = x_halo(9 + x - 36, False)
+        if 1 <= x < 39:
+            row = SLAB_V + 4 * (x - 1)
+            stiff[x, 32:36] = y_halo(row, 4, False)
+            stiff[x, 36:40] = y_halo(row, 4, True)
+        if 2 <= x < 38:
             for k in range(3):
-                row = 9 * i + 3 * k
-                y0[k, i + 2, 32:35] = high[row : row + 3]
-                y0[k, i + 2, 37:40] = low[row : row + 3]
-        for i in range(38):
-            row = SLAB_V + 4 * i
-            stiff[i + 1, 32:36] = high[row : row + 4]
-            stiff[i + 1, 36:40] = low[row : row + 4]
-
-    @pl.when(even_x)
-    def _():
-        put_x(xb, xa)
-
-    @pl.when(jnp.logical_not(even_x))
-    def _():
-        put_x(xa, xb)
-
-    @pl.when(even_y)
-    def _():
-        put_y(yb, ya)
-
-    @pl.when(jnp.logical_not(even_y))
-    def _():
-        put_y(ya, yb)
+                row = 9 * (x - 2) + 3 * k
+                halo[k, x, 0:3] = y_halo(row, 3, False)
+                halo[k, x, 5:8] = y_halo(row, 3, True)
 
     lane = lax.broadcasted_iota(jnp.int32, (EY, NZ), 1)
     not_last = lane < NZ - 1
     not_first = lane > 0
 
-    def prepare(x, carry):
+    for x in range(1, 39):
         here = stiff[x]
         after = stiff[x + 1]
         y_next = up(here)
@@ -287,11 +246,17 @@
         wx[x] = 0.5 * (here + after)
         wy[x] = 0.5 * (here + y_next)
         wz[x] = jnp.where(not_last, 0.5 * (here + z_next), 0.0)
-        for k in range(3):
-            y0[k, x] = y0[k, x] * inverse
-        return carry
-
-    lax.fori_loop(1, 39, prepare, 0)
+        if 4 <= x < 36:
+            scale[x - 4] = diag[0:NY]
+        for k in range(3):
+            if x < 4:
+                center = x_halo(3 * k + x - 1, True)
+            elif x < 36:
+                center = vs[k, x - 4]
+            else:
+                center = x_halo(3 * k + x - 36, False)
+            y0[k, x, 0:NY] = center * inverse[0:NY]
+            y0[k, x, NY:EY] = halo[k, x] * inverse[NY:EY]
 
     def update(source, k, x):
         here = source[k, x]
@@ -304,40 +269,37 @@
         )
         return y0[k, x] + KEEP * here + ratio[x] * total
 
-    def sweep(source, target, first, last):
-        def step(x, carry):
-            for k in range(3):
-                target[k, x] = update(source, k, x)
-            return carry
-
-        lax.fori_loop(first, last, step, 0)
-
-    sweep(y0, y1, 2, 38)
-    sweep(y1, y2, 3, 37)
-
-    lane_field = lax.broadcasted_iota(jnp.int32, (NY, NZ), 1)
-
-    def last_step(x, carry):
-        scale = stiff[x]
-        sides = (stiff[x - 1] + stiff[x + 1]) + (up(scale) + down(scale))
-        z_next = jnp.where(not_last, pltpu.roll(scale, NZ - 1, 1), 0.0)
-        z_prev = jnp.where(not_first, pltpu.roll(scale, 1, 1), 0.0)
-        diag = (3.0 * scale + 0.5 * (sides + (z_next + z_prev)))[0:NY]
+    for x in range(2, 38):
+        for k in range(3):
+            y1[k, x] = update(y0, k, x)
+    for x in range(3, 37):
+        for k in range(3):
+            y2[k, x] = update(y1, k, x)
+
+    group = lax.broadcasted_iota(jnp.int32, (NY, NZ), 1) // CAP
+    writes = []
+    for x in range(4, 36):
         picked = jnp.zeros((NY, NZ), F32)
         for k in range(3):
             fresh = update(y2, k, x)[0:NY]
-            field[k, x - 4] = fresh * diag
+            out[k, x - 4] = fresh * scale[x - 4]
             wide = jnp.broadcast_to(fresh[:, 0:1], (NY, NZ))
-            picked = jnp.where(lane_field // CAP == k, wide, picked)
-        rows = pl.ds(pl.multiple_of((x - 4) * NY, NY), NY)
+            picked = jnp.where(group == k, wide, picked)
+        rows = slice((x - 4) * NY, (x - 3) * NY)
         spread[rows] = (OMEGA * picked) * to_slot[rows]
-        return carry
-
-    lax.fori_loop(4, 36, last_step, 0)
+        if x % 8 == 3:
+            part = slice(x - 11, x - 3)
+            write = pltpu.make_async_copy(
+                out.at[:, part], field.at[:, part], sem.at[len(writes)]
+            )
+            write.start()
+            writes.append(write)
     high, mid, low = three_pieces(spread[...])
     hot = to_patch[...]
     send[:, 0:128] = meta[...]
     send[:, 128:256] = dot(hot, high) + dot(hot, mid) + dot(hot, low)
+    for write in writes:
+        write.wait()
 
 
 def sweeps(vs, c, xa, xb, ya, yb, to_patch, to_slot, meta):
@@ -350,8 +312,15 @@
             jax.ShapeDtypeStruct((DEV, 256), F32),
         ),
         in_specs=[vmem()] * 9,
-        out_specs=(vmem(),) * 2,
-        scratch_shapes=[plane] * 5 + [cube] * 3 + [pltpu.VMEM((ROWS, 128), F32)],
+        out_specs=(pl.BlockSpec(memory_space=pl.ANY), vmem()),
+        scratch_shapes=[plane] * 5
+        + [pltpu.VMEM((NX, NY, NZ), F32), pltpu.VMEM((3, EX, 8, NZ), F32)]
+        + [cube] * 3
+        + [
+            pltpu.VMEM((ROWS, 128), F32),
+            pltpu.VMEM((3, NX, NY, NZ), F32),
+            pltpu.SemaphoreType.DMA((4,)),
+        ],
         compiler_params=params(),
         cost_estimate=pl.CostEstimate(flops=60_000_000, bytes_accessed=6_000_000, transcendentals=0),
         name="sweeps",

time: 69 us -> 58.8 us (0.85)
  Pallas kernels: 26.3 us -> 17.1 us
    pallas_call x1, Pallas kernels: 17.9 us -> 10.7 us  [sweeps(): pl.pallas_call(sweep_kernel, out_shape=(jax.ShapeDtypeStruct((3, NX, NY,...]
    pallas_call x1, Pallas kernels: 2.35 us -> 0.11 us  [y_messages(): pl.pallas_call(y_message_kernel, out_shape=(shape, shape), in_specs=[vmem...]
    unnamed x19 -> x11, local copies, waits for them, and re-layouts: 0.72 us -> 0.03 us
  transfers between devices with their start and end apart: 4 -> 4, of which waited for: 2 -> 2; matrix products, arithmetic and copies ran while one was open for 0% -> 0% of each run, Pallas kernels for 1% -> 2%
where the time goes in v2:
time: 58.8 us; the launch traced here: 58.6 us
  blocking collectives  27.4 us (47%)
  Pallas kernels  17.1 us (29%)
  starting transfers between devices  6.72 us (11%)
  waiting for transfers between devices  6.5 us (11%)
  between operations  0.74 us (1%)
    all_to_all x1, blocking collectives, body(): got = lax.all_to_all(send, ('gx', 'gy'), 0, 0, tiled=True)  27.4 us
    pallas_call x1, Pallas kernels, sweeps(): pl.pallas_call(sweep_kernel, out_shape=(jax.ShapeDtypeStruct((3, NX, NY,...  10.7 us
    ppermute x4, starting transfers between devices, swap(): return (lax.ppermute(one, axis, first), lax.ppermute(two, axis, second))  6.72 us
    ppermute x4, waiting for transfers between devices, swap(): return (lax.ppermute(one, axis, first), lax.ppermute(two, axis, second))  6.5 us
    pallas_call x1, Pallas kernels, gather(): pl.pallas_call(gather_kernel, out_shape=jax.ShapeDtypeStruct((1, 3, NC, N...  3.23 us
    pallas_call x1, Pallas kernels, x_messages(): pl.pallas_call(x_message_kernel, out_shape=(shape, shape), grid=(1,), in_...  2 us
  transfers between devices with their start and end apart: 4, of which 2 were waited for; matrix products, arithmetic and copies ran while one was open for 0% of the time, Pallas kernels for 2%

profile of v2, /device:TPU:1, one launch (start us, length us, event | category | flops | bytes accessed | tf_op | source)
XLA Modules:
  0.0 58.6 jit_solution(9622234372435724524)
XLA Ops:
  0.6 0.0 copy-start.1
  0.6 0.0 copy-start
  0.6 2.0 %x_messages.1 = (f32[13,32,128]{2,1,0:T(8,128)}, f32[13,32,128]{2,1,0:T(8,128)}) custom-call(f32[3,32,32,128]{3,2,1,0:T(8,128)} %vs.3, f32[3,32,32,128]{3,2,1,0:T(8,128)} %vs.3, f32[32,32,128]{2,1,0:T(8,128)} %c.3, f32[32,32,128]{2,1,0:T(8,128)} %c.3), custom_call_target="tpu_custom_call" | custom-call | tf_op jit(solution)/shard_map/x_messages/pallas_call | solution.py:84
  2.7 0.0 copy-start.2
  2.7 0.0 copy-start.3
  2.7 0.0 copy-start.4
  2.7 1.5 %collective-permute-start = (f32[13,32,128]{2,1,0:T(8,128)}, f32[13,32,128]{2,1,0:T(8,128)S(1)}, u32[]{:S(2)}, u32[]{:S(2)}) collective-permute-start(f32[13,32,128]{2,1,0:T(8,128)} %get-tuple-element.11), channel_id=1, source_target_pairs={{0,16},{16,0},{32,48},{48,32},{64,80},{80,64},{96,112},{112,96},{1... | collective-permute-start | bytes 638984 | tf_op jit(solution)/shard_map/ppermute | solution.py:47
  4.2 3.2 %collective-permute-start.1 = (f32[13,32,128]{2,1,0:T(8,128)}, f32[13,32,128]{2,1,0:T(8,128)S(1)}, u32[]{:S(2)}, u32[]{:S(2)}) collective-permute-start(f32[13,32,128]{2,1,0:T(8,128)} %get-tuple-element.12), channel_id=1, source_target_pairs={{16,32},{32,16},{48,64},{64,48},{80,96},{96,80},{17,33},{33,17},{4... | collective-permute-start | bytes 638984 | tf_op jit(solution)/shard_map/ppermute | solution.py:47
  7.4 0.0 collective-permute-done.got_one.xa
  7.4 4.5 %collective-permute-done.1.got_two.xb = f32[13,32,128]{2,1,0:T(8,128)S(1)} collective-permute-done((f32[13,32,128]{2,1,0:T(8,128)}, f32[13,32,128]{2,1,0:T(8,128)S(1)}, u32[]{:S(2)}, u32[]{:S(2)}) %collective-permute-start.1) | collective-permute-done | bytes 213024 | tf_op jit(solution)/shard_map/ppermute | solution.py:47
  11.8 0.0 copy-done.1
  11.8 0.0 copy-done
  11.8 0.1 y_messages.1
  11.9 1.4 %collective-permute-start.2 = (f32[480,128]{1,0:T(8,128)S(1)}, f32[480,128]{1,0:T(8,128)S(1)}, u32[]{:S(2)}, u32[]{:S(2)}) collective-permute-start(f32[480,128]{1,0:T(8,128)S(1)} %get-tuple-element.13), channel_id=1, source_target_pairs={{0,1},{1,0},{2,3},{3,2},{4,5},{5,4},{6,7},{7,6},{8,9},{9,8},{10,11... | collective-permute-start | bytes 737288 | tf_op jit(solution)/shard_map/ppermute | solution.py:47
  13.3 0.7 %collective-permute-start.3 = (f32[480,128]{1,0:T(8,128)S(1)}, f32[480,128]{1,0:T(8,128)S(1)}, u32[]{:S(2)}, u32[]{:S(2)}) collective-permute-start(f32[480,128]{1,0:T(8,128)S(1)} %get-tuple-element.14), channel_id=1, source_target_pairs={{1,2},{2,1},{3,4},{4,3},{5,6},{6,5},{7,8},{8,7},{9,10},{10,9},{11,... | collective-permute-start | bytes 737288 | tf_op jit(solution)/shard_map/ppermute | solution.py:47
  14.0 0.0 copy-done.2
  14.0 0.0 copy-done.3
  14.0 0.0 copy-done.4
  14.0 1.0 %route.1 = (bf16[128,1024]{1,0:T(8,128)(2,1)S(1)}, f32[1024,128]{1,0:T(8,128)S(1)}, f32[128,128]{1,0:T(8,128)S(1)}) custom-call(s32[1,1024]{1,0:T(1,128)S(1)} %bitcast.15, s32[2,1024]{1,0:T(2,128)S(1)} %bitcast.13, f32[2,1024]{1,0:T(2,128)S(1)} %bitcast.14), custom_call_target="tpu_custom_call" | custom-call | flops 400000000 | bytes 2000000 | tf_op jit(solution)/shard_map/route/pallas_call | solution.py:178
  15.0 2.0 %collective-permute-done.2.ya = f32[480,128]{1,0:T(8,128)S(1)} collective-permute-done((f32[480,128]{1,0:T(8,128)S(1)}, f32[480,128]{1,0:T(8,128)S(1)}, u32[]{:S(2)}, u32[]{:S(2)}) %collective-permute-start.2) | collective-permute-done | bytes 245792 | tf_op jit(solution)/shard_map/ppermute | solution.py:47
  17.1 0.0 collective-permute-done.3.yb
  17.1 10.7 %sweeps.1 = (f32[3,32,32,128]{3,2,1,0:T(8,128)}, f32[128,256]{1,0:T(8,128)S(1)}) custom-call(f32[3,32,32,128]{3,2,1,0:T(8,128)S(1)} %copy-done, f32[32,32,128]{2,1,0:T(8,128)S(1)} %copy-done.1, f32[13,32,128]{2,1,0:T(8,128)S(1)} %collective-permute-done.got_one.xa, f32[13,32,128]{2,1,0:T(8,128)S(1)} %collective-permute-done.1.got_two.xb, ...), custom_call_target="tpu_custom_call" | custom-call | flops 60000000 | bytes 6000000 | tf_op jit(solution)/shard_map/sweeps/pallas_call | solution.py:308
  27.8 0.1 copy.7
  28.0 27.4 %all_to_all.11 = f32[128,1,256]{2,1,0:T(1,128)S(1)} all-to-all(f32[128,1,256]{2,1,0:T(1,128)S(1)} %copy.7), channel_id=1, replica_groups=mesh['gx'=8,'gy'=16] {'gx','gy'}, dimensions={0} | all-to-all | bytes 262144 | tf_op jit(solution)/shard_map/all_to_all | solution.py:398
  55.4 3.2 %gather.1 = f32[1,3,64,64]{3,2,1,0:T(8,128)} custom-call(f32[128,256]{1,0:T(8,128)S(1)} %bitcast.12), custom_call_target="tpu_custom_call" | custom-call | flops 400000000 | bytes 200000 | tf_op jit(solution)/shard_map/gather/pallas_call | solution.py:373
  (1 shorter events, 0.0 us)
Async XLA Ops:
  0.6 11.2 %copy-start.1 = (f32[32,32,128]{2,1,0:T(8,128)S(1)}, f32[32,32,128]{2,1,0:T(8,128)}, u32[]{:S(2)}) copy-start(f32[32,32,128]{2,1,0:T(8,128)} %c.3) | copy-start | bytes 1572868
  0.6 11.2 %copy-start = (f32[3,32,32,128]{3,2,1,0:T(8,128)S(1)}, f32[3,32,32,128]{3,2,1,0:T(8,128)}, u32[]{:S(2)}) copy-start(f32[3,32,32,128]{3,2,1,0:T(8,128)} %vs.3) | copy-start | bytes 4718596
  2.7 11.3 %copy-start.2 = (s32[1,1024,2]{1,2,0:T(2,128)S(1)}, s32[1,1024,2]{1,2,0:T(2,128)}, u32[]{:S(2)}) copy-start(s32[1,1024,2]{1,2,0:T(2,128)} %param.8) | copy-start | bytes 24580
  2.7 11.4 %copy-start.3 = (f32[1,1024,2]{1,2,0:T(2,128)S(1)}, f32[1,1024,2]{1,2,0:T(2,128)}, u32[]{:S(2)}) copy-start(f32[1,1024,2]{1,2,0:T(2,128)} %param.9) | copy-start | bytes 24580
  2.7 11.4 %copy-start.4 = (s32[1,1024,1]{1,2,0:T(1,128)S(1)}, s32[1,1024,1]{1,2,0:T(1,128)}, u32[]{:S(2)}) copy-start(s32[1,1024,1]{1,2,0:T(1,128)} %param.7) | copy-start | bytes 12292
  2.7 4.7 %collective-permute-start = (f32[13,32,128]{2,1,0:T(8,128)}, f32[13,32,128]{2,1,0:T(8,128)S(1)}, u32[]{:S(2)}, u32[]{:S(2)}) collective-permute-start(f32[13,32,128]{2,1,0:T(8,128)} %get-tuple-element.11), channel_id=1, source_target_pairs={{0,16},{16,0},{32,48},{48,32},{64,80},{80,64},{96,112},{112,96},{1... | collective-permute-start | bytes 638984 | tf_op jit(solution)/shard_map/ppermute | solution.py:47
  4.2 7.7 %collective-permute-start.1 = (f32[13,32,128]{2,1,0:T(8,128)}, f32[13,32,128]{2,1,0:T(8,128)S(1)}, u32[]{:S(2)}, u32[]{:S(2)}) collective-permute-start(f32[13,32,128]{2,1,0:T(8,128)} %get-tuple-element.12), channel_id=1, source_target_pairs={{16,32},{32,16},{48,64},{64,48},{80,96},{96,80},{17,33},{33,17},{4... | collective-permute-start | bytes 638984 | tf_op jit(solution)/shard_map/ppermute | solution.py:47
  11.9 5.1 %collective-permute-start.2 = (f32[480,128]{1,0:T(8,128)S(1)}, f32[480,128]{1,0:T(8,128)S(1)}, u32[]{:S(2)}, u32[]{:S(2)}) collective-permute-start(f32[480,128]{1,0:T(8,128)S(1)} %get-tuple-element.13), channel_id=1, source_target_pairs={{0,1},{1,0},{2,3},{3,2},{4,5},{5,4},{6,7},{7,6},{8,9},{9,8},{10,11... | collective-permute-start | bytes 737288 | tf_op jit(solution)/shard_map/ppermute | solution.py:47
  13.3 3.8 %collective-permute-start.3 = (f32[480,128]{1,0:T(8,128)S(1)}, f32[480,128]{1,0:T(8,128)S(1)}, u32[]{:S(2)}, u32[]{:S(2)}) collective-permute-start(f32[480,128]{1,0:T(8,128)S(1)} %get-tuple-element.14), channel_id=1, source_target_pairs={{1,2},{2,1},{3,4},{4,3},{5,6},{6,5},{7,8},{8,7},{9,10},{10,9},{11,... | collective-permute-start | bytes 737288 | tf_op jit(solution)/shard_map/ppermute | solution.py:47

commit v3 on v2

v3 whole, which is shorter than its diff:
```python
import jax
import jax.numpy as jnp
from jax import lax
from jax.experimental import pallas as pl
from jax.experimental.pallas import tpu as pltpu
from jax.sharding import PartitionSpec as P

NC = 64
OMEGA = 2.0 / 3.0
KEEP = 1.0 - OMEGA
NX = 32
NY = 32
NZ = 128
ROWS = NX * NY
CAP = 32
DEV = 128
CHUNK = 8
EX = NX + 8
EY = NY + 8
SLAB_V = 9 * NX
SLAB = 13 * NX
F32 = jnp.float32
BF16 = jnp.bfloat16
VMEM_LIMIT = 24 * 1024 * 1024


def vmem():
    return pl.BlockSpec(memory_space=pltpu.VMEM)


def params():
    return pltpu.CompilerParams(vmem_limit_bytes=VMEM_LIMIT)


def is_even(axis):
    return lax.rem(lax.axis_index(axis), 2) == 0


def exchange(along_x, one, two):
    count_x, count_y = lax.axis_size("gx"), lax.axis_size("gy")

    def partner(i, last):
        return i if i in (0, last) else ((i + 1) ^ 1) - 1

    first, second = [], []
    for i in range(count_x):
        for j in range(count_y):
            if along_x:
                near, far = (i ^ 1, j), (partner(i, count_x - 1), j)
                far = (i, j ^ 1) if far == (i, j) else far
            else:
                near, far = (i, j ^ 1), (i, partner(j, count_y - 1))
                far = (i ^ 1, j) if far == (i, j) else far
            here = i * count_y + j
            first.append((here, near[0] * count_y + near[1]))
            second.append((here, far[0] * count_y + far[1]))
    both = ("gx", "gy")
    return lax.ppermute(one, both, first), lax.ppermute(two, both, second)


def at_end(axis):
    here = lax.axis_index(axis)
    return jnp.logical_or(here == 0, here == lax.axis_size(axis) - 1)


def two_pieces(x):
    high = x.astype(BF16)
    return high, (x - high.astype(F32)).astype(BF16)


def three_pieces(x):
    high = x.astype(BF16)
    rest = x - high.astype(F32)
    mid = rest.astype(BF16)
    return high, mid, (rest - mid.astype(F32)).astype(BF16)


def dot(a, b):
    return jnp.dot(a, b, preferred_element_type=F32)


def dot_nt(a, b):
    return lax.dot_general(a, b, (((1,), (1,)), ((), ())), preferred_element_type=F32)


def message_kernel(vs, c, y_one, y_two, x_one, x_two, low_v, high_v, low_c, high_c, sems):
    slabs = [
        pltpu.make_async_copy(vs.at[:, :, 0:8], low_v, sems.at[0]),
        pltpu.make_async_copy(vs.at[:, :, NY - 8 : NY], high_v, sems.at[1]),
        pltpu.make_async_copy(c.at[:, 0:8], low_c, sems.at[2]),
        pltpu.make_async_copy(c.at[:, NY - 8 : NY], high_c, sems.at[3]),
    ]
    for copy in slabs:
        copy.start()

    def layers(low, high):
        copies = []
        for k in range(3):
            spot = slice(3 * k, 3 * k + 3)
            copies.append(pltpu.make_async_copy(vs.at[k, 0:3], low.at[spot], sems.at[4 + k]))
            copies.append(
                pltpu.make_async_copy(vs.at[k, NX - 3 : NX], high.at[spot], sems.at[7 + k])
            )
        copies.append(pltpu.make_async_copy(c.at[0:4], low.at[9:13], sems.at[10]))
        copies.append(pltpu.make_async_copy(c.at[NX - 4 : NX], high.at[9:13], sems.at[11]))
        return copies

    even_x = is_even("gx")
    even_y = is_even("gy")

    @pl.when(even_x)
    def _():
        for copy in layers(x_two, x_one):
            copy.start()

    @pl.when(jnp.logical_not(even_x))
    def _():
        for copy in layers(x_one, x_two):
            copy.start()

    inside_y = jnp.where(at_end("gy"), 0.0, 1.0)

    def put(row, size, low, high):
        y_one[row : row + size] = jnp.where(even_y, high, low)
        y_two[row : row + size] = jnp.where(even_y, low, high) * inside_y

    for copy in slabs:
        copy.wait()
    for x in range(NX):
        for k in range(3):
            put(9 * x + 3 * k, 3, low_v[k, x, 0:3], high_v[k, x, 5:8])
        put(SLAB_V + 4 * x, 4, low_c[x, 0:4], high_c[x, 4:8])

    @pl.when(even_x)
    def _():
        for copy in layers(x_two, x_one):
            copy.wait()

    @pl.when(jnp.logical_not(even_x))
    def _():
        for copy in layers(x_one, x_two):
            copy.wait()

    @pl.when(at_end("gx"))
    def _():
        x_two[...] = jnp.zeros((13, NY, NZ), F32)


def messages(vs, c):
    y_shape = jax.ShapeDtypeStruct((SLAB, NZ), F32)
    x_shape = jax.ShapeDtypeStruct((13, NY, NZ), F32)
    return pl.pallas_call(
        message_kernel,
        out_shape=(y_shape, y_shape, x_shape, x_shape),
        in_specs=[pl.BlockSpec(memory_space=pltpu.HBM)] * 2,
        out_specs=(vmem(),) * 4,
        scratch_shapes=[
            pltpu.VMEM((3, NX, 8, NZ), F32),
            pltpu.VMEM((3, NX, 8, NZ), F32),
            pltpu.VMEM((NX, 8, NZ), F32),
            pltpu.VMEM((NX, 8, NZ), F32),
            pltpu.SemaphoreType.DMA((12,)),
        ],
        compiler_params=params(),
        name="messages",
    )(vs, c)


def y_halo(even, one, two, first, size, before):
    rows = slice(first, first + size)
    return jnp.where(even == before, two[rows], one[rows])


def corner_kernel(ya, yb, _, one, two):
    even_x = is_even("gx")
    even_y = is_even("gy")
    inside_x = jnp.where(at_end("gx"), 0.0, 1.0)
    blank = jnp.zeros((2, NZ), F32)
    for i in range(13):
        if i < 9:
            k, layer = divmod(i, 3)
            size, places = 3, (9 * layer + 3 * k, 9 * (NX - 3 + layer) + 3 * k)
            one[i, 3:5] = blank
            two[i, 3:5] = blank
        else:
            size, places = 4, (SLAB_V + 4 * (i - 9), SLAB_V + 4 * (NX - 4 + i - 9))
        for spot, before in ((slice(0, size), False), (slice(8 - size, 8), True)):
            low, high = (y_halo(even_y, ya, yb, row, size, before) for row in places)
            one[i, spot] = jnp.where(even_x, high, low)
            two[i, spot] = jnp.where(even_x, low, high) * inside_x


def corners(ya, yb, meta):
    shape = jax.ShapeDtypeStruct((13, 8, NZ), F32)
    return pl.pallas_call(
        corner_kernel,
        out_shape=(shape, shape),
        in_specs=[vmem()] * 3,
        out_specs=(vmem(), vmem()),
        compiler_params=params(),
        name="corners",
    )(ya, yb, meta)


def route_kernel(patch, spans, par, to_patch, to_slot, meta):
    patch_row = patch[...]
    hot = (lax.broadcasted_iota(jnp.int32, (DEV, ROWS), 0) == patch_row).astype(F32)
    hot16 = hot.astype(BF16)
    to_patch[...] = hot16
    upper = (
        lax.broadcasted_iota(jnp.int32, (128, 128), 0)
        <= lax.broadcasted_iota(jnp.int32, (128, 128), 1)
    ).astype(BF16)
    before = jnp.zeros((DEV, 1), F32)
    ranks = []
    for block in range(ROWS // 128):
        part = slice(128 * block, 128 * block + 128)
        count = dot(hot16[:, part], upper) + before
        ranks.append(jnp.sum(count * hot[:, part], axis=0, keepdims=True) - 1.0)
        before = count[:, 127:128]
    rank = jnp.concatenate(ranks, axis=1)
    lane_slot = lax.rem(lax.broadcasted_iota(jnp.int32, (128, ROWS), 0), CAP).astype(F32)
    slot_hot = (lane_slot == rank).astype(F32)
    to_slot[...] = slot_hot.T
    fields = [
        spans[0:1].astype(F32),
        spans[1:2].astype(F32),
        par[0:1],
        par[1:2],
    ]
    spread = jnp.concatenate(
        [slot_hot[CAP * f : CAP * f + CAP] * fields[f] for f in range(4)], axis=0
    )
    high, mid, low = three_pieces(spread)
    meta[...] = dot_nt(hot16, high) + dot_nt(hot16, mid) + dot_nt(hot16, low)


def route(patch, spans, par):
    return pl.pallas_call(
        route_kernel,
        out_shape=(
            jax.ShapeDtypeStruct((DEV, ROWS), BF16),
            jax.ShapeDtypeStruct((ROWS, 128), F32),
            jax.ShapeDtypeStruct((DEV, 128), F32),
        ),
        in_specs=[vmem()] * 3,
        out_specs=(vmem(),) * 3,
        compiler_params=params(),
        cost_estimate=pl.CostEstimate(flops=400_000_000, bytes_accessed=2_000_000, transcendentals=0),
        name="route",
    )(patch, spans, par)


def up(x):
    return pltpu.roll(x, x.shape[0] - 1, 0)


def down(x):
    return pltpu.roll(x, 1, 0)


class Rows:
    def __init__(self):
        self.place = {}

    def hold(self, ref, rows):
        for index, x in enumerate(rows):
            self.place[x] = (ref, index)
        return self

    def __getitem__(self, x):
        ref, index = self.place[x]
        return ref[index]

    def __setitem__(self, x, value):
        ref, index = self.place[x]
        ref[index] = value


EDGE = [4, 5, 6, 7, 8, 31, 32, 33, 34, 35]
MIDDLE = list(range(9, 31))


class Stencil:
    def __init__(self, stiff, ratio, wx, wy, wz, scale, y0, y1, y2):
        self.stiff, self.ratio, self.scale = stiff, ratio, scale
        self.wx, self.wy, self.wz = wx, wy, wz
        self.fields = (y0, y1, y2)
        lane = lax.broadcasted_iota(jnp.int32, (EY, NZ), 1)
        self.not_last = lane < NZ - 1
        self.not_first = lane > 0
        self.group = lax.broadcasted_iota(jnp.int32, (NY, NZ), 1) // CAP

    def prepare(self, x, source):
        here, after, before = self.stiff[x], self.stiff[x + 1], self.stiff[x - 1]
        y_next = up(here)
        z_next = jnp.where(self.not_last, pltpu.roll(here, NZ - 1, 1), 0.0)
        z_prev = jnp.where(self.not_first, pltpu.roll(here, 1, 1), 0.0)
        sides = (before + after) + (y_next + down(here)) + (z_next + z_prev)
        diag = 3.0 * here + 0.5 * sides
        inverse = jnp.where(here > 0.0, 1.0 / diag, 0.0)
        self.ratio[x] = OMEGA * inverse
        self.wx[x] = 0.5 * (here + after)
        self.wy[x] = 0.5 * (here + y_next)
        self.wz[x] = jnp.where(self.not_last, 0.5 * (here + z_next), 0.0)
        self.scale[x] = diag
        for k in range(3):
            self.fields[0][k][x] = source(k, x) * inverse

    def update(self, level, k, x):
        source = self.fields[level][k]
        here = source[x]
        face_y, face_z = self.wy[x], self.wz[x]
        total = self.wx[x] * source[x + 1] + self.wx[x - 1] * source[x - 1]
        total = total + (face_y * up(here) + down(face_y * here))
        total = total + (
            face_z * pltpu.roll(here, NZ - 1, 1) + pltpu.roll(face_z * here, 1, 1)
        )
        return self.fields[0][k][x] + KEEP * here + self.ratio[x] * total

    def sweep(self, level, rows):
        for x in rows:
            for k in range(3):
                self.fields[level + 1][k][x] = self.update(level, k, x)

    def finish(self, x, out, index, slots):
        picked = jnp.zeros((NY, NZ), F32)
        for k in range(3):
            fresh = self.update(2, k, x)[0:NY]
            out[k, index] = fresh * self.scale[x][0:NY]
            wide = jnp.broadcast_to(fresh[:, 0:1], (NY, NZ))
            picked = jnp.where(self.group == k, wide, picked)
        return (OMEGA * picked) * slots


def scatter_rows(hot, spread):
    high, mid, low = three_pieces(spread)
    return dot(hot, high) + dot(hot, mid) + dot(hot, low)


def cube_rows(refs, rows):
    return [Rows().hold(ref, rows) for ref in refs]


def interior_kernel(
    vs, c, ya, yb, to_patch, to_slot, field, partial, keep, keep3,
    stiff, mids, mids3, spread, out, sem,
):
    even_y = is_even("gy")
    for x in range(NX):
        row = SLAB_V + 4 * x
        stiff[x, 0:NY] = c[x]
        stiff[x, NY : NY + 4] = y_halo(even_y, ya, yb, row, 4, False)
        stiff[x, EY - 4 : EY] = y_halo(even_y, ya, yb, row, 4, True)
    for x in range(1, NX - 1):
        for k in range(3):
            row = 9 * x + 3 * k
            place = (keep3.at[0, k], EDGE.index(x + 4)) if x + 4 in EDGE else (mids3.at[0, k], x - 5)
            ref, index = place
            ref[index, NY : NY + 3] = y_halo(even_y, ya, yb, row, 3, False)
            ref[index, EY - 3 : EY] = y_halo(even_y, ya, yb, row, 3, True)

    def source(k, x):
        ref, index = fields[0][k].place[x]
        return jnp.concatenate([vs[k, x - 4], ref[index, NY:EY]], axis=0)

    def plane(n):
        return Rows().hold(keep.at[n], EDGE).hold(mids.at[n], MIDDLE)

    fields = [
        [Rows().hold(keep3.at[n, k], EDGE).hold(mids3.at[n, k], MIDDLE) for k in range(3)]
        for n in range(3)
    ]
    grid = Stencil(
        Rows().hold(stiff, range(4, 36)), plane(0), plane(1), plane(2), plane(3), plane(4), *fields
    )
    for x in (4, 5, 34, 35):
        keep[5, EDGE.index(x)] = grid.stiff[x]
    for x in range(5, 35):
        grid.prepare(x, source)
    grid.sweep(0, range(6, 34))
    grid.sweep(1, range(7, 33))
    writes = []
    total = jnp.zeros((DEV, 128), F32)
    for x in range(8, 32):
        rows = slice((x - 4) * NY, (x - 3) * NY)
        spread[(x - 8) * NY : (x - 7) * NY] = grid.finish(x, out, x - 8, to_slot[rows])
        if x % 8 == 7:
            part = slice(x - 15, x - 7)
            last = (x - 7) * NY
            total = total + scatter_rows(
                to_patch[:, last - 128 : last + 128], spread[last - 256 : last]
            )
            write = pltpu.make_async_copy(
                out.at[:, part], field.at[:, x - 11 : x - 3], sem.at[len(writes)]
            )
            write.start()
            writes.append(write)
    partial[...] = total
    for write in writes:
        write.wait()


def interior(vs, c, ya, yb, to_patch, to_slot):
    return pl.pallas_call(
        interior_kernel,
        out_shape=(
            jax.ShapeDtypeStruct((3, NX, NY, NZ), F32),
            jax.ShapeDtypeStruct((DEV, 128), F32),
            jax.ShapeDtypeStruct((6, len(EDGE), EY, NZ), F32),
            jax.ShapeDtypeStruct((3, 3, len(EDGE), EY, NZ), F32),
        ),
        in_specs=[vmem()] * 6,
        out_specs=(pl.BlockSpec(memory_space=pl.ANY), vmem(), vmem(), vmem()),
        scratch_shapes=[
            pltpu.VMEM((NX, EY, NZ), F32),
            pltpu.VMEM((5, len(MIDDLE), EY, NZ), F32),
            pltpu.VMEM((3, 3, len(MIDDLE), EY, NZ), F32),
            pltpu.VMEM((768, 128), F32),
            pltpu.VMEM((3, 24, NY, NZ), F32),
            pltpu.SemaphoreType.DMA((3,)),
        ],
        compiler_params=params(),
        cost_estimate=pl.CostEstimate(flops=60_000_000, bytes_accessed=6_000_000, transcendentals=0),
        name="interior",
    )(vs, c, ya, yb, to_patch, to_slot)


def edge_kernel(
    vs, ya, yb, xa, xb, za, zb, to_patch, to_slot, meta, partial, keep, keep3, _, field, send,
    fresh, fresh3, spread, out, sem,
):
    even_x = is_even("gx")
    even_y = is_even("gy")

    def x_halo(layer, before):
        center = jnp.where(even_x == before, xb[layer], xa[layer])
        corner = jnp.where(even_x == before, zb[layer], za[layer])
        return jnp.concatenate([center, corner], axis=0)

    class Given:
        def __getitem__(self, x):
            if x < 4:
                return x_halo(9 + x, True)
            if x < 36:
                return keep[5, EDGE.index(x)]
            return x_halo(9 + x - 36, False)

    def source(k, x):
        if x == 4 or x == 35:
            spot = 0 if x == 4 else 1
            row = 9 * (x - 4) + 3 * k
            fresh3[3, k, spot, NY : NY + 3] = y_halo(even_y, ya, yb, row, 3, False)
            fresh3[3, k, spot, EY - 3 : EY] = y_halo(even_y, ya, yb, row, 3, True)
            return jnp.concatenate([vs[k, x - 4], fresh3[3, k, spot, NY:EY]], axis=0)
        if x < 4:
            return x_halo(3 * k + x - 1, True)
        return x_halo(3 * k + x - 36, False)

    def hold(ref3, n, k, rows):
        return Rows().hold(keep3.at[n, k], EDGE).hold(ref3.at[n, k], rows)

    first = [1, 2, 3, 4, 35, 36, 37, 38]
    second = [2, 3, 4, 5, 34, 35, 36, 37]
    third = [3, 4, 5, 6, 33, 34, 35, 36]
    last = [4, 5, 6, 7, 32, 33, 34, 35]
    planes = [Rows().hold(keep.at[n], EDGE).hold(fresh.at[n], first) for n in range(5)]
    fields = [
        [hold(fresh3, n, k, rows) for k in range(3)] for n, rows in enumerate((first, second, third))
    ]
    grid = Stencil(Given(), *planes, *fields)
    for x in first:
        grid.prepare(x, source)
    grid.sweep(0, second)
    grid.sweep(1, third)
    for index, x in enumerate(last):
        rows = slice((x - 4) * NY, (x - 3) * NY)
        spread[index * NY : (index + 1) * NY] = grid.finish(x, out, index, to_slot[rows])
    writes = [
        pltpu.make_async_copy(out.at[:, 0:4], field.at[:, 0:4], sem.at[0]),
        pltpu.make_async_copy(out.at[:, 4:8], field.at[:, 28:32], sem.at[1]),
    ]
    for write in writes:
        write.start()
    send[:, 0:128] = meta[...]
    send[:, 128:256] = (
        partial[...]
        + scatter_rows(
            jnp.concatenate([to_patch[:, 0:128], to_patch[:, 896:1024]], axis=1), spread[...]
        )
    )
    for write in writes:
        write.wait()


def edges(vs, ya, yb, xa, xb, za, zb, to_patch, to_slot, meta, partial, keep, keep3, field):
    return pl.pallas_call(
        edge_kernel,
        out_shape=(
            jax.ShapeDtypeStruct((3, NX, NY, NZ), F32),
            jax.ShapeDtypeStruct((DEV, 256), F32),
        ),
        in_specs=[vmem()] * 13 + [pl.BlockSpec(memory_space=pl.ANY)],
        out_specs=(pl.BlockSpec(memory_space=pl.ANY), vmem()),
        scratch_shapes=[
            pltpu.VMEM((5, 8, EY, NZ), F32),
            pltpu.VMEM((4, 3, 8, EY, NZ), F32),
            pltpu.VMEM((256, 128), F32),
            pltpu.VMEM((3, 8, NY, NZ), F32),
            pltpu.SemaphoreType.DMA((2,)),
        ],
        input_output_aliases={13: 0},
        compiler_params=params(),
        cost_estimate=pl.CostEstimate(flops=20_000_000, bytes_accessed=2_000_000, transcendentals=0),
        name="edges",
    )(vs, ya, yb, xa, xb, za, zb, to_patch, to_slot, meta, partial, keep, keep3, field)


def pieces(param):
    other = 1.0 - param
    return [
        other * other * other / 6.0,
        (3.0 * param * param * param - 6.0 * param * param + 4.0) / 6.0,
        (-3.0 * param * param * param + 3.0 * param * param + 3.0 * param + 1.0) / 6.0,
        param * param * param / 6.0,
    ]


def gather_kernel(got, grads, table, left, right):
    table[0:128] = got[:, 0:128].T
    table[128:256] = got[:, 128:256].T
    basis_u = pieces(table[64:96])
    basis_v = pieces(table[96:128])
    knot = lax.broadcasted_iota(jnp.int32, (NC, DEV), 0).astype(F32)

    def spline(span, basis, slot):
        offset = knot - table[span + slot : span + slot + 1]
        rows = jnp.zeros((NC, DEV), F32)
        for index in range(4):
            rows = jnp.where(offset == float(index), basis[index][slot : slot + 1], rows)
        return rows

    product = jnp.zeros((6 * NC, 2 * NC), F32)
    for slot in range(CAP):
        part = slice(DEV * slot, DEV * slot + DEV)
        along_u = spline(0, basis_u, slot)
        for k in range(3):
            value = table[128 + CAP * k + slot : 128 + CAP * k + slot + 1]
            high, low = two_pieces(along_u * value)
            left[NC * k : NC * k + NC, part] = high
            left[3 * NC + NC * k : 3 * NC + NC * k + NC, part] = low
        high, low = two_pieces(spline(CAP, basis_v, slot))
        right[0:NC, part] = high
        right[NC : 2 * NC, part] = low
        if slot % CHUNK == CHUNK - 1:
            block = slice(DEV * (slot + 1 - CHUNK), DEV * (slot + 1))
            product = product + dot_nt(left[:, block], right[:, block])
    total = product[0 : 3 * NC, 0:NC] + (
        product[0 : 3 * NC, NC : 2 * NC] + product[3 * NC : 6 * NC, 0:NC]
    )
    grads[0] = total.reshape(3, NC, NC)


def gather(got):
    return pl.pallas_call(
        gather_kernel,
        out_shape=jax.ShapeDtypeStruct((1, 3, NC, NC), F32),
        in_specs=[vmem()],
        out_specs=vmem(),
        scratch_shapes=[
            pltpu.VMEM((256, DEV), F32),
            pltpu.VMEM((6 * NC, DEV * CAP), BF16),
            pltpu.VMEM((2 * NC, DEV * CAP), BF16),
        ],
        compiler_params=params(),
        cost_estimate=pl.CostEstimate(flops=400_000_000, bytes_accessed=200_000, transcendentals=0),
        name="gather",
    )(got)


def body(volume_sens, stiffness, patch_of_row, knot_spans, span_params):
    y_one, y_two, x_one, x_two = messages(
        pltpu.with_memory_space_constraint(volume_sens, pltpu.HBM),
        pltpu.with_memory_space_constraint(stiffness, pltpu.HBM),
    )
    ya, yb = exchange(False, y_one, y_two)
    xa, xb = exchange(True, x_one, x_two)
    to_patch, to_slot, meta = route(
        patch_of_row.reshape(1, ROWS), knot_spans[0].T, span_params[0].T
    )
    za, zb = exchange(True, *corners(ya, yb, meta))
    field, partial, keep, keep3 = interior(volume_sens, stiffness, ya, yb, to_patch, to_slot)
    field, send = edges(
        volume_sens, ya, yb, xa, xb, za, zb, to_patch, to_slot, meta, partial, keep, keep3, field
    )
    got = lax.all_to_all(send, ("gx", "gy"), 0, 0, tiled=True)
    return field, gather(got)


def solution(mesh):
    placed = (
        P(None, "gx", "gy", None),
        P("gx", "gy", None),
        P(("gx", "gy"), None, None),
        P(("gx", "gy"), None, None),
        P(("gx", "gy"), None, None),
    )
    return jax.shard_map(
        body,
        mesh=mesh,
        in_specs=placed,
        out_specs=(P(None, "gx", "gy", None), P(("gx", "gy"), None, None, None)),
        check_vma=False,
    )
```

time: 58.8 us -> 49.5 us (0.84)
  waiting for transfers between devices: 6.5 us -> 0.11 us
  blocking collectives: 27.4 us -> 22.3 us
  starting transfers between devices: 6.72 us -> 8.12 us
  local copies, waits for them, and re-layouts: 0.17 us -> 0.86 us
    ppermute x4 -> x6, waiting for transfers between devices: 6.5 us -> 0.11 us  [exchange(): return (lax.ppermute(one, both, first), lax.ppermute(two, both, second))]
    all_to_all x1, blocking collectives: 27.4 us -> 22.3 us  [body(): got = lax.all_to_all(send, ('gx', 'gy'), 0, 0, tiled=True)]
    ppermute x4 -> x6, starting transfers between devices: 6.72 us -> 8.12 us  [exchange(): return (lax.ppermute(one, both, first), lax.ppermute(two, both, second))]
    unnamed x11, local copies, waits for them, and re-layouts: 0.03 us -> 0.72 us
    pallas_call x3 -> x4, Pallas kernels: 12.8 us -> 13 us  [the longest x1 8.74 us: interior(): pl.pallas_call(interior_kernel, out_shape=(jax.ShapeDtypeStruct((3, NX, N...]
  transfers between devices with their start and end apart: 4 -> 6, of which waited for: 2 -> 1; matrix products, arithmetic and copies ran while one was open for 0% -> 0% of each run, Pallas kernels for 2% -> 20%
where the time goes in v3:
time: 49.5 us; the launch traced here: 49.3 us
  blocking collectives  22.3 us (45%)
  Pallas kernels  17.2 us (35%)
  starting transfers between devices  8.12 us (16%)
  local copies, waits for them, and re-layouts  0.86 us (2%)
  between operations  0.75 us (2%)
    all_to_all x1, blocking collectives, body(): got = lax.all_to_all(send, ('gx', 'gy'), 0, 0, tiled=True)  22.3 us
    pallas_call x1, Pallas kernels, interior(): pl.pallas_call(interior_kernel, out_shape=(jax.ShapeDtypeStruct((3, NX, N...  8.74 us
    ppermute x6, starting transfers between devices, exchange(): return (lax.ppermute(one, both, first), lax.ppermute(two, both, second))  8.12 us
    pallas_call x1, Pallas kernels, gather(): pl.pallas_call(gather_kernel, out_shape=jax.ShapeDtypeStruct((1, 3, NC, N...  3.16 us
    pallas_call x1, Pallas kernels, edges(): pl.pallas_call(edge_kernel, out_shape=(jax.ShapeDtypeStruct((3, NX, NY, N...  2.66 us
    pallas_call x1, Pallas kernels, messages(): pl.pallas_call(message_kernel, out_shape=(y_shape, y_shape, x_shape, x_sh...  1.55 us
    pallas_call x1, Pallas kernels, route(): pl.pallas_call(route_kernel, out_shape=(jax.ShapeDtypeStruct((DEV, ROWS),...  1 us
  transfers between devices with their start and end apart: 6, of which 1 were waited for; matrix products, arithmetic and copies ran while one was open for 0% of the time, Pallas kernels for 20%

profile of v3, /device:TPU:1, one launch (start us, length us, event | category | flops | bytes accessed | tf_op | source)
XLA Modules:
  0.0 49.3 jit_solution(3253902493909550137)
XLA Ops:
  0.6 0.0 copy-start
  0.6 0.0 copy-start.1
  0.7 0.0 copy-start.2
  0.7 0.0 copy-start.4
  0.7 1.6 %messages.1 = (f32[416,128]{1,0:T(8,128)S(1)}, f32[416,128]{1,0:T(8,128)S(1)}, f32[13,32,128]{2,1,0:T(8,128)S(1)}, f32[13,32,128]{2,1,0:T(8,128)S(1)}) custom-call(f32[3,32,32,128]{3,2,1,0:T(8,128)} %vs.5, f32[32,32,128]{2,1,0:T(8,128)} %c.3), custom_call_target="tpu_custom_call" | custom-call | tf_op jit(solution)/shard_map/messages/pallas_call | solution.py:152
  2.2 2.1 %collective-permute-start = (f32[416,128]{1,0:T(8,128)S(1)}, f32[416,128]{1,0:T(8,128)S(1)}, u32[]{:S(2)}, u32[]{:S(2)}) collective-permute-start(f32[416,128]{1,0:T(8,128)S(1)} %get-tuple-element.17), channel_id=1, source_target_pairs={{0,1},{1,0},{2,3},{3,2},{4,5},{5,4},{6,7},{7,6},{8,9},{9,8},{10,11... | collective-permute-start | bytes 638984 | tf_op jit(solution)/shard_map/ppermute | solution.py:58
  4.4 1.0 %collective-permute-start.1 = (f32[416,128]{1,0:T(8,128)S(1)}, f32[416,128]{1,0:T(8,128)S(1)}, u32[]{:S(2)}, u32[]{:S(2)}) collective-permute-start(f32[416,128]{1,0:T(8,128)S(1)} %get-tuple-element.18), channel_id=1, source_target_pairs={{0,16},{1,2},{2,1},{3,4},{4,3},{5,6},{6,5},{7,8},{8,7},{9,10},{10,... | collective-permute-start | bytes 638984 | tf_op jit(solution)/shard_map/ppermute | solution.py:58
  5.3 0.0 collective-permute-start.2
  5.3 1.7 %collective-permute-start.3 = (f32[13,32,128]{2,1,0:T(8,128)S(1)}, f32[13,32,128]{2,1,0:T(8,128)S(1)}, u32[]{:S(2)}, u32[]{:S(2)}) collective-permute-start(f32[13,32,128]{2,1,0:T(8,128)S(1)} %get-tuple-element.20), channel_id=1, source_target_pairs={{0,1},{1,0},{2,3},{3,2},{4,5},{5,4},{6,7},{7,6},{8,9},{9,8},{10,11... | collective-permute-start | bytes 638984 | tf_op jit(solution)/shard_map/ppermute | solution.py:58
  7.0 0.0 copy-done.2
  7.0 0.0 copy-done.4
  7.0 0.0 copy-start.3
  7.0 0.7 %copy-done.3 = f32[1,1024,2]{1,2,0:T(2,128)S(1)} copy-done((f32[1,1024,2]{1,2,0:T(2,128)S(1)}, f32[1,1024,2]{1,2,0:T(2,128)}, u32[]{:S(2)}) %copy-start.3) | copy-done | bytes 8216
  7.7 1.0 %route.1 = (bf16[128,1024]{1,0:T(8,128)(2,1)S(1)}, f32[1024,128]{1,0:T(8,128)S(1)}, f32[128,128]{1,0:T(8,128)S(1)}) custom-call(s32[1,1024]{1,0:T(1,128)S(1)} %bitcast.15, s32[2,1024]{1,0:T(2,128)S(1)} %bitcast.13, f32[2,1024]{1,0:T(2,128)S(1)} %bitcast.14), custom_call_target="tpu_custom_call" | custom-call | flops 400000000 | bytes 2000000 | tf_op jit(solution)/shard_map/route/pallas_call | solution.py:239
  8.7 0.1 collective-permute-done.ya
  8.8 0.0 collective-permute-done.1.yb
  8.9 1.8 %collective-permute-start.4 = (f32[13,8,128]{2,1,0:T(8,128)S(1)}, f32[13,8,128]{2,1,0:T(8,128)S(1)}, u32[]{:S(2)}, u32[]{:S(2)}) collective-permute-start(f32[13,8,128]{2,1,0:T(8,128)S(1)} %get-tuple-element.22), channel_id=1, source_target_pairs={{0,16},{1,17},{2,18},{3,19},{4,20},{5,21},{6,22},{7,23},{8,24},{9,... | collective-permute-start | bytes 159752 | tf_op jit(solution)/shard_map/ppermute | solution.py:58
  10.7 1.5 %collective-permute-start.5 = (f32[13,8,128]{2,1,0:T(8,128)S(1)}, f32[13,8,128]{2,1,0:T(8,128)S(1)}, u32[]{:S(2)}, u32[]{:S(2)}) collective-permute-start(f32[13,8,128]{2,1,0:T(8,128)S(1)} %get-tuple-element.23), channel_id=1, source_target_pairs={{0,1},{1,0},{2,3},{3,2},{4,5},{5,4},{6,7},{7,6},{8,9},{9,8},{10,11... | collective-permute-start | bytes 159752 | tf_op jit(solution)/shard_map/ppermute | solution.py:58
  12.2 0.0 copy-done
  12.2 0.0 copy-done.1
  12.2 8.7 %interior.1 = (f32[3,32,32,128]{3,2,1,0:T(8,128)}, f32[128,128]{1,0:T(8,128)S(1)}, f32[6,10,40,128]{3,2,1,0:T(8,128)S(1)}, f32[3,3,10,40,128]{4,3,2,1,0:T(8,128)S(1)}) custom-call(f32[3,32,32,128]{3,2,1,0:T(8,128)S(1)} %copy-done, f32[32,32,128]{2,1,0:T(8,128)S(1)} %copy-done.1, f32[416,128]{1,0:T(8,128)S(1)} %collective-permute-done.ya, ...), custom_call_target="tpu_custom_call" | custom-call | flops 60000000 | bytes 6000000 | tf_op jit(solution)/shard_map/interior/pallas_call | solution.py:405
  21.0 0.0 collective-permute-done.2.xa
  21.0 0.0 collective-permute-done.3.xb
  21.0 0.0 collective-permute-done.4.za
  21.0 0.0 collective-permute-done.5.zb
  21.0 2.7 %edges.1 = (f32[3,32,32,128]{3,2,1,0:T(8,128)}, f32[128,256]{1,0:T(8,128)S(1)}) custom-call(f32[3,32,32,128]{3,2,1,0:T(8,128)S(1)} %copy-done, f32[416,128]{1,0:T(8,128)S(1)} %collective-permute-done.ya, f32[416,128]{1,0:T(8,128)S(1)} %collective-permute-done.1.yb, f32[13,32,128]{2,1,0:T(8,128)S(1)} %collective-permute-done.2.xa, ...), custom_call_target="tpu_custom_call", output_to_operand_aliasing={{0}: (13, {})} | custom-call | flops 20000000 | bytes 2000000 | tf_op jit(solution)/shard_map/edges/pallas_call | solution.py:497
  23.7 0.1 copy.8
  23.8 22.3 %all_to_all.11 = f32[128,1,256]{2,1,0:T(1,128)S(1)} all-to-all(f32[128,1,256]{2,1,0:T(1,128)S(1)} %copy.8), channel_id=1, replica_groups=mesh['gx'=8,'gy'=16] {'gx','gy'}, dimensions={0} | all-to-all | bytes 262144 | tf_op jit(solution)/shard_map/all_to_all | solution.py:596
  46.1 3.2 %gather.1 = f32[1,3,64,64]{3,2,1,0:T(8,128)} custom-call(f32[128,256]{1,0:T(8,128)S(1)} %bitcast.12), custom_call_target="tpu_custom_call" | custom-call | flops 400000000 | bytes 200000 | tf_op jit(solution)/shard_map/gather/pallas_call | solution.py:565
  (2 shorter events, 0.0 us)
Async XLA Ops:
  0.6 11.6 %copy-start = (f32[3,32,32,128]{3,2,1,0:T(8,128)S(1)}, f32[3,32,32,128]{3,2,1,0:T(8,128)}, u32[]{:S(2)}) copy-start(f32[3,32,32,128]{3,2,1,0:T(8,128)} %vs.5) | copy-start | bytes 4718596
  0.6 11.6 %copy-start.1 = (f32[32,32,128]{2,1,0:T(8,128)S(1)}, f32[32,32,128]{2,1,0:T(8,128)}, u32[]{:S(2)}) copy-start(f32[32,32,128]{2,1,0:T(8,128)} %c.3) | copy-start | bytes 1572868
  0.7 6.4 %copy-start.2 = (s32[1,1024,2]{1,2,0:T(2,128)S(1)}, s32[1,1024,2]{1,2,0:T(2,128)}, u32[]{:S(2)}) copy-start(s32[1,1024,2]{1,2,0:T(2,128)} %param.8) | copy-start | bytes 24580
  0.7 6.3 %copy-start.4 = (s32[1,1024,1]{1,2,0:T(1,128)S(1)}, s32[1,1024,1]{1,2,0:T(1,128)}, u32[]{:S(2)}) copy-start(s32[1,1024,1]{1,2,0:T(1,128)} %param.7) | copy-start | bytes 12292
  2.2 6.6 %collective-permute-start = (f32[416,128]{1,0:T(8,128)S(1)}, f32[416,128]{1,0:T(8,128)S(1)}, u32[]{:S(2)}, u32[]{:S(2)}) collective-permute-start(f32[416,128]{1,0:T(8,128)S(1)} %get-tuple-element.17), channel_id=1, source_target_pairs={{0,1},{1,0},{2,3},{3,2},{4,5},{5,4},{6,7},{7,6},{8,9},{9,8},{10,11... | collective-permute-start | bytes 638984 | tf_op jit(solution)/shard_map/ppermute | solution.py:58
  4.4 4.5 %collective-permute-start.1 = (f32[416,128]{1,0:T(8,128)S(1)}, f32[416,128]{1,0:T(8,128)S(1)}, u32[]{:S(2)}, u32[]{:S(2)}) collective-permute-start(f32[416,128]{1,0:T(8,128)S(1)} %get-tuple-element.18), channel_id=1, source_target_pairs={{0,16},{1,2},{2,1},{3,4},{4,3},{5,6},{6,5},{7,8},{8,7},{9,10},{10,... | collective-permute-start | bytes 638984 | tf_op jit(solution)/shard_map/ppermute | solution.py:58
  5.3 15.6 %collective-permute-start.2 = (f32[13,32,128]{2,1,0:T(8,128)S(1)}, f32[13,32,128]{2,1,0:T(8,128)S(1)}, u32[]{:S(2)}, u32[]{:S(2)}) collective-permute-start(f32[13,32,128]{2,1,0:T(8,128)S(1)} %get-tuple-element.19), channel_id=1, source_target_pairs={{0,16},{1,17},{2,18},{3,19},{4,20},{5,21},{6,22},{7,23},{8,24},{9,... | collective-permute-start | bytes 638984 | tf_op jit(solution)/shard_map/ppermute | solution.py:58
  5.3 15.7 %collective-permute-start.3 = (f32[13,32,128]{2,1,0:T(8,128)S(1)}, f32[13,32,128]{2,1,0:T(8,128)S(1)}, u32[]{:S(2)}, u32[]{:S(2)}) collective-permute-start(f32[13,32,128]{2,1,0:T(8,128)S(1)} %get-tuple-element.20), channel_id=1, source_target_pairs={{0,1},{1,0},{2,3},{3,2},{4,5},{5,4},{6,7},{7,6},{8,9},{9,8},{10,11... | collective-permute-start | bytes 638984 | tf_op jit(solution)/shard_map/ppermute | solution.py:58
  7.0 0.7 %copy-start.3 = (f32[1,1024,2]{1,2,0:T(2,128)S(1)}, f32[1,1024,2]{1,2,0:T(2,128)}, u32[]{:S(2)}) copy-start(f32[1,1024,2]{1,2,0:T(2,128)} %param.9) | copy-start | bytes 24580
  8.9 12.1 %collective-permute-start.4 = (f32[13,8,128]{2,1,0:T(8,128)S(1)}, f32[13,8,128]{2,1,0:T(8,128)S(1)}, u32[]{:S(2)}, u32[]{:S(2)}) collective-permute-start(f32[13,8,128]{2,1,0:T(8,128)S(1)} %get-tuple-element.22), channel_id=1, source_target_pairs={{0,16},{1,17},{2,18},{3,19},{4,20},{5,21},{6,22},{7,23},{8,24},{9,... | collective-permute-start | bytes 159752 | tf_op jit(solution)/shard_map/ppermute | solution.py:58
  10.7 10.3 %collective-permute-start.5 = (f32[13,8,128]{2,1,0:T(8,128)S(1)}, f32[13,8,128]{2,1,0:T(8,128)S(1)}, u32[]{:S(2)}, u32[]{:S(2)}) collective-permute-start(f32[13,8,128]{2,1,0:T(8,128)S(1)} %get-tuple-element.23), channel_id=1, source_target_pairs={{0,1},{1,0},{2,3},{3,2},{4,5},{5,4},{6,7},{7,6},{8,9},{9,8},{10,11... | collective-permute-start | bytes 159752 | tf_op jit(solution)/shard_map/ppermute | solution.py:58

commit v4 on v3

--- a/solution.py
+++ b/solution.py
@@ -219,9 +219,8 @@
         ranks.append(jnp.sum(count * hot[:, part], axis=0, keepdims=True) - 1.0)
         before = count[:, 127:128]
     rank = jnp.concatenate(ranks, axis=1)
-    lane_slot = lax.rem(lax.broadcasted_iota(jnp.int32, (128, ROWS), 0), CAP).astype(F32)
-    slot_hot = (lane_slot == rank).astype(F32)
-    to_slot[...] = slot_hot.T
+    slot_hot = (lax.broadcasted_iota(jnp.int32, (CAP, ROWS), 0).astype(F32) == rank).astype(F32)
+    to_slot[...] = slot_hot
     fields = [
         spans[0:1].astype(F32),
         spans[1:2].astype(F32),
@@ -229,7 +228,7 @@
         par[1:2],
     ]
     spread = jnp.concatenate(
-        [slot_hot[CAP * f : CAP * f + CAP] * fields[f] for f in range(4)], axis=0
+        [slot_hot * field for field in fields], axis=0
     )
     high, mid, low = three_pieces(spread)
     meta[...] = dot_nt(hot16, high) + dot_nt(hot16, mid) + dot_nt(hot16, low)
@@ -240,7 +239,7 @@
         route_kernel,
         out_shape=(
             jax.ShapeDtypeStruct((DEV, ROWS), BF16),
-            jax.ShapeDtypeStruct((ROWS, 128), F32),
+            jax.ShapeDtypeStruct((CAP, ROWS), F32),
             jax.ShapeDtypeStruct((DEV, 128), F32),
         ),
         in_specs=[vmem()] * 3,
@@ -289,7 +288,6 @@
         lane = lax.broadcasted_iota(jnp.int32, (EY, NZ), 1)
         self.not_last = lane < NZ - 1
         self.not_first = lane > 0
-        self.group = lax.broadcasted_iota(jnp.int32, (NY, NZ), 1) // CAP
 
     def prepare(self, x, source):
         here, after, before = self.stiff[x], self.stiff[x + 1], self.stiff[x - 1]
@@ -323,28 +321,15 @@
             for k in range(3):
                 self.fields[level + 1][k][x] = self.update(level, k, x)
 
-    def finish(self, x, out, index, slots):
-        picked = jnp.zeros((NY, NZ), F32)
+    def finish(self, x, out, surface, index):
         for k in range(3):
             fresh = self.update(2, k, x)[0:NY]
+            surface[k, index] = fresh
             out[k, index] = fresh * self.scale[x][0:NY]
-            wide = jnp.broadcast_to(fresh[:, 0:1], (NY, NZ))
-            picked = jnp.where(self.group == k, wide, picked)
-        return (OMEGA * picked) * slots
-
-
-def scatter_rows(hot, spread):
-    high, mid, low = three_pieces(spread)
-    return dot(hot, high) + dot(hot, mid) + dot(hot, low)
-
-
-def cube_rows(refs, rows):
-    return [Rows().hold(ref, rows) for ref in refs]
 
 
 def interior_kernel(
-    vs, c, ya, yb, to_patch, to_slot, field, partial, keep, keep3,
-    stiff, mids, mids3, spread, out, sem,
+    vs, c, ya, yb, out, surface, keep, keep3, stiff, mids, mids3,
 ):
     even_y = is_even("gy")
     for x in range(NX):
@@ -380,55 +365,35 @@
         grid.prepare(x, source)
     grid.sweep(0, range(6, 34))
     grid.sweep(1, range(7, 33))
-    writes = []
-    total = jnp.zeros((DEV, 128), F32)
     for x in range(8, 32):
-        rows = slice((x - 4) * NY, (x - 3) * NY)
-        spread[(x - 8) * NY : (x - 7) * NY] = grid.finish(x, out, x - 8, to_slot[rows])
-        if x % 8 == 7:
-            part = slice(x - 15, x - 7)
-            last = (x - 7) * NY
-            total = total + scatter_rows(
-                to_patch[:, last - 128 : last + 128], spread[last - 256 : last]
-            )
-            write = pltpu.make_async_copy(
-                out.at[:, part], field.at[:, x - 11 : x - 3], sem.at[len(writes)]
-            )
-            write.start()
-            writes.append(write)
-    partial[...] = total
-    for write in writes:
-        write.wait()
-
-
-def interior(vs, c, ya, yb, to_patch, to_slot):
+        grid.finish(x, out, surface, x - 8)
+
+
+def interior(vs, c, ya, yb):
+    rows = jax.ShapeDtypeStruct((3, 24, NY, NZ), F32)
     return pl.pallas_call(
         interior_kernel,
         out_shape=(
-            jax.ShapeDtypeStruct((3, NX, NY, NZ), F32),
-            jax.ShapeDtypeStruct((DEV, 128), F32),
+            rows,
+            rows,
             jax.ShapeDtypeStruct((6, len(EDGE), EY, NZ), F32),
             jax.ShapeDtypeStruct((3, 3, len(EDGE), EY, NZ), F32),
         ),
-        in_specs=[vmem()] * 6,
-        out_specs=(pl.BlockSpec(memory_space=pl.ANY), vmem(), vmem(), vmem()),
+        in_specs=[vmem()] * 4,
+        out_specs=(vmem(),) * 4,
         scratch_shapes=[
             pltpu.VMEM((NX, EY, NZ), F32),
             pltpu.VMEM((5, len(MIDDLE), EY, NZ), F32),
             pltpu.VMEM((3, 3, len(MIDDLE), EY, NZ), F32),
-            pltpu.VMEM((768, 128), F32),
-            pltpu.VMEM((3, 24, NY, NZ), F32),
-            pltpu.SemaphoreType.DMA((3,)),
         ],
         compiler_params=params(),
         cost_estimate=pl.CostEstimate(flops=60_000_000, bytes_accessed=6_000_000, transcendentals=0),
         name="interior",
-    )(vs, c, ya, yb, to_patch, to_slot)
+    )(vs, c, ya, yb)
 
 
 def edge_kernel(
-    vs, ya, yb, xa, xb, za, zb, to_patch, to_slot, meta, partial, keep, keep3, _, field, send,
-    fresh, fresh3, spread, out, sem,
+    vs, ya, yb, xa, xb, za, zb, keep, keep3, out, surface, fresh, fresh3,
 ):
     even_x = is_even("gx")
     even_y = is_even("gy")
@@ -474,46 +439,58 @@
     grid.sweep(0, second)
     grid.sweep(1, third)
     for index, x in enumerate(last):
-        rows = slice((x - 4) * NY, (x - 3) * NY)
-        spread[index * NY : (index + 1) * NY] = grid.finish(x, out, index, to_slot[rows])
-    writes = [
-        pltpu.make_async_copy(out.at[:, 0:4], field.at[:, 0:4], sem.at[0]),
-        pltpu.make_async_copy(out.at[:, 4:8], field.at[:, 28:32], sem.at[1]),
-    ]
-    for write in writes:
-        write.start()
-    send[:, 0:128] = meta[...]
-    send[:, 128:256] = (
-        partial[...]
-        + scatter_rows(
-            jnp.concatenate([to_patch[:, 0:128], to_patch[:, 896:1024]], axis=1), spread[...]
-        )
-    )
-    for write in writes:
-        write.wait()
-
-
-def edges(vs, ya, yb, xa, xb, za, zb, to_patch, to_slot, meta, partial, keep, keep3, field):
+        grid.finish(x, out, surface, index)
+
+
+def edges(vs, ya, yb, xa, xb, za, zb, keep, keep3):
+    rows = jax.ShapeDtypeStruct((3, 8, NY, NZ), F32)
     return pl.pallas_call(
         edge_kernel,
-        out_shape=(
-            jax.ShapeDtypeStruct((3, NX, NY, NZ), F32),
-            jax.ShapeDtypeStruct((DEV, 256), F32),
-        ),
-        in_specs=[vmem()] * 13 + [pl.BlockSpec(memory_space=pl.ANY)],
-        out_specs=(pl.BlockSpec(memory_space=pl.ANY), vmem()),
+        out_shape=(rows, rows),
+        in_specs=[vmem()] * 9,
+        out_specs=(vmem(),) * 2,
         scratch_shapes=[
             pltpu.VMEM((5, 8, EY, NZ), F32),
             pltpu.VMEM((4, 3, 8, EY, NZ), F32),
-            pltpu.VMEM((256, 128), F32),
-            pltpu.VMEM((3, 8, NY, NZ), F32),
-            pltpu.SemaphoreType.DMA((2,)),
         ],
-        input_output_aliases={13: 0},
         compiler_params=params(),
         cost_estimate=pl.CostEstimate(flops=20_000_000, bytes_accessed=2_000_000, transcendentals=0),
         name="edges",
-    )(vs, ya, yb, xa, xb, za, zb, to_patch, to_slot, meta, partial, keep, keep3, field)
+    )(vs, ya, yb, xa, xb, za, zb, keep, keep3)
+
+
+def pack_kernel(to_patch, to_slot, meta, outer, inner, send):
+    column = lax.broadcasted_iota(jnp.int32, (DEV, NZ), 1)
+    values = []
+    for block in range(ROWS // DEV):
+        if block == 0:
+            ref, part = outer, slice(0, 4)
+        elif block == 7:
+            ref, part = outer, slice(4, 8)
+        else:
+            ref, part = inner, slice(4 * block - 4, 4 * block)
+        first, second, third = (ref[k, part].reshape(DEV, NZ) for k in range(3))
+        mixed = jnp.where(column == 1, pltpu.roll(second, 1, 1), first)
+        mixed = jnp.where(column == 2, pltpu.roll(third, 2, 1), mixed)
+        values.append(OMEGA * mixed.T[0:3])
+    values = jnp.concatenate(values, axis=1)
+    slots = to_slot[...]
+    spread = jnp.concatenate([slots * values[k : k + 1] for k in range(3)], axis=0)
+    sent = dot_nt(jnp.concatenate(three_pieces(spread), axis=0), to_patch[...])
+    sent = sent[0:96] + sent[96:192] + sent[192:288]
+    send[:, 0:128] = meta[...]
+    send[:, 128:256] = jnp.concatenate([sent, jnp.zeros((CAP, DEV), F32)], axis=0).T
+
+
+def pack(to_patch, to_slot, meta, outer, inner):
+    return pl.pallas_call(
+        pack_kernel,
+        out_shape=jax.ShapeDtypeStruct((DEV, 256), F32),
+        in_specs=[vmem()] * 5,
+        out_specs=vmem(),
+        compiler_params=params(),
+        name="pack",
+    )(to_patch, to_slot, meta, outer, inner)
 
 
 def pieces(param):
@@ -526,7 +503,14 @@
     ]
 
 
-def gather_kernel(got, grads, table, left, right):
+def gather_kernel(got, inner, outer, field, grads, table, left, right, sems):
+    writes = [
+        pltpu.make_async_copy(inner, field.at[:, 4:28], sems.at[0]),
+        pltpu.make_async_copy(outer.at[:, 0:4], field.at[:, 0:4], sems.at[1]),
+        pltpu.make_async_copy(outer.at[:, 4:8], field.at[:, 28:32], sems.at[2]),
+    ]
+    for write in writes:
+        write.start()
     table[0:128] = got[:, 0:128].T
     table[128:256] = got[:, 128:256].T
     basis_u = pieces(table[64:96])
@@ -559,23 +543,29 @@
         product[0 : 3 * NC, NC : 2 * NC] + product[3 * NC : 6 * NC, 0:NC]
     )
     grads[0] = total.reshape(3, NC, NC)
-
-
-def gather(got):
+    for write in writes:
+        write.wait()
+
+
+def gather(got, inner, outer):
     return pl.pallas_call(
         gather_kernel,
-        out_shape=jax.ShapeDtypeStruct((1, 3, NC, NC), F32),
-        in_specs=[vmem()],
-        out_specs=vmem(),
+        out_shape=(
+            jax.ShapeDtypeStruct((3, NX, NY, NZ), F32),
+            jax.ShapeDtypeStruct((1, 3, NC, NC), F32),
+        ),
+        in_specs=[vmem()] * 3,
+        out_specs=(pl.BlockSpec(memory_space=pl.ANY), vmem()),
         scratch_shapes=[
             pltpu.VMEM((256, DEV), F32),
             pltpu.VMEM((6 * NC, DEV * CAP), BF16),
             pltpu.VMEM((2 * NC, DEV * CAP), BF16),
+            pltpu.SemaphoreType.DMA((3,)),
         ],
         compiler_params=params(),
         cost_estimate=pl.CostEstimate(flops=400_000_000, bytes_accessed=200_000, transcendentals=0),
         name="gather",
-    )(got)
+    )(got, inner, outer)
 
 
 def body(volume_sens, stiffness, patch_of_row, knot_spans, span_params):
@@ -589,12 +579,11 @@
         patch_of_row.reshape(1, ROWS), knot_spans[0].T, span_params[0].T
     )
     za, zb = exchange(True, *corners(ya, yb, meta))
-    field, partial, keep, keep3 = interior(volume_sens, stiffness, ya, yb, to_patch, to_slot)
-    field, send = edges(
-        volume_sens, ya, yb, xa, xb, za, zb, to_patch, to_slot, meta, partial, keep, keep3, field
-    )
+    inner, inner_surface, keep, keep3 = interior(volume_sens, stiffness, ya, yb)
+    outer, outer_surface = edges(volume_sens, ya, yb, xa, xb, za, zb, keep, keep3)
+    send = pack(to_patch, to_slot, meta, outer_surface, inner_surface)
     got = lax.all_to_all(send, ("gx", "gy"), 0, 0, tiled=True)
-    return field, gather(got)
+    return gather(got, inner, outer)
 
 
 def solution(mesh):

time: 49.5 us -> 44.8 us (0.905)
  Pallas kernels: 17.2 us -> 12.4 us
    pallas_call x3 -> x4, Pallas kernels: 14.6 us -> 9.86 us  [the longest x1 4.5 us: interior(): pl.pallas_call(interior_kernel, out_shape=(rows, rows, jax.ShapeDtypeStru...]
  transfers between devices with their start and end apart: 6 -> 6, of which waited for: 1 -> 1; matrix products, arithmetic and copies ran while one was open for 0% -> 0% of each run, Pallas kernels for 20% -> 12%
where the time goes in v4:
time: 44.8 us; the launch traced here: 44.6 us
  blocking collectives  22.3 us (50%)
  Pallas kernels  12.4 us (28%)
  starting transfers between devices  8.12 us (18%)
  local copies, waits for them, and re-layouts  0.86 us (2%)
  between operations  0.75 us (2%)
    all_to_all x1, blocking collectives, body(): got = lax.all_to_all(send, ('gx', 'gy'), 0, 0, tiled=True)  22.3 us
    ppermute x6, starting transfers between devices, exchange(): return (lax.ppermute(one, both, first), lax.ppermute(two, both, second))  8.12 us
    pallas_call x1, Pallas kernels, interior(): pl.pallas_call(interior_kernel, out_shape=(rows, rows, jax.ShapeDtypeStru...  4.5 us
    pallas_call x1, Pallas kernels, gather(): pl.pallas_call(gather_kernel, out_shape=(jax.ShapeDtypeStruct((3, NX, NY,...  3.19 us
    pallas_call x1, Pallas kernels, messages(): pl.pallas_call(message_kernel, out_shape=(y_shape, y_shape, x_shape, x_sh...  1.55 us
    pallas_call x1, Pallas kernels, edges(): pl.pallas_call(edge_kernel, out_shape=(rows, rows), in_specs=[vmem()] * 9...  1.35 us
    pallas_call x1, Pallas kernels, route(): pl.pallas_call(route_kernel, out_shape=(jax.ShapeDtypeStruct((DEV, ROWS),...  1 us
  transfers between devices with their start and end apart: 6, of which 1 were waited for; matrix products, arithmetic and copies ran while one was open for 0% of the time, Pallas kernels for 12%

profile of v4, /device:TPU:1, one launch (start us, length us, event | category | flops | bytes accessed | tf_op | source)
XLA Modules:
  0.0 44.6 jit_solution(11002239518551223402)
XLA Ops:
  0.6 0.0 copy-start
  0.6 0.0 copy-start.1
  0.7 0.0 copy-start.2
  0.7 0.0 copy-start.4
  0.7 1.6 %messages.1 = (f32[416,128]{1,0:T(8,128)S(1)}, f32[416,128]{1,0:T(8,128)S(1)}, f32[13,32,128]{2,1,0:T(8,128)S(1)}, f32[13,32,128]{2,1,0:T(8,128)S(1)}) custom-call(f32[3,32,32,128]{3,2,1,0:T(8,128)} %vs.5, f32[32,32,128]{2,1,0:T(8,128)} %c.3), custom_call_target="tpu_custom_call" | custom-call | tf_op jit(solution)/shard_map/messages/pallas_call | solution.py:152
  2.2 2.1 %collective-permute-start = (f32[416,128]{1,0:T(8,128)S(1)}, f32[416,128]{1,0:T(8,128)S(1)}, u32[]{:S(2)}, u32[]{:S(2)}) collective-permute-start(f32[416,128]{1,0:T(8,128)S(1)} %get-tuple-element.20), channel_id=1, source_target_pairs={{0,1},{1,0},{2,3},{3,2},{4,5},{5,4},{6,7},{7,6},{8,9},{9,8},{10,11... | collective-permute-start | bytes 638984 | tf_op jit(solution)/shard_map/ppermute | solution.py:58
  4.4 1.0 %collective-permute-start.1 = (f32[416,128]{1,0:T(8,128)S(1)}, f32[416,128]{1,0:T(8,128)S(1)}, u32[]{:S(2)}, u32[]{:S(2)}) collective-permute-start(f32[416,128]{1,0:T(8,128)S(1)} %get-tuple-element.21), channel_id=1, source_target_pairs={{0,16},{1,2},{2,1},{3,4},{4,3},{5,6},{6,5},{7,8},{8,7},{9,10},{10,... | collective-permute-start | bytes 638984 | tf_op jit(solution)/shard_map/ppermute | solution.py:58
  5.3 0.0 collective-permute-start.2
  5.3 1.7 %collective-permute-start.3 = (f32[13,32,128]{2,1,0:T(8,128)S(1)}, f32[13,32,128]{2,1,0:T(8,128)S(1)}, u32[]{:S(2)}, u32[]{:S(2)}) collective-permute-start(f32[13,32,128]{2,1,0:T(8,128)S(1)} %get-tuple-element.23), channel_id=1, source_target_pairs={{0,1},{1,0},{2,3},{3,2},{4,5},{5,4},{6,7},{7,6},{8,9},{9,8},{10,11... | collective-permute-start | bytes 638984 | tf_op jit(solution)/shard_map/ppermute | solution.py:58
  7.0 0.0 copy-done.2
  7.0 0.0 copy-done.4
  7.0 0.0 copy-start.3
  7.0 0.7 %copy-done.3 = f32[1,1024,2]{1,2,0:T(2,128)S(1)} copy-done((f32[1,1024,2]{1,2,0:T(2,128)S(1)}, f32[1,1024,2]{1,2,0:T(2,128)}, u32[]{:S(2)}) %copy-start.3) | copy-done | bytes 8216
  7.7 1.0 %route.1 = (bf16[128,1024]{1,0:T(8,128)(2,1)S(1)}, f32[32,1024]{1,0:T(8,128)S(1)}, f32[128,128]{1,0:T(8,128)S(1)}) custom-call(s32[1,1024]{1,0:T(1,128)S(1)} %bitcast.15, s32[2,1024]{1,0:T(2,128)S(1)} %bitcast.13, f32[2,1024]{1,0:T(2,128)S(1)} %bitcast.14), custom_call_target="tpu_custom_call" | custom-call | flops 400000000 | bytes 2000000 | tf_op jit(solution)/shard_map/route/pallas_call | solution.py:238
  8.7 0.1 collective-permute-done.ya
  8.8 0.0 collective-permute-done.1.yb
  8.9 1.8 %collective-permute-start.4 = (f32[13,8,128]{2,1,0:T(8,128)S(1)}, f32[13,8,128]{2,1,0:T(8,128)S(1)}, u32[]{:S(2)}, u32[]{:S(2)}) collective-permute-start(f32[13,8,128]{2,1,0:T(8,128)S(1)} %get-tuple-element.24), channel_id=1, source_target_pairs={{0,16},{1,17},{2,18},{3,19},{4,20},{5,21},{6,22},{7,23},{8,24},{9,... | collective-permute-start | bytes 159752 | tf_op jit(solution)/shard_map/ppermute | solution.py:58
  10.7 1.5 %collective-permute-start.5 = (f32[13,8,128]{2,1,0:T(8,128)S(1)}, f32[13,8,128]{2,1,0:T(8,128)S(1)}, u32[]{:S(2)}, u32[]{:S(2)}) collective-permute-start(f32[13,8,128]{2,1,0:T(8,128)S(1)} %get-tuple-element.25), channel_id=1, source_target_pairs={{0,1},{1,0},{2,3},{3,2},{4,5},{5,4},{6,7},{7,6},{8,9},{9,8},{10,11... | collective-permute-start | bytes 159752 | tf_op jit(solution)/shard_map/ppermute | solution.py:58
  12.2 0.0 copy-done
  12.2 0.0 copy-done.1
  12.2 4.5 %interior.1 = (f32[3,24,32,128]{3,2,1,0:T(8,128)S(1)}, f32[3,24,32,128]{3,2,1,0:T(8,128)S(1)}, f32[6,10,40,128]{3,2,1,0:T(8,128)S(1)}, f32[3,3,10,40,128]{4,3,2,1,0:T(8,128)S(1)}) custom-call(f32[3,32,32,128]{3,2,1,0:T(8,128)S(1)} %copy-done, f32[32,32,128]{2,1,0:T(8,128)S(1)} %copy-done.1, f32[416,128]{1,0:T(8,128)S(1)} %collective-permute-done.ya, ...), custom_call_target="tpu_custom_call" | custom-call | flops 60000000 | bytes 6000000 | tf_op jit(solution)/shard_map/interior/pallas_call | solution.py:374
  16.7 0.0 collective-permute-done.2.xa
  16.7 0.0 collective-permute-done.3.xb
  16.7 0.0 collective-permute-done.4.za
  16.8 0.0 collective-permute-done.5.zb
  16.8 1.3 %edges.1 = (f32[3,8,32,128]{3,2,1,0:T(8,128)S(1)}, f32[3,8,32,128]{3,2,1,0:T(8,128)S(1)}) custom-call(f32[3,32,32,128]{3,2,1,0:T(8,128)S(1)} %copy-done, f32[416,128]{1,0:T(8,128)S(1)} %collective-permute-done.ya, f32[416,128]{1,0:T(8,128)S(1)} %collective-permute-done.1.yb, f32[13,32,128]{2,1,0:T(8,128)S(1)} %collective-permute-done.2.xa, ...), custom_call_target="tpu_custom_call" | custom-call | flops 20000000 | bytes 2000000 | tf_op jit(solution)/shard_map/edges/pallas_call | solution.py:447
  18.1 0.8 %pack.1 = f32[128,256]{1,0:T(8,128)S(1)} custom-call(bf16[128,1024]{1,0:T(8,128)(2,1)S(1)} %get-tuple-element.17.to_patch, f32[32,1024]{1,0:T(8,128)S(1)} %get-tuple-element.18.to_slot, f32[128,128]{1,0:T(8,128)S(1)} %get-tuple-element.19._.meta, f32[3,8,32,128]{3,2,1,0:T(8,128)S(1)} %get-tuple-element.28.outer, f32[3,24,32,128]{3,2,1,0:T(8,128)S(1)} %get-tuple-element.29.inner), custom_call_target="tpu_custom_call" | custom-call | tf_op jit(solution)/shard_map/pack/pallas_call | solution.py:486
  18.9 0.1 copy.7
  19.1 22.3 %all_to_all.11 = f32[128,1,256]{2,1,0:T(1,128)S(1)} all-to-all(f32[128,1,256]{2,1,0:T(1,128)S(1)} %copy.7), channel_id=1, replica_groups=mesh['gx'=8,'gy'=16] {'gx','gy'}, dimensions={0} | all-to-all | bytes 262144 | tf_op jit(solution)/shard_map/all_to_all | solution.py:585
  41.4 3.2 %gather.1 = (f32[3,32,32,128]{3,2,1,0:T(8,128)}, f32[1,3,64,64]{3,2,1,0:T(8,128)}) custom-call(f32[128,256]{1,0:T(8,128)S(1)} %bitcast.12, f32[3,24,32,128]{3,2,1,0:T(8,128)S(1)} %get-tuple-element.30.inner, f32[3,8,32,128]{3,2,1,0:T(8,128)S(1)} %get-tuple-element.31.outer), custom_call_target="tpu_custom_call" | custom-call | flops 400000000 | bytes 200000 | tf_op jit(solution)/shard_map/gather/pallas_call | solution.py:551
  (2 shorter events, 0.0 us)
Async XLA Ops:
  0.6 11.6 %copy-start = (f32[3,32,32,128]{3,2,1,0:T(8,128)S(1)}, f32[3,32,32,128]{3,2,1,0:T(8,128)}, u32[]{:S(2)}) copy-start(f32[3,32,32,128]{3,2,1,0:T(8,128)} %vs.5) | copy-start | bytes 4718596
  0.6 11.6 %copy-start.1 = (f32[32,32,128]{2,1,0:T(8,128)S(1)}, f32[32,32,128]{2,1,0:T(8,128)}, u32[]{:S(2)}) copy-start(f32[32,32,128]{2,1,0:T(8,128)} %c.3) | copy-start | bytes 1572868
  0.7 6.4 %copy-start.2 = (s32[1,1024,2]{1,2,0:T(2,128)S(1)}, s32[1,1024,2]{1,2,0:T(2,128)}, u32[]{:S(2)}) copy-start(s32[1,1024,2]{1,2,0:T(2,128)} %param.8) | copy-start | bytes 24580
  0.7 6.3 %copy-start.4 = (s32[1,1024,1]{1,2,0:T(1,128)S(1)}, s32[1,1024,1]{1,2,0:T(1,128)}, u32[]{:S(2)}) copy-start(s32[1,1024,1]{1,2,0:T(1,128)} %param.7) | copy-start | bytes 12292
  2.2 6.6 %collective-permute-start = (f32[416,128]{1,0:T(8,128)S(1)}, f32[416,128]{1,0:T(8,128)S(1)}, u32[]{:S(2)}, u32[]{:S(2)}) collective-permute-start(f32[416,128]{1,0:T(8,128)S(1)} %get-tuple-element.20), channel_id=1, source_target_pairs={{0,1},{1,0},{2,3},{3,2},{4,5},{5,4},{6,7},{7,6},{8,9},{9,8},{10,11... | collective-permute-start | bytes 638984 | tf_op jit(solution)/shard_map/ppermute | solution.py:58
  4.4 4.5 %collective-permute-start.1 = (f32[416,128]{1,0:T(8,128)S(1)}, f32[416,128]{1,0:T(8,128)S(1)}, u32[]{:S(2)}, u32[]{:S(2)}) collective-permute-start(f32[416,128]{1,0:T(8,128)S(1)} %get-tuple-element.21), channel_id=1, source_target_pairs={{0,16},{1,2},{2,1},{3,4},{4,3},{5,6},{6,5},{7,8},{8,7},{9,10},{10,... | collective-permute-start | bytes 638984 | tf_op jit(solution)/shard_map/ppermute | solution.py:58
  5.3 11.4 %collective-permute-start.2 = (f32[13,32,128]{2,1,0:T(8,128)S(1)}, f32[13,32,128]{2,1,0:T(8,128)S(1)}, u32[]{:S(2)}, u32[]{:S(2)}) collective-permute-start(f32[13,32,128]{2,1,0:T(8,128)S(1)} %get-tuple-element.22), channel_id=1, source_target_pairs={{0,16},{1,17},{2,18},{3,19},{4,20},{5,21},{6,22},{7,23},{8,24},{9,... | collective-permute-start | bytes 638984 | tf_op jit(solution)/shard_map/ppermute | solution.py:58
  5.3 11.4 %collective-permute-start.3 = (f32[13,32,128]{2,1,0:T(8,128)S(1)}, f32[13,32,128]{2,1,0:T(8,128)S(1)}, u32[]{:S(2)}, u32[]{:S(2)}) collective-permute-start(f32[13,32,128]{2,1,0:T(8,128)S(1)} %get-tuple-element.23), channel_id=1, source_target_pairs={{0,1},{1,0},{2,3},{3,2},{4,5},{5,4},{6,7},{7,6},{8,9},{9,8},{10,11... | collective-permute-start | bytes 638984 | tf_op jit(solution)/shard_map/ppermute | solution.py:58
  7.0 0.7 %copy-start.3 = (f32[1,1024,2]{1,2,0:T(2,128)S(1)}, f32[1,1024,2]{1,2,0:T(2,128)}, u32[]{:S(2)}) copy-start(f32[1,1024,2]{1,2,0:T(2,128)} %param.9) | copy-start | bytes 24580
  8.9 7.9 %collective-permute-start.4 = (f32[13,8,128]{2,1,0:T(8,128)S(1)}, f32[13,8,128]{2,1,0:T(8,128)S(1)}, u32[]{:S(2)}, u32[]{:S(2)}) collective-permute-start(f32[13,8,128]{2,1,0:T(8,128)S(1)} %get-tuple-element.24), channel_id=1, source_target_pairs={{0,16},{1,17},{2,18},{3,19},{4,20},{5,21},{6,22},{7,23},{8,24},{9,... | collective-permute-start | bytes 159752 | tf_op jit(solution)/shard_map/ppermute | solution.py:58
  10.7 6.1 %collective-permute-start.5 = (f32[13,8,128]{2,1,0:T(8,128)S(1)}, f32[13,8,128]{2,1,0:T(8,128)S(1)}, u32[]{:S(2)}, u32[]{:S(2)}) collective-permute-start(f32[13,8,128]{2,1,0:T(8,128)S(1)} %get-tuple-element.25), channel_id=1, source_target_pairs={{0,1},{1,0},{2,3},{3,2},{4,5},{5,4},{6,7},{7,6},{8,9},{9,8},{10,11... | collective-permute-start | bytes 159752 | tf_op jit(solution)/shard_map/ppermute | solution.py:58

commit v5 on v4

--- a/solution.py
+++ b/solution.py
@@ -47,7 +47,7 @@
         for j in range(count_y):
             if along_x:
                 near, far = (i ^ 1, j), (partner(i, count_x - 1), j)
-                far = (i, j ^ 1) if far == (i, j) else far
+                far = (count_x - 1 - i, j) if far == (i, j) else far
             else:
                 near, far = (i, j ^ 1), (i, partner(j, count_y - 1))
                 far = (i ^ 1, j) if far == (i, j) else far
@@ -171,7 +171,7 @@
     return jnp.where(even == before, two[rows], one[rows])
 
 
-def corner_kernel(ya, yb, _, one, two):
+def corner_kernel(ya, yb, _, __, one, two):
     even_x = is_even("gx")
     even_y = is_even("gy")
     inside_x = jnp.where(at_end("gx"), 0.0, 1.0)
@@ -190,16 +190,16 @@
             two[i, spot] = jnp.where(even_x, low, high) * inside_x
 
 
-def corners(ya, yb, meta):
+def corners(ya, yb, meta, early):
     shape = jax.ShapeDtypeStruct((13, 8, NZ), F32)
     return pl.pallas_call(
         corner_kernel,
         out_shape=(shape, shape),
-        in_specs=[vmem()] * 3,
+        in_specs=[vmem()] * 4,
         out_specs=(vmem(), vmem()),
         compiler_params=params(),
         name="corners",
-    )(ya, yb, meta)
+    )(ya, yb, meta, early)
 
 
 def route_kernel(patch, spans, par, to_patch, to_slot, meta):
@@ -280,21 +280,66 @@
 MIDDLE = list(range(9, 31))
 
 
+class Joined:
+    def __init__(self, whole, rest, ahead):
+        self.whole, self.rest, self.ahead = whole, rest, ahead
+
+    def __getitem__(self, x):
+        if x in EDGE:
+            return self.whole[EDGE.index(x)]
+        spot = MIDDLE.index(x)
+        return jnp.concatenate(
+            [self.rest[spot, 16:24], self.ahead[x - 5, 8:24], self.rest[spot, 0:16]], axis=0
+        )
+
+    def __setitem__(self, x, value):
+        if x in EDGE:
+            spot = EDGE.index(x)
+            self.whole[spot, 24:40] = value[0:16]
+            self.whole[spot, 8:24] = self.ahead[x - 5, 8:24]
+            self.whole[spot, 0:8] = value[16:24]
+        else:
+            self.rest[MIDDLE.index(x)] = value
+
+
+def all_rows(v):
+    return v
+
+
+def outer_rows(v):
+    return jnp.concatenate([v[24:40], v[0:8]], axis=0)
+
+
+def last_outer_rows(v):
+    return jnp.concatenate([v[24:32], v[0:8]], axis=0)
+
+
+def inner_rows(v):
+    return v[8:24]
+
+
+def center_rows(v):
+    return v[0:NY]
+
+
 class Stencil:
-    def __init__(self, stiff, ratio, wx, wy, wz, scale, y0, y1, y2):
+    def __init__(self, part, last_part, height, stiff, ratio, wx, wy, wz, scale, y0, y1, y2):
+        self.part, self.last_part = part, last_part
         self.stiff, self.ratio, self.scale = stiff, ratio, scale
         self.wx, self.wy, self.wz = wx, wy, wz
         self.fields = (y0, y1, y2)
-        lane = lax.broadcasted_iota(jnp.int32, (EY, NZ), 1)
+        lane = lax.broadcasted_iota(jnp.int32, (height, NZ), 1)
         self.not_last = lane < NZ - 1
         self.not_first = lane > 0
 
     def prepare(self, x, source):
-        here, after, before = self.stiff[x], self.stiff[x + 1], self.stiff[x - 1]
-        y_next = up(here)
+        part = self.part
+        whole = self.stiff[x]
+        here, after, before = part(whole), part(self.stiff[x + 1]), part(self.stiff[x - 1])
+        y_next = part(up(whole))
         z_next = jnp.where(self.not_last, pltpu.roll(here, NZ - 1, 1), 0.0)
         z_prev = jnp.where(self.not_first, pltpu.roll(here, 1, 1), 0.0)
-        sides = (before + after) + (y_next + down(here)) + (z_next + z_prev)
+        sides = (before + after) + (y_next + part(down(whole))) + (z_next + z_prev)
         diag = 3.0 * here + 0.5 * sides
         inverse = jnp.where(here > 0.0, 1.0 / diag, 0.0)
         self.ratio[x] = OMEGA * inverse
@@ -305,31 +350,70 @@
         for k in range(3):
             self.fields[0][k][x] = source(k, x) * inverse
 
-    def update(self, level, k, x):
+    def update(self, level, k, x, part):
         source = self.fields[level][k]
-        here = source[x]
-        face_y, face_z = self.wy[x], self.wz[x]
-        total = self.wx[x] * source[x + 1] + self.wx[x - 1] * source[x - 1]
-        total = total + (face_y * up(here) + down(face_y * here))
+        whole, face_y = source[x], self.wy[x]
+        here, face_z = part(whole), part(self.wz[x])
+        total = part(self.wx[x]) * part(source[x + 1]) + part(self.wx[x - 1]) * part(source[x - 1])
+        total = total + (part(face_y) * part(up(whole)) + part(down(face_y * whole)))
         total = total + (
             face_z * pltpu.roll(here, NZ - 1, 1) + pltpu.roll(face_z * here, 1, 1)
         )
-        return self.fields[0][k][x] + KEEP * here + self.ratio[x] * total
+        return part(self.fields[0][k][x]) + KEEP * here + part(self.ratio[x]) * total
 
     def sweep(self, level, rows):
         for x in rows:
             for k in range(3):
-                self.fields[level + 1][k][x] = self.update(level, k, x)
+                self.fields[level + 1][k][x] = self.update(level, k, x, self.part)
 
     def finish(self, x, out, surface, index):
         for k in range(3):
-            fresh = self.update(2, k, x)[0:NY]
+            fresh = self.update(2, k, x, self.last_part)
             surface[k, index] = fresh
-            out[k, index] = fresh * self.scale[x][0:NY]
+            out[k, index] = fresh * self.last_part(self.scale[x])
+
+
+PREPARED = list(range(5, 35))
+
+
+def ahead_kernel(vs, c, out, surface, planes, cubes):
+    class Given:
+        def __getitem__(self, x):
+            return c[x - 4]
+
+    fields = [[Rows().hold(cubes.at[n, k], PREPARED) for k in range(3)] for n in range(3)]
+    grid = Stencil(
+        all_rows, inner_rows, NY, Given(),
+        *(Rows().hold(planes.at[n], PREPARED) for n in range(5)), *fields,
+    )
+    for x in range(5, 35):
+        grid.prepare(x, lambda k, x: vs[k, x - 4])
+    grid.sweep(0, range(6, 34))
+    grid.sweep(1, range(7, 33))
+    for x in range(8, 32):
+        grid.finish(x, out, surface, x - 8)
+
+
+def ahead(vs, c):
+    rows = jax.ShapeDtypeStruct((3, 24, 16, NZ), F32)
+    return pl.pallas_call(
+        ahead_kernel,
+        out_shape=(
+            rows,
+            rows,
+            jax.ShapeDtypeStruct((5, len(PREPARED), NY, NZ), F32),
+            jax.ShapeDtypeStruct((3, 3, len(PREPARED), NY, NZ), F32),
+        ),
+        in_specs=[vmem()] * 2,
+        out_specs=(vmem(),) * 4,
+        compiler_params=params(),
+        cost_estimate=pl.CostEstimate(flops=60_000_000, bytes_accessed=6_000_000, transcendentals=0),
+        name="ahead",
+    )(vs, c)
 
 
 def interior_kernel(
-    vs, c, ya, yb, out, surface, keep, keep3, stiff, mids, mids3,
+    vs, c, ya, yb, planes, cubes, out, surface, keep, keep3, stiff, rest, rest3, halo,
 ):
     even_y = is_even("gy")
     for x in range(NX):
@@ -340,24 +424,18 @@
     for x in range(1, NX - 1):
         for k in range(3):
             row = 9 * x + 3 * k
-            place = (keep3.at[0, k], EDGE.index(x + 4)) if x + 4 in EDGE else (mids3.at[0, k], x - 5)
-            ref, index = place
-            ref[index, NY : NY + 3] = y_halo(even_y, ya, yb, row, 3, False)
-            ref[index, EY - 3 : EY] = y_halo(even_y, ya, yb, row, 3, True)
+            halo[k, x, 0:3] = y_halo(even_y, ya, yb, row, 3, False)
+            halo[k, x, 5:8] = y_halo(even_y, ya, yb, row, 3, True)
 
     def source(k, x):
-        ref, index = fields[0][k].place[x]
-        return jnp.concatenate([vs[k, x - 4], ref[index, NY:EY]], axis=0)
-
-    def plane(n):
-        return Rows().hold(keep.at[n], EDGE).hold(mids.at[n], MIDDLE)
+        return jnp.concatenate([vs[k, x - 4, 24:32], halo[k, x - 4], vs[k, x - 4, 0:8]], axis=0)
 
     fields = [
-        [Rows().hold(keep3.at[n, k], EDGE).hold(mids3.at[n, k], MIDDLE) for k in range(3)]
-        for n in range(3)
+        [Joined(keep3.at[n, k], rest3.at[n, k], cubes.at[n, k]) for k in range(3)] for n in range(3)
     ]
     grid = Stencil(
-        Rows().hold(stiff, range(4, 36)), plane(0), plane(1), plane(2), plane(3), plane(4), *fields
+        outer_rows, last_outer_rows, 24, Rows().hold(stiff, range(4, 36)),
+        *(Joined(keep.at[n], rest.at[n], planes.at[n]) for n in range(5)), *fields,
     )
     for x in (4, 5, 34, 35):
         keep[5, EDGE.index(x)] = grid.stiff[x]
@@ -369,8 +447,8 @@
         grid.finish(x, out, surface, x - 8)
 
 
-def interior(vs, c, ya, yb):
-    rows = jax.ShapeDtypeStruct((3, 24, NY, NZ), F32)
+def interior(vs, c, ya, yb, planes, cubes):
+    rows = jax.ShapeDtypeStruct((3, 24, 16, NZ), F32)
     return pl.pallas_call(
         interior_kernel,
         out_shape=(
@@ -379,17 +457,18 @@
             jax.ShapeDtypeStruct((6, len(EDGE), EY, NZ), F32),
             jax.ShapeDtypeStruct((3, 3, len(EDGE), EY, NZ), F32),
         ),
-        in_specs=[vmem()] * 4,
+        in_specs=[vmem()] * 6,
         out_specs=(vmem(),) * 4,
         scratch_shapes=[
             pltpu.VMEM((NX, EY, NZ), F32),
-            pltpu.VMEM((5, len(MIDDLE), EY, NZ), F32),
-            pltpu.VMEM((3, 3, len(MIDDLE), EY, NZ), F32),
+            pltpu.VMEM((5, len(MIDDLE), 24, NZ), F32),
+            pltpu.VMEM((3, 3, len(MIDDLE), 24, NZ), F32),
+            pltpu.VMEM((3, NX, 8, NZ), F32),
         ],
         compiler_params=params(),
         cost_estimate=pl.CostEstimate(flops=60_000_000, bytes_accessed=6_000_000, transcendentals=0),
         name="interior",
-    )(vs, c, ya, yb)
+    )(vs, c, ya, yb, planes, cubes)
 
 
 def edge_kernel(
@@ -433,7 +512,7 @@
     fields = [
         [hold(fresh3, n, k, rows) for k in range(3)] for n, rows in enumerate((first, second, third))
     ]
-    grid = Stencil(Given(), *planes, *fields)
+    grid = Stencil(all_rows, center_rows, EY, Given(), *planes, *fields)
     for x in first:
         grid.prepare(x, source)
     grid.sweep(0, second)
@@ -459,17 +538,18 @@
     )(vs, ya, yb, xa, xb, za, zb, keep, keep3)
 
 
-def pack_kernel(to_patch, to_slot, meta, outer, inner, send):
+def pack_kernel(to_patch, to_slot, meta, outer, inner, early, send):
     column = lax.broadcasted_iota(jnp.int32, (DEV, NZ), 1)
     values = []
     for block in range(ROWS // DEV):
-        if block == 0:
-            ref, part = outer, slice(0, 4)
-        elif block == 7:
-            ref, part = outer, slice(4, 8)
-        else:
-            ref, part = inner, slice(4 * block - 4, 4 * block)
-        first, second, third = (ref[k, part].reshape(DEV, NZ) for k in range(3))
+        pieces_of = [[], [], []]
+        for k in range(3):
+            for x in range(4 * block, 4 * block + 4):
+                if 4 <= x < 28:
+                    pieces_of[k] += [inner[k, x - 4, 8:16], early[k, x - 4], inner[k, x - 4, 0:8]]
+                else:
+                    pieces_of[k].append(outer[k, x if x < 4 else x - 24])
+        first, second, third = (jnp.concatenate(p, axis=0) for p in pieces_of)
         mixed = jnp.where(column == 1, pltpu.roll(second, 1, 1), first)
         mixed = jnp.where(column == 2, pltpu.roll(third, 2, 1), mixed)
         values.append(OMEGA * mixed.T[0:3])
@@ -482,15 +562,15 @@
     send[:, 128:256] = jnp.concatenate([sent, jnp.zeros((CAP, DEV), F32)], axis=0).T
 
 
-def pack(to_patch, to_slot, meta, outer, inner):
+def pack(to_patch, to_slot, meta, outer, inner, early):
     return pl.pallas_call(
         pack_kernel,
         out_shape=jax.ShapeDtypeStruct((DEV, 256), F32),
-        in_specs=[vmem()] * 5,
+        in_specs=[vmem()] * 6,
         out_specs=vmem(),
         compiler_params=params(),
         name="pack",
-    )(to_patch, to_slot, meta, outer, inner)
+    )(to_patch, to_slot, meta, outer, inner, early)
 
 
 def pieces(param):
@@ -503,9 +583,11 @@
     ]
 
 
-def gather_kernel(got, inner, outer, field, grads, table, left, right, sems):
+def gather_kernel(got, early, inner, outer, field, grads, table, left, right, sems):
     writes = [
-        pltpu.make_async_copy(inner, field.at[:, 4:28], sems.at[0]),
+        pltpu.make_async_copy(early, field.at[:, 4:28, 8:24], sems.at[0]),
+        pltpu.make_async_copy(inner.at[:, :, 0:8], field.at[:, 4:28, 24:32], sems.at[3]),
+        pltpu.make_async_copy(inner.at[:, :, 8:16], field.at[:, 4:28, 0:8], sems.at[4]),
         pltpu.make_async_copy(outer.at[:, 0:4], field.at[:, 0:4], sems.at[1]),
         pltpu.make_async_copy(outer.at[:, 4:8], field.at[:, 28:32], sems.at[2]),
     ]
@@ -547,25 +629,25 @@
         write.wait()
 
 
-def gather(got, inner, outer):
+def gather(got, early, inner, outer):
     return pl.pallas_call(
         gather_kernel,
         out_shape=(
             jax.ShapeDtypeStruct((3, NX, NY, NZ), F32),
             jax.ShapeDtypeStruct((1, 3, NC, NC), F32),
         ),
-        in_specs=[vmem()] * 3,
+        in_specs=[vmem()] * 4,
         out_specs=(pl.BlockSpec(memory_space=pl.ANY), vmem()),
         scratch_shapes=[
             pltpu.VMEM((256, DEV), F32),
             pltpu.VMEM((6 * NC, DEV * CAP), BF16),
             pltpu.VMEM((2 * NC, DEV * CAP), BF16),
-            pltpu.SemaphoreType.DMA((3,)),
+            pltpu.SemaphoreType.DMA((5,)),
         ],
         compiler_params=params(),
         cost_estimate=pl.CostEstimate(flops=400_000_000, bytes_accessed=200_000, transcendentals=0),
         name="gather",
-    )(got, inner, outer)
+    )(got, early, inner, outer)
 
 
 def body(volume_sens, stiffness, patch_of_row, knot_spans, span_params):
@@ -578,12 +660,13 @@
     to_patch, to_slot, meta = route(
         patch_of_row.reshape(1, ROWS), knot_spans[0].T, span_params[0].T
     )
-    za, zb = exchange(True, *corners(ya, yb, meta))
-    inner, inner_surface, keep, keep3 = interior(volume_sens, stiffness, ya, yb)
+    early, early_surface, planes, cubes = ahead(volume_sens, stiffness)
+    za, zb = exchange(True, *corners(ya, yb, meta, early_surface))
+    inner, inner_surface, keep, keep3 = interior(volume_sens, stiffness, ya, yb, planes, cubes)
     outer, outer_surface = edges(volume_sens, ya, yb, xa, xb, za, zb, keep, keep3)
-    send = pack(to_patch, to_slot, meta, outer_surface, inner_surface)
+    send = pack(to_patch, to_slot, meta, outer_surface, inner_surface, early_surface)
     got = lax.all_to_all(send, ("gx", "gy"), 0, 0, tiled=True)
-    return gather(got, inner, outer)
+    return gather(got, early, inner, outer)
 
 
 def solution(mesh):

time: 44.8 us -> 43.7 us (0.975)
  starting transfers between devices: 8.12 us -> 6.54 us
  Pallas kernels: 12.4 us -> 13.5 us
  local copies, waits for them, and re-layouts: 0.86 us -> 0.17 us
  waiting for transfers between devices: 0.12 us -> 0.67 us
    pallas_call x0 -> x1, Pallas kernels: none -> 2.93 us  [ahead(): pl.pallas_call(ahead_kernel, out_shape=(rows, rows, jax.ShapeDtypeStruct(...]
    pallas_call x1, Pallas kernels: 4.5 us -> 2.62 us  [interior(): pl.pallas_call(interior_kernel, out_shape=(rows, rows, jax.ShapeDtypeStru...]
    ppermute x6, starting transfers between devices: 8.12 us -> 6.54 us  [exchange(): return (lax.ppermute(one, both, first), lax.ppermute(two, both, second))]
    unnamed x11, local copies, waits for them, and re-layouts: 0.72 us -> 0.03 us
    ppermute x6, waiting for transfers between devices: 0.12 us -> 0.67 us  [exchange(): return (lax.ppermute(one, both, first), lax.ppermute(two, both, second))]
  transfers between devices with their start and end apart: 6 -> 6, of which waited for: 1 -> 1; matrix products, arithmetic and copies ran while one was open for 0% -> 0% of each run, Pallas kernels for 12% -> 15%
where the time goes in v5:
time: 43.7 us; the launch traced here: 43.6 us
  blocking collectives  22 us (50%)
  Pallas kernels  13.5 us (31%)
  starting transfers between devices  6.54 us (15%)
  between operations  0.79 us (2%)
  waiting for transfers between devices  0.67 us (2%)
    all_to_all x1, blocking collectives, body(): got = lax.all_to_all(send, ('gx', 'gy'), 0, 0, tiled=True)  22 us
    ppermute x6, starting transfers between devices, exchange(): return (lax.ppermute(one, both, first), lax.ppermute(two, both, second))  6.54 us
    pallas_call x1, Pallas kernels, gather(): pl.pallas_call(gather_kernel, out_shape=(jax.ShapeDtypeStruct((3, NX, NY,...  3.23 us
    pallas_call x1, Pallas kernels, ahead(): pl.pallas_call(ahead_kernel, out_shape=(rows, rows, jax.ShapeDtypeStruct(...  2.93 us
    pallas_call x1, Pallas kernels, interior(): pl.pallas_call(interior_kernel, out_shape=(rows, rows, jax.ShapeDtypeStru...  2.62 us
    pallas_call x1, Pallas kernels, messages(): pl.pallas_call(message_kernel, out_shape=(y_shape, y_shape, x_shape, x_sh...  1.55 us
    pallas_call x1, Pallas kernels, edges(): pl.pallas_call(edge_kernel, out_shape=(rows, rows), in_specs=[vmem()] * 9...  1.28 us
    pallas_call x1, Pallas kernels, route(): pl.pallas_call(route_kernel, out_shape=(jax.ShapeDtypeStruct((DEV, ROWS),...  0.99 us
  transfers between devices with their start and end apart: 6, of which 1 were waited for; matrix products, arithmetic and copies ran while one was open for 0% of the time, Pallas kernels for 15%

profile of v5, /device:TPU:1, one launch (start us, length us, event | category | flops | bytes accessed | tf_op | source)
XLA Modules:
  0.0 43.6 jit_solution(16563007495379694230)
XLA Ops:
  0.6 0.0 copy-start
  0.6 0.0 copy-start.1
  0.7 0.0 copy-start.4
  0.7 0.0 copy-start.2
  0.7 0.0 copy-start.3
  0.7 1.6 %messages.1 = (f32[416,128]{1,0:T(8,128)S(1)}, f32[416,128]{1,0:T(8,128)S(1)}, f32[13,32,128]{2,1,0:T(8,128)S(1)}, f32[13,32,128]{2,1,0:T(8,128)S(1)}) custom-call(f32[3,32,32,128]{3,2,1,0:T(8,128)} %vs.7, f32[32,32,128]{2,1,0:T(8,128)} %c.5), custom_call_target="tpu_custom_call" | custom-call | tf_op jit(solution)/shard_map/messages/pallas_call | solution.py:152
  2.2 2.1 %collective-permute-start = (f32[416,128]{1,0:T(8,128)S(1)}, f32[416,128]{1,0:T(8,128)S(1)}, u32[]{:S(2)}, u32[]{:S(2)}) collective-permute-start(f32[416,128]{1,0:T(8,128)S(1)} %get-tuple-element.24), channel_id=1, source_target_pairs={{0,1},{1,0},{2,3},{3,2},{4,5},{5,4},{6,7},{7,6},{8,9},{9,8},{10,11... | collective-permute-start | bytes 638984 | tf_op jit(solution)/shard_map/ppermute | solution.py:58
  4.4 1.0 %collective-permute-start.1 = (f32[416,128]{1,0:T(8,128)S(1)}, f32[416,128]{1,0:T(8,128)S(1)}, u32[]{:S(2)}, u32[]{:S(2)}) collective-permute-start(f32[416,128]{1,0:T(8,128)S(1)} %get-tuple-element.25), channel_id=1, source_target_pairs={{0,16},{1,2},{2,1},{3,4},{4,3},{5,6},{6,5},{7,8},{8,7},{9,10},{10,... | collective-permute-start | bytes 638984 | tf_op jit(solution)/shard_map/ppermute | solution.py:58
  5.3 0.0 collective-permute-start.2
  5.3 1.7 %collective-permute-start.3 = (f32[13,32,128]{2,1,0:T(8,128)S(1)}, f32[13,32,128]{2,1,0:T(8,128)S(1)}, u32[]{:S(2)}, u32[]{:S(2)}) collective-permute-start(f32[13,32,128]{2,1,0:T(8,128)S(1)} %get-tuple-element.27), channel_id=1, source_target_pairs={{0,112},{1,113},{2,114},{3,115},{4,116},{5,117},{6,118},{7,119},{8... | collective-permute-start | bytes 638984 | tf_op jit(solution)/shard_map/ppermute | solution.py:58
  7.0 0.0 copy-done
  7.0 0.0 copy-done.1
  7.0 2.9 %ahead.1 = (f32[3,24,16,128]{3,2,1,0:T(8,128)S(1)}, f32[3,24,16,128]{3,2,1,0:T(8,128)S(1)}, f32[5,30,32,128]{3,2,1,0:T(8,128)S(1)}, f32[3,3,30,32,128]{4,3,2,1,0:T(8,128)S(1)}) custom-call(f32[3,32,32,128]{3,2,1,0:T(8,128)S(1)} %copy-done, f32[32,32,128]{2,1,0:T(8,128)S(1)} %copy-done.1), custom_call_target="tpu_custom_call" | custom-call | flops 60000000 | bytes 6000000 | tf_op jit(solution)/shard_map/ahead/pallas_call | solution.py:399
  10.0 0.0 copy-done.4
  10.0 0.0 copy-done.2
  10.0 0.0 copy-done.3
  10.0 1.0 %route.1 = (bf16[128,1024]{1,0:T(8,128)(2,1)S(1)}, f32[32,1024]{1,0:T(8,128)S(1)}, f32[128,128]{1,0:T(8,128)S(1)}) custom-call(s32[1,1024]{1,0:T(1,128)S(1)} %bitcast.15, s32[2,1024]{1,0:T(2,128)S(1)} %bitcast.13, f32[2,1024]{1,0:T(2,128)S(1)} %bitcast.14), custom_call_target="tpu_custom_call" | custom-call | flops 400000000 | bytes 2000000 | tf_op jit(solution)/shard_map/route/pallas_call | solution.py:238
  11.0 0.0 collective-permute-done.ya
  11.0 0.0 collective-permute-done.1.yb
  11.1 1.5 %collective-permute-start.4 = (f32[13,8,128]{2,1,0:T(8,128)S(1)}, f32[13,8,128]{2,1,0:T(8,128)S(1)}, u32[]{:S(2)}, u32[]{:S(2)}) collective-permute-start(f32[13,8,128]{2,1,0:T(8,128)S(1)} %get-tuple-element.29), channel_id=1, source_target_pairs={{0,16},{1,17},{2,18},{3,19},{4,20},{5,21},{6,22},{7,23},{8,24},{9,... | collective-permute-start | bytes 159752 | tf_op jit(solution)/shard_map/ppermute | solution.py:58
  12.6 0.3 collective-permute-start.5
  12.8 2.6 %interior.1 = (f32[3,24,16,128]{3,2,1,0:T(8,128)S(1)}, f32[3,24,16,128]{3,2,1,0:T(8,128)S(1)}, f32[6,10,40,128]{3,2,1,0:T(8,128)S(1)}, f32[3,3,10,40,128]{4,3,2,1,0:T(8,128)S(1)}) custom-call(f32[3,32,32,128]{3,2,1,0:T(8,128)S(1)} %copy-done, f32[32,32,128]{2,1,0:T(8,128)S(1)} %copy-done.1, f32[416,128]{1,0:T(8,128)S(1)} %collective-permute-done.ya, ...), custom_call_target="tpu_custom_call" | custom-call | flops 60000000 | bytes 6000000 | tf_op jit(solution)/shard_map/interior/pallas_call | solution.py:452
  15.4 0.0 collective-permute-done.2.xa
  15.5 0.0 collective-permute-done.3.xb
  15.5 0.0 collective-permute-done.4.za
  15.5 0.7 %collective-permute-done.5.zb = f32[13,8,128]{2,1,0:T(8,128)S(1)} collective-permute-done((f32[13,8,128]{2,1,0:T(8,128)S(1)}, f32[13,8,128]{2,1,0:T(8,128)S(1)}, u32[]{:S(2)}, u32[]{:S(2)}) %collective-permute-start.5) | collective-permute-done | bytes 53280 | tf_op jit(solution)/shard_map/ppermute | solution.py:58
  16.1 1.3 %edges.1 = (f32[3,8,32,128]{3,2,1,0:T(8,128)S(1)}, f32[3,8,32,128]{3,2,1,0:T(8,128)S(1)}) custom-call(f32[3,32,32,128]{3,2,1,0:T(8,128)S(1)} %copy-done, f32[416,128]{1,0:T(8,128)S(1)} %collective-permute-done.ya, f32[416,128]{1,0:T(8,128)S(1)} %collective-permute-done.1.yb, f32[13,32,128]{2,1,0:T(8,128)S(1)} %collective-permute-done.2.xa, ...), custom_call_target="tpu_custom_call" | custom-call | flops 20000000 | bytes 2000000 | tf_op jit(solution)/shard_map/edges/pallas_call | solution.py:526
  17.4 0.8 %pack.1 = f32[128,256]{1,0:T(8,128)S(1)} custom-call(bf16[128,1024]{1,0:T(8,128)(2,1)S(1)} %get-tuple-element.21.to_patch, f32[32,1024]{1,0:T(8,128)S(1)} %get-tuple-element.22.to_slot, f32[128,128]{1,0:T(8,128)S(1)} %get-tuple-element.23._.meta, f32[3,8,32,128]{3,2,1,0:T(8,128)S(1)} %get-tuple-element.35.outer, ...), custom_call_target="tpu_custom_call" | custom-call | tf_op jit(solution)/shard_map/pack/pallas_call | solution.py:566
  18.2 0.1 copy.7
  18.4 22.0 %all_to_all.11 = f32[128,1,256]{2,1,0:T(1,128)S(1)} all-to-all(f32[128,1,256]{2,1,0:T(1,128)S(1)} %copy.7), channel_id=1, replica_groups=mesh['gx'=8,'gy'=16] {'gx','gy'}, dimensions={0} | all-to-all | bytes 262144 | tf_op jit(solution)/shard_map/all_to_all | solution.py:668
  40.4 3.2 %gather.1 = (f32[3,32,32,128]{3,2,1,0:T(8,128)}, f32[1,3,64,64]{3,2,1,0:T(8,128)}) custom-call(f32[128,256]{1,0:T(8,128)S(1)} %bitcast.12, f32[3,24,16,128]{3,2,1,0:T(8,128)S(1)} %get-tuple-element.37.early, f32[3,24,16,128]{3,2,1,0:T(8,128)S(1)} %get-tuple-element.38.inner, f32[3,8,32,128]{3,2,1,0:T(8,128)S(1)} %get-tuple-element.39.outer), custom_call_target="tpu_custom_call" | custom-call | flops 400000000 | bytes 200000 | tf_op jit(solution)/shard_map/gather/pallas_call | solution.py:633
  (2 shorter events, 0.0 us)
Async XLA Ops:
  0.6 6.4 %copy-start = (f32[3,32,32,128]{3,2,1,0:T(8,128)S(1)}, f32[3,32,32,128]{3,2,1,0:T(8,128)}, u32[]{:S(2)}) copy-start(f32[3,32,32,128]{3,2,1,0:T(8,128)} %vs.7) | copy-start | bytes 4718596
  0.6 6.4 %copy-start.1 = (f32[32,32,128]{2,1,0:T(8,128)S(1)}, f32[32,32,128]{2,1,0:T(8,128)}, u32[]{:S(2)}) copy-start(f32[32,32,128]{2,1,0:T(8,128)} %c.5) | copy-start | bytes 1572868
  0.7 9.3 %copy-start.4 = (s32[1,1024,1]{1,2,0:T(1,128)S(1)}, s32[1,1024,1]{1,2,0:T(1,128)}, u32[]{:S(2)}) copy-start(s32[1,1024,1]{1,2,0:T(1,128)} %param.7) | copy-start | bytes 12292
  0.7 9.3 %copy-start.2 = (s32[1,1024,2]{1,2,0:T(2,128)S(1)}, s32[1,1024,2]{1,2,0:T(2,128)}, u32[]{:S(2)}) copy-start(s32[1,1024,2]{1,2,0:T(2,128)} %param.8) | copy-start | bytes 24580
  0.7 9.3 %copy-start.3 = (f32[1,1024,2]{1,2,0:T(2,128)S(1)}, f32[1,1024,2]{1,2,0:T(2,128)}, u32[]{:S(2)}) copy-start(f32[1,1024,2]{1,2,0:T(2,128)} %param.9) | copy-start | bytes 24580
  2.2 8.7 %collective-permute-start = (f32[416,128]{1,0:T(8,128)S(1)}, f32[416,128]{1,0:T(8,128)S(1)}, u32[]{:S(2)}, u32[]{:S(2)}) collective-permute-start(f32[416,128]{1,0:T(8,128)S(1)} %get-tuple-element.24), channel_id=1, source_target_pairs={{0,1},{1,0},{2,3},{3,2},{4,5},{5,4},{6,7},{7,6},{8,9},{9,8},{10,11... | collective-permute-start | bytes 638984 | tf_op jit(solution)/shard_map/ppermute | solution.py:58
  4.4 6.6 %collective-permute-start.1 = (f32[416,128]{1,0:T(8,128)S(1)}, f32[416,128]{1,0:T(8,128)S(1)}, u32[]{:S(2)}, u32[]{:S(2)}) collective-permute-start(f32[416,128]{1,0:T(8,128)S(1)} %get-tuple-element.25), channel_id=1, source_target_pairs={{0,16},{1,2},{2,1},{3,4},{4,3},{5,6},{6,5},{7,8},{8,7},{9,10},{10,... | collective-permute-start | bytes 638984 | tf_op jit(solution)/shard_map/ppermute | solution.py:58
  5.3 10.1 %collective-permute-start.2 = (f32[13,32,128]{2,1,0:T(8,128)S(1)}, f32[13,32,128]{2,1,0:T(8,128)S(1)}, u32[]{:S(2)}, u32[]{:S(2)}) collective-permute-start(f32[13,32,128]{2,1,0:T(8,128)S(1)} %get-tuple-element.26), channel_id=1, source_target_pairs={{0,16},{1,17},{2,18},{3,19},{4,20},{5,21},{6,22},{7,23},{8,24},{9,... | collective-permute-start | bytes 638984 | tf_op jit(solution)/shard_map/ppermute | solution.py:58
  5.3 10.1 %collective-permute-start.3 = (f32[13,32,128]{2,1,0:T(8,128)S(1)}, f32[13,32,128]{2,1,0:T(8,128)S(1)}, u32[]{:S(2)}, u32[]{:S(2)}) collective-permute-start(f32[13,32,128]{2,1,0:T(8,128)S(1)} %get-tuple-element.27), channel_id=1, source_target_pairs={{0,112},{1,113},{2,114},{3,115},{4,116},{5,117},{6,118},{7,119},{8... | collective-permute-start | bytes 638984 | tf_op jit(solution)/shard_map/ppermute | solution.py:58
  11.1 4.4 %collective-permute-start.4 = (f32[13,8,128]{2,1,0:T(8,128)S(1)}, f32[13,8,128]{2,1,0:T(8,128)S(1)}, u32[]{:S(2)}, u32[]{:S(2)}) collective-permute-start(f32[13,8,128]{2,1,0:T(8,128)S(1)} %get-tuple-element.29), channel_id=1, source_target_pairs={{0,16},{1,17},{2,18},{3,19},{4,20},{5,21},{6,22},{7,23},{8,24},{9,... | collective-permute-start | bytes 159752 | tf_op jit(solution)/shard_map/ppermute | solution.py:58
  12.6 3.6 %collective-permute-start.5 = (f32[13,8,128]{2,1,0:T(8,128)S(1)}, f32[13,8,128]{2,1,0:T(8,128)S(1)}, u32[]{:S(2)}, u32[]{:S(2)}) collective-permute-start(f32[13,8,128]{2,1,0:T(8,128)S(1)} %get-tuple-element.30), channel_id=1, source_target_pairs={{0,112},{1,113},{2,114},{3,115},{4,116},{5,117},{6,118},{7,119},{8... | collective-permute-start | bytes 159752 | tf_op jit(solution)/shard_map/ppermute | solution.py:58

commit v6 on v5

--- a/solution.py
+++ b/solution.py
@@ -55,7 +55,8 @@
             first.append((here, near[0] * count_y + near[1]))
             second.append((here, far[0] * count_y + far[1]))
     both = ("gx", "gy")
-    return lax.ppermute(one, both, first), lax.ppermute(two, both, second)
+    far = lax.ppermute(two, both, second)
+    return lax.ppermute(one, both, first), far
 
 
 def at_end(axis):
@@ -171,7 +172,7 @@
     return jnp.where(even == before, two[rows], one[rows])
 
 
-def corner_kernel(ya, yb, _, __, one, two):
+def corner_kernel(yb, ya, _, __, one, two):
     even_x = is_even("gx")
     even_y = is_even("gy")
     inside_x = jnp.where(at_end("gx"), 0.0, 1.0)
@@ -199,7 +200,7 @@
         out_specs=(vmem(), vmem()),
         compiler_params=params(),
         name="corners",
-    )(ya, yb, meta, early)
+    )(yb, ya, meta, early)
 
 
 def route_kernel(patch, spans, par, to_patch, to_slot, meta):
@@ -413,7 +414,7 @@
 
 
 def interior_kernel(
-    vs, c, ya, yb, planes, cubes, out, surface, keep, keep3, stiff, rest, rest3, halo,
+    vs, c, yb, ya, planes, cubes, out, surface, keep, keep3, stiff, rest, rest3, halo,
 ):
     even_y = is_even("gy")
     for x in range(NX):
@@ -468,11 +469,11 @@
         compiler_params=params(),
         cost_estimate=pl.CostEstimate(flops=60_000_000, bytes_accessed=6_000_000, transcendentals=0),
         name="interior",
-    )(vs, c, ya, yb, planes, cubes)
+    )(vs, c, yb, ya, planes, cubes)
 
 
 def edge_kernel(
-    vs, ya, yb, xa, xb, za, zb, keep, keep3, out, surface, fresh, fresh3,
+    vs, yb, ya, xb, xa, zb, za, keep, keep3, out, surface, fresh, fresh3,
 ):
     even_x = is_even("gx")
     even_y = is_even("gy")
@@ -535,7 +536,7 @@
         compiler_params=params(),
         cost_estimate=pl.CostEstimate(flops=20_000_000, bytes_accessed=2_000_000, transcendentals=0),
         name="edges",
-    )(vs, ya, yb, xa, xb, za, zb, keep, keep3)
+    )(vs, yb, ya, xb, xa, zb, za, keep, keep3)
 
 
 def pack_kernel(to_patch, to_slot, meta, outer, inner, early, send):

time: 43.7 us -> 42.5 us (0.973)
  blocking collectives: 22 us -> 20.2 us
  starting transfers between devices: 6.54 us -> 7.78 us
  waiting for transfers between devices: 0.67 us -> 0.02 us
    all_to_all x1, blocking collectives: 22 us -> 20.2 us  [body(): got = lax.all_to_all(send, ('gx', 'gy'), 0, 0, tiled=True)]
    ppermute x6, starting transfers between devices: 6.54 us -> 7.78 us  [the longest x3 4.97 us: exchange(): far = lax.ppermute(two, both, second)]
    ppermute x6, waiting for transfers between devices: 0.67 us -> 0.02 us  [the longest x3 0.01 us: exchange(): far = lax.ppermute(two, both, second)]
  transfers between devices with their start and end apart: 6 -> 6, of which waited for: 1 -> 0; matrix products, arithmetic and copies ran while one was open for 0% -> 0% of each run, Pallas kernels for 15% -> 16%
where the time goes in v6:
time: 42.5 us; the launch traced here: 42.4 us
  blocking collectives  20.2 us (48%)
  Pallas kernels  13.5 us (32%)
  starting transfers between devices  7.78 us (18%)
  between operations  0.8 us (2%)
    all_to_all x1, blocking collectives, body(): got = lax.all_to_all(send, ('gx', 'gy'), 0, 0, tiled=True)  20.2 us
    ppermute x3, starting transfers between devices, exchange(): far = lax.ppermute(two, both, second)  4.97 us
    pallas_call x1, Pallas kernels, gather(): pl.pallas_call(gather_kernel, out_shape=(jax.ShapeDtypeStruct((3, NX, NY,...  3.23 us
    pallas_call x1, Pallas kernels, ahead(): pl.pallas_call(ahead_kernel, out_shape=(rows, rows, jax.ShapeDtypeStruct(...  2.93 us
    ppermute x3, starting transfers between devices, exchange(): return (lax.ppermute(one, both, first), far)  2.81 us
    pallas_call x1, Pallas kernels, interior(): pl.pallas_call(interior_kernel, out_shape=(rows, rows, jax.ShapeDtypeStru...  2.62 us
    pallas_call x1, Pallas kernels, messages(): pl.pallas_call(message_kernel, out_shape=(y_shape, y_shape, x_shape, x_sh...  1.55 us
    pallas_call x1, Pallas kernels, edges(): pl.pallas_call(edge_kernel, out_shape=(rows, rows), in_specs=[vmem()] * 9...  1.28 us
  transfers between devices with their start and end apart: 6, of which 0 were waited for; matrix products, arithmetic and copies ran while one was open for 0% of the time, Pallas kernels for 16%

profile of v6, /device:TPU:1, one launch (start us, length us, event | category | flops | bytes accessed | tf_op | source)
XLA Modules:
  0.0 42.4 jit_solution(8105388366020884301)
XLA Ops:
  0.6 0.0 copy-start
  0.6 0.0 copy-start.1
  0.7 0.0 copy-start.4
  0.7 0.0 copy-start.2
  0.7 0.0 copy-start.3
  0.7 1.6 %messages.1 = (f32[416,128]{1,0:T(8,128)S(1)}, f32[416,128]{1,0:T(8,128)S(1)}, f32[13,32,128]{2,1,0:T(8,128)S(1)}, f32[13,32,128]{2,1,0:T(8,128)S(1)}) custom-call(f32[3,32,32,128]{3,2,1,0:T(8,128)} %vs.7, f32[32,32,128]{2,1,0:T(8,128)} %c.5), custom_call_target="tpu_custom_call" | custom-call | tf_op jit(solution)/shard_map/messages/pallas_call | solution.py:153
  2.2 1.5 %collective-permute-start = (f32[416,128]{1,0:T(8,128)S(1)}, f32[416,128]{1,0:T(8,128)S(1)}, u32[]{:S(2)}, u32[]{:S(2)}) collective-permute-start(f32[416,128]{1,0:T(8,128)S(1)} %get-tuple-element.24), channel_id=1, source_target_pairs={{0,16},{1,2},{2,1},{3,4},{4,3},{5,6},{6,5},{7,8},{8,7},{9,10},{10,... | collective-permute-start | bytes 638984 | tf_op jit(solution)/shard_map/ppermute | solution.py:58
  3.8 1.8 %collective-permute-start.1 = (f32[416,128]{1,0:T(8,128)S(1)}, f32[416,128]{1,0:T(8,128)S(1)}, u32[]{:S(2)}, u32[]{:S(2)}) collective-permute-start(f32[416,128]{1,0:T(8,128)S(1)} %get-tuple-element.25), channel_id=1, source_target_pairs={{0,1},{1,0},{2,3},{3,2},{4,5},{5,4},{6,7},{7,6},{8,9},{9,8},{10,11... | collective-permute-start | bytes 638984 | tf_op jit(solution)/shard_map/ppermute | solution.py:59
  5.6 2.4 %collective-permute-start.2 = (f32[13,32,128]{2,1,0:T(8,128)S(1)}, f32[13,32,128]{2,1,0:T(8,128)S(1)}, u32[]{:S(2)}, u32[]{:S(2)}) collective-permute-start(f32[13,32,128]{2,1,0:T(8,128)S(1)} %get-tuple-element.26), channel_id=1, source_target_pairs={{0,112},{1,113},{2,114},{3,115},{4,116},{5,117},{6,118},{7,119},{8... | collective-permute-start | bytes 638984 | tf_op jit(solution)/shard_map/ppermute | solution.py:58
  8.0 0.7 %collective-permute-start.3 = (f32[13,32,128]{2,1,0:T(8,128)S(1)}, f32[13,32,128]{2,1,0:T(8,128)S(1)}, u32[]{:S(2)}, u32[]{:S(2)}) collective-permute-start(f32[13,32,128]{2,1,0:T(8,128)S(1)} %get-tuple-element.27), channel_id=1, source_target_pairs={{0,16},{1,17},{2,18},{3,19},{4,20},{5,21},{6,22},{7,23},{8,24},{9,... | collective-permute-start | bytes 638984 | tf_op jit(solution)/shard_map/ppermute | solution.py:59
  8.7 0.0 copy-done
  8.7 0.0 copy-done.1
  8.7 2.9 %ahead.1 = (f32[3,24,16,128]{3,2,1,0:T(8,128)S(1)}, f32[3,24,16,128]{3,2,1,0:T(8,128)S(1)}, f32[5,30,32,128]{3,2,1,0:T(8,128)S(1)}, f32[3,3,30,32,128]{4,3,2,1,0:T(8,128)S(1)}) custom-call(f32[3,32,32,128]{3,2,1,0:T(8,128)S(1)} %copy-done, f32[32,32,128]{2,1,0:T(8,128)S(1)} %copy-done.1), custom_call_target="tpu_custom_call" | custom-call | flops 60000000 | bytes 6000000 | tf_op jit(solution)/shard_map/ahead/pallas_call | solution.py:400
  11.7 0.0 copy-done.4
  11.7 0.0 copy-done.2
  11.7 0.0 copy-done.3
  11.7 1.0 %route.1 = (bf16[128,1024]{1,0:T(8,128)(2,1)S(1)}, f32[32,1024]{1,0:T(8,128)S(1)}, f32[128,128]{1,0:T(8,128)S(1)}) custom-call(s32[1,1024]{1,0:T(1,128)S(1)} %bitcast.15, s32[2,1024]{1,0:T(2,128)S(1)} %bitcast.13, f32[2,1024]{1,0:T(2,128)S(1)} %bitcast.14), custom_call_target="tpu_custom_call" | custom-call | flops 400000000 | bytes 2000000 | tf_op jit(solution)/shard_map/route/pallas_call | solution.py:239
  12.7 0.0 collective-permute-done.yb
  12.7 0.0 collective-permute-done.1.ya
  12.8 1.0 %collective-permute-start.4 = (f32[13,8,128]{2,1,0:T(8,128)S(1)}, f32[13,8,128]{2,1,0:T(8,128)S(1)}, u32[]{:S(2)}, u32[]{:S(2)}) collective-permute-start(f32[13,8,128]{2,1,0:T(8,128)S(1)} %get-tuple-element.29), channel_id=1, source_target_pairs={{0,112},{1,113},{2,114},{3,115},{4,116},{5,117},{6,118},{7,119},{8... | collective-permute-start | bytes 159752 | tf_op jit(solution)/shard_map/ppermute | solution.py:58
  13.8 0.3 collective-permute-start.5
  14.1 2.6 %interior.1 = (f32[3,24,16,128]{3,2,1,0:T(8,128)S(1)}, f32[3,24,16,128]{3,2,1,0:T(8,128)S(1)}, f32[6,10,40,128]{3,2,1,0:T(8,128)S(1)}, f32[3,3,10,40,128]{4,3,2,1,0:T(8,128)S(1)}) custom-call(f32[3,32,32,128]{3,2,1,0:T(8,128)S(1)} %copy-done, f32[32,32,128]{2,1,0:T(8,128)S(1)} %copy-done.1, f32[416,128]{1,0:T(8,128)S(1)} %collective-permute-done.yb, ...), custom_call_target="tpu_custom_call" | custom-call | flops 60000000 | bytes 6000000 | tf_op jit(solution)/shard_map/interior/pallas_call | solution.py:453
  16.7 0.0 collective-permute-done.2.xb
  16.7 0.0 collective-permute-done.3.xa
  16.7 0.0 collective-permute-done.4.zb
  16.7 0.0 collective-permute-done.5.za
  16.7 1.3 %edges.1 = (f32[3,8,32,128]{3,2,1,0:T(8,128)S(1)}, f32[3,8,32,128]{3,2,1,0:T(8,128)S(1)}) custom-call(f32[3,32,32,128]{3,2,1,0:T(8,128)S(1)} %copy-done, f32[416,128]{1,0:T(8,128)S(1)} %collective-permute-done.yb, f32[416,128]{1,0:T(8,128)S(1)} %collective-permute-done.1.ya, f32[13,32,128]{2,1,0:T(8,128)S(1)} %collective-permute-done.2.xb, ...), custom_call_target="tpu_custom_call" | custom-call | flops 20000000 | bytes 2000000 | tf_op jit(solution)/shard_map/edges/pallas_call | solution.py:527
  18.0 0.8 %pack.1 = f32[128,256]{1,0:T(8,128)S(1)} custom-call(bf16[128,1024]{1,0:T(8,128)(2,1)S(1)} %get-tuple-element.21.to_patch, f32[32,1024]{1,0:T(8,128)S(1)} %get-tuple-element.22.to_slot, f32[128,128]{1,0:T(8,128)S(1)} %get-tuple-element.23._.meta, f32[3,8,32,128]{3,2,1,0:T(8,128)S(1)} %get-tuple-element.35.outer, ...), custom_call_target="tpu_custom_call" | custom-call | tf_op jit(solution)/shard_map/pack/pallas_call | solution.py:567
  18.8 0.1 copy.7
  19.0 20.2 %all_to_all.11 = f32[128,1,256]{2,1,0:T(1,128)S(1)} all-to-all(f32[128,1,256]{2,1,0:T(1,128)S(1)} %copy.7), channel_id=1, replica_groups=mesh['gx'=8,'gy'=16] {'gx','gy'}, dimensions={0} | all-to-all | bytes 262144 | tf_op jit(solution)/shard_map/all_to_all | solution.py:669
  39.2 3.2 %gather.1 = (f32[3,32,32,128]{3,2,1,0:T(8,128)}, f32[1,3,64,64]{3,2,1,0:T(8,128)}) custom-call(f32[128,256]{1,0:T(8,128)S(1)} %bitcast.12, f32[3,24,16,128]{3,2,1,0:T(8,128)S(1)} %get-tuple-element.37.early, f32[3,24,16,128]{3,2,1,0:T(8,128)S(1)} %get-tuple-element.38.inner, f32[3,8,32,128]{3,2,1,0:T(8,128)S(1)} %get-tuple-element.39.outer), custom_call_target="tpu_custom_call" | custom-call | flops 400000000 | bytes 200000 | tf_op jit(solution)/shard_map/gather/pallas_call | solution.py:634
  (2 shorter events, 0.0 us)
Async XLA Ops:
  0.6 8.1 %copy-start = (f32[3,32,32,128]{3,2,1,0:T(8,128)S(1)}, f32[3,32,32,128]{3,2,1,0:T(8,128)}, u32[]{:S(2)}) copy-start(f32[3,32,32,128]{3,2,1,0:T(8,128)} %vs.7) | copy-start | bytes 4718596
  0.6 8.1 %copy-start.1 = (f32[32,32,128]{2,1,0:T(8,128)S(1)}, f32[32,32,128]{2,1,0:T(8,128)}, u32[]{:S(2)}) copy-start(f32[32,32,128]{2,1,0:T(8,128)} %c.5) | copy-start | bytes 1572868
  0.7 11.0 %copy-start.4 = (s32[1,1024,1]{1,2,0:T(1,128)S(1)}, s32[1,1024,1]{1,2,0:T(1,128)}, u32[]{:S(2)}) copy-start(s32[1,1024,1]{1,2,0:T(1,128)} %param.7) | copy-start | bytes 12292
  0.7 11.0 %copy-start.2 = (s32[1,1024,2]{1,2,0:T(2,128)S(1)}, s32[1,1024,2]{1,2,0:T(2,128)}, u32[]{:S(2)}) copy-start(s32[1,1024,2]{1,2,0:T(2,128)} %param.8) | copy-start | bytes 24580
  0.7 11.0 %copy-start.3 = (f32[1,1024,2]{1,2,0:T(2,128)S(1)}, f32[1,1024,2]{1,2,0:T(2,128)}, u32[]{:S(2)}) copy-start(f32[1,1024,2]{1,2,0:T(2,128)} %param.9) | copy-start | bytes 24580
  2.2 10.5 %collective-permute-start = (f32[416,128]{1,0:T(8,128)S(1)}, f32[416,128]{1,0:T(8,128)S(1)}, u32[]{:S(2)}, u32[]{:S(2)}) collective-permute-start(f32[416,128]{1,0:T(8,128)S(1)} %get-tuple-element.24), channel_id=1, source_target_pairs={{0,16},{1,2},{2,1},{3,4},{4,3},{5,6},{6,5},{7,8},{8,7},{9,10},{10,... | collective-permute-start | bytes 638984 | tf_op jit(solution)/shard_map/ppermute | solution.py:58
  3.8 9.0 %collective-permute-start.1 = (f32[416,128]{1,0:T(8,128)S(1)}, f32[416,128]{1,0:T(8,128)S(1)}, u32[]{:S(2)}, u32[]{:S(2)}) collective-permute-start(f32[416,128]{1,0:T(8,128)S(1)} %get-tuple-element.25), channel_id=1, source_target_pairs={{0,1},{1,0},{2,3},{3,2},{4,5},{5,4},{6,7},{7,6},{8,9},{9,8},{10,11... | collective-permute-start | bytes 638984 | tf_op jit(solution)/shard_map/ppermute | solution.py:59
  5.6 11.1 %collective-permute-start.2 = (f32[13,32,128]{2,1,0:T(8,128)S(1)}, f32[13,32,128]{2,1,0:T(8,128)S(1)}, u32[]{:S(2)}, u32[]{:S(2)}) collective-permute-start(f32[13,32,128]{2,1,0:T(8,128)S(1)} %get-tuple-element.26), channel_id=1, source_target_pairs={{0,112},{1,113},{2,114},{3,115},{4,116},{5,117},{6,118},{7,119},{8... | collective-permute-start | bytes 638984 | tf_op jit(solution)/shard_map/ppermute | solution.py:58
  8.0 8.7 %collective-permute-start.3 = (f32[13,32,128]{2,1,0:T(8,128)S(1)}, f32[13,32,128]{2,1,0:T(8,128)S(1)}, u32[]{:S(2)}, u32[]{:S(2)}) collective-permute-start(f32[13,32,128]{2,1,0:T(8,128)S(1)} %get-tuple-element.27), channel_id=1, source_target_pairs={{0,16},{1,17},{2,18},{3,19},{4,20},{5,21},{6,22},{7,23},{8,24},{9,... | collective-permute-start | bytes 638984 | tf_op jit(solution)/shard_map/ppermute | solution.py:59
  12.8 3.9 %collective-permute-start.4 = (f32[13,8,128]{2,1,0:T(8,128)S(1)}, f32[13,8,128]{2,1,0:T(8,128)S(1)}, u32[]{:S(2)}, u32[]{:S(2)}) collective-permute-start(f32[13,8,128]{2,1,0:T(8,128)S(1)} %get-tuple-element.29), channel_id=1, source_target_pairs={{0,112},{1,113},{2,114},{3,115},{4,116},{5,117},{6,118},{7,119},{8... | collective-permute-start | bytes 159752 | tf_op jit(solution)/shard_map/ppermute | solution.py:58
  13.8 2.9 %collective-permute-start.5 = (f32[13,8,128]{2,1,0:T(8,128)S(1)}, f32[13,8,128]{2,1,0:T(8,128)S(1)}, u32[]{:S(2)}, u32[]{:S(2)}) collective-permute-start(f32[13,8,128]{2,1,0:T(8,128)S(1)} %get-tuple-element.30), channel_id=1, source_target_pairs={{0,16},{1,17},{2,18},{3,19},{4,20},{5,21},{6,22},{7,23},{8,24},{9,... | collective-permute-start | bytes 159752 | tf_op jit(solution)/shard_map/ppermute | solution.py:59

commit v7 on v6

--- a/solution.py
+++ b/solution.py
@@ -172,7 +172,7 @@
     return jnp.where(even == before, two[rows], one[rows])
 
 
-def corner_kernel(yb, ya, _, __, one, two):
+def corner_kernel(yb, ya, _, one, two):
     even_x = is_even("gx")
     even_y = is_even("gy")
     inside_x = jnp.where(at_end("gx"), 0.0, 1.0)
@@ -191,16 +191,16 @@
             two[i, spot] = jnp.where(even_x, low, high) * inside_x
 
 
-def corners(ya, yb, meta, early):
+def corners(ya, yb, early):
     shape = jax.ShapeDtypeStruct((13, 8, NZ), F32)
     return pl.pallas_call(
         corner_kernel,
         out_shape=(shape, shape),
-        in_specs=[vmem()] * 4,
+        in_specs=[vmem()] * 3,
         out_specs=(vmem(), vmem()),
         compiler_params=params(),
         name="corners",
-    )(yb, ya, meta, early)
+    )(yb, ya, early)
 
 
 def route_kernel(patch, spans, par, to_patch, to_slot, meta):
@@ -662,7 +662,7 @@
         patch_of_row.reshape(1, ROWS), knot_spans[0].T, span_params[0].T
     )
     early, early_surface, planes, cubes = ahead(volume_sens, stiffness)
-    za, zb = exchange(True, *corners(ya, yb, meta, early_surface))
+    za, zb = exchange(True, *corners(ya, yb, early_surface))
     inner, inner_surface, keep, keep3 = interior(volume_sens, stiffness, ya, yb, planes, cubes)
     outer, outer_surface = edges(volume_sens, ya, yb, xa, xb, za, zb, keep, keep3)
     send = pack(to_patch, to_slot, meta, outer_surface, inner_surface, early_surface)

time: 42.5 us -> 43.6 us (1.026)
  blocking collectives: 20.2 us -> 20.7 us
  starting transfers between devices: 7.78 us -> 8.25 us
    all_to_all x1, blocking collectives: 20.2 us -> 20.7 us  [body(): got = lax.all_to_all(send, ('gx', 'gy'), 0, 0, tiled=True)]
  transfers between devices with their start and end apart: 6 -> 6, of which waited for: 0 -> 0; matrix products, arithmetic and copies ran while one was open for 0% -> 0% of each run, Pallas kernels for 16% -> 15%
where the time goes in v7:
time: 43.6 us; the launch traced here: 43.4 us
  blocking collectives  20.7 us (47%)
  Pallas kernels  13.5 us (31%)
  starting transfers between devices  8.25 us (19%)
  between operations  0.78 us (2%)
    all_to_all x1, blocking collectives, body(): got = lax.all_to_all(send, ('gx', 'gy'), 0, 0, tiled=True)  20.7 us
    ppermute x3, starting transfers between devices, exchange(): far = lax.ppermute(two, both, second)  5.28 us
    pallas_call x1, Pallas kernels, gather(): pl.pallas_call(gather_kernel, out_shape=(jax.ShapeDtypeStruct((3, NX, NY,...  3.23 us
    ppermute x3, starting transfers between devices, exchange(): return (lax.ppermute(one, both, first), far)  2.97 us
    pallas_call x1, Pallas kernels, ahead(): pl.pallas_call(ahead_kernel, out_shape=(rows, rows, jax.ShapeDtypeStruct(...  2.93 us
    pallas_call x1, Pallas kernels, interior(): pl.pallas_call(interior_kernel, out_shape=(rows, rows, jax.ShapeDtypeStru...  2.62 us
    pallas_call x1, Pallas kernels, messages(): pl.pallas_call(message_kernel, out_shape=(y_shape, y_shape, x_shape, x_sh...  1.56 us
    pallas_call x1, Pallas kernels, edges(): pl.pallas_call(edge_kernel, out_shape=(rows, rows), in_specs=[vmem()] * 9...  1.28 us
  transfers between devices with their start and end apart: 6, of which 0 were waited for; matrix products, arithmetic and copies ran while one was open for 0% of the time, Pallas kernels for 15%

profile of v7, /device:TPU:1, one launch (start us, length us, event | category | flops | bytes accessed | tf_op | source)
XLA Modules:
  0.0 43.4 jit_solution(4696734252893610675)
XLA Ops:
  0.6 0.0 copy-start
  0.6 0.0 copy-start.1
  0.6 1.6 %messages.1 = (f32[416,128]{1,0:T(8,128)S(1)}, f32[416,128]{1,0:T(8,128)S(1)}, f32[13,32,128]{2,1,0:T(8,128)S(1)}, f32[13,32,128]{2,1,0:T(8,128)S(1)}) custom-call(f32[3,32,32,128]{3,2,1,0:T(8,128)} %vs.7, f32[32,32,128]{2,1,0:T(8,128)} %c.5), custom_call_target="tpu_custom_call" | custom-call | tf_op jit(solution)/shard_map/messages/pallas_call | solution.py:153
  2.2 0.0 copy-start.2
  2.2 0.0 copy-start.3
  2.2 0.0 copy-start.4
  2.2 1.5 %collective-permute-start = (f32[416,128]{1,0:T(8,128)S(1)}, f32[416,128]{1,0:T(8,128)S(1)}, u32[]{:S(2)}, u32[]{:S(2)}) collective-permute-start(f32[416,128]{1,0:T(8,128)S(1)} %get-tuple-element.24), channel_id=1, source_target_pairs={{0,16},{1,2},{2,1},{3,4},{4,3},{5,6},{6,5},{7,8},{8,7},{9,10},{10,... | collective-permute-start | bytes 638984 | tf_op jit(solution)/shard_map/ppermute | solution.py:58
  3.8 1.8 %collective-permute-start.1 = (f32[416,128]{1,0:T(8,128)S(1)}, f32[416,128]{1,0:T(8,128)S(1)}, u32[]{:S(2)}, u32[]{:S(2)}) collective-permute-start(f32[416,128]{1,0:T(8,128)S(1)} %get-tuple-element.25), channel_id=1, source_target_pairs={{0,1},{1,0},{2,3},{3,2},{4,5},{5,4},{6,7},{7,6},{8,9},{9,8},{10,11... | collective-permute-start | bytes 638984 | tf_op jit(solution)/shard_map/ppermute | solution.py:59
  5.6 2.4 %collective-permute-start.2 = (f32[13,32,128]{2,1,0:T(8,128)S(1)}, f32[13,32,128]{2,1,0:T(8,128)S(1)}, u32[]{:S(2)}, u32[]{:S(2)}) collective-permute-start(f32[13,32,128]{2,1,0:T(8,128)S(1)} %get-tuple-element.26), channel_id=1, source_target_pairs={{0,112},{1,113},{2,114},{3,115},{4,116},{5,117},{6,118},{7,119},{8... | collective-permute-start | bytes 638984 | tf_op jit(solution)/shard_map/ppermute | solution.py:58
  8.0 0.7 %collective-permute-start.3 = (f32[13,32,128]{2,1,0:T(8,128)S(1)}, f32[13,32,128]{2,1,0:T(8,128)S(1)}, u32[]{:S(2)}, u32[]{:S(2)}) collective-permute-start(f32[13,32,128]{2,1,0:T(8,128)S(1)} %get-tuple-element.27), channel_id=1, source_target_pairs={{0,16},{1,17},{2,18},{3,19},{4,20},{5,21},{6,22},{7,23},{8,24},{9,... | collective-permute-start | bytes 638984 | tf_op jit(solution)/shard_map/ppermute | solution.py:59
  8.7 0.0 copy-done
  8.7 0.0 copy-done.1
  8.7 2.9 %ahead.1 = (f32[3,24,16,128]{3,2,1,0:T(8,128)S(1)}, f32[3,24,16,128]{3,2,1,0:T(8,128)S(1)}, f32[5,30,32,128]{3,2,1,0:T(8,128)S(1)}, f32[3,3,30,32,128]{4,3,2,1,0:T(8,128)S(1)}) custom-call(f32[3,32,32,128]{3,2,1,0:T(8,128)S(1)} %copy-done, f32[32,32,128]{2,1,0:T(8,128)S(1)} %copy-done.1), custom_call_target="tpu_custom_call" | custom-call | flops 60000000 | bytes 6000000 | tf_op jit(solution)/shard_map/ahead/pallas_call | solution.py:400
  11.7 0.0 collective-permute-done.yb
  11.7 0.0 collective-permute-done.1.ya
  11.7 1.4 %collective-permute-start.4 = (f32[13,8,128]{2,1,0:T(8,128)S(1)}, f32[13,8,128]{2,1,0:T(8,128)S(1)}, u32[]{:S(2)}, u32[]{:S(2)}) collective-permute-start(f32[13,8,128]{2,1,0:T(8,128)S(1)} %get-tuple-element.29), channel_id=1, source_target_pairs={{0,112},{1,113},{2,114},{3,115},{4,116},{5,117},{6,118},{7,119},{8... | collective-permute-start | bytes 159752 | tf_op jit(solution)/shard_map/ppermute | solution.py:58
  13.1 0.4 collective-permute-start.5
  13.5 0.0 copy-done.2
  13.5 0.0 copy-done.3
  13.5 0.0 copy-done.4
  13.5 1.0 %route.1 = (bf16[128,1024]{1,0:T(8,128)(2,1)S(1)}, f32[32,1024]{1,0:T(8,128)S(1)}, f32[128,128]{1,0:T(8,128)S(1)}) custom-call(s32[1,1024]{1,0:T(1,128)S(1)} %bitcast.15, s32[2,1024]{1,0:T(2,128)S(1)} %bitcast.13, f32[2,1024]{1,0:T(2,128)S(1)} %bitcast.14), custom_call_target="tpu_custom_call" | custom-call | flops 400000000 | bytes 2000000 | tf_op jit(solution)/shard_map/route/pallas_call | solution.py:239
  14.5 2.6 %interior.1 = (f32[3,24,16,128]{3,2,1,0:T(8,128)S(1)}, f32[3,24,16,128]{3,2,1,0:T(8,128)S(1)}, f32[6,10,40,128]{3,2,1,0:T(8,128)S(1)}, f32[3,3,10,40,128]{4,3,2,1,0:T(8,128)S(1)}) custom-call(f32[3,32,32,128]{3,2,1,0:T(8,128)S(1)} %copy-done, f32[32,32,128]{2,1,0:T(8,128)S(1)} %copy-done.1, f32[416,128]{1,0:T(8,128)S(1)} %collective-permute-done.yb, ...), custom_call_target="tpu_custom_call" | custom-call | flops 60000000 | bytes 6000000 | tf_op jit(solution)/shard_map/interior/pallas_call | solution.py:453
  17.2 0.0 collective-permute-done.2.xb
  17.2 0.0 collective-permute-done.3.xa
  17.2 0.0 collective-permute-done.4.zb
  17.2 0.0 collective-permute-done.5.za
  17.2 1.3 %edges.1 = (f32[3,8,32,128]{3,2,1,0:T(8,128)S(1)}, f32[3,8,32,128]{3,2,1,0:T(8,128)S(1)}) custom-call(f32[3,32,32,128]{3,2,1,0:T(8,128)S(1)} %copy-done, f32[416,128]{1,0:T(8,128)S(1)} %collective-permute-done.yb, f32[416,128]{1,0:T(8,128)S(1)} %collective-permute-done.1.ya, f32[13,32,128]{2,1,0:T(8,128)S(1)} %collective-permute-done.2.xb, ...), custom_call_target="tpu_custom_call" | custom-call | flops 20000000 | bytes 2000000 | tf_op jit(solution)/shard_map/edges/pallas_call | solution.py:527
  18.5 0.8 %pack.1 = f32[128,256]{1,0:T(8,128)S(1)} custom-call(bf16[128,1024]{1,0:T(8,128)(2,1)S(1)} %get-tuple-element.21.to_patch, f32[32,1024]{1,0:T(8,128)S(1)} %get-tuple-element.22.to_slot, f32[128,128]{1,0:T(8,128)S(1)} %get-tuple-element.23.meta, f32[3,8,32,128]{3,2,1,0:T(8,128)S(1)} %get-tuple-element.35.outer, ...), custom_call_target="tpu_custom_call" | custom-call | tf_op jit(solution)/shard_map/pack/pallas_call | solution.py:567
  19.3 0.1 copy.7
  19.5 20.7 %all_to_all.11 = f32[128,1,256]{2,1,0:T(1,128)S(1)} all-to-all(f32[128,1,256]{2,1,0:T(1,128)S(1)} %copy.7), channel_id=1, replica_groups=mesh['gx'=8,'gy'=16] {'gx','gy'}, dimensions={0} | all-to-all | bytes 262144 | tf_op jit(solution)/shard_map/all_to_all | solution.py:669
  40.2 3.2 %gather.1 = (f32[3,32,32,128]{3,2,1,0:T(8,128)}, f32[1,3,64,64]{3,2,1,0:T(8,128)}) custom-call(f32[128,256]{1,0:T(8,128)S(1)} %bitcast.12, f32[3,24,16,128]{3,2,1,0:T(8,128)S(1)} %get-tuple-element.37.early, f32[3,24,16,128]{3,2,1,0:T(8,128)S(1)} %get-tuple-element.38.inner, f32[3,8,32,128]{3,2,1,0:T(8,128)S(1)} %get-tuple-element.39.outer), custom_call_target="tpu_custom_call" | custom-call | flops 400000000 | bytes 200000 | tf_op jit(solution)/shard_map/gather/pallas_call | solution.py:634
  (2 shorter events, 0.0 us)
Async XLA Ops:
  0.6 8.1 %copy-start = (f32[3,32,32,128]{3,2,1,0:T(8,128)S(1)}, f32[3,32,32,128]{3,2,1,0:T(8,128)}, u32[]{:S(2)}) copy-start(f32[3,32,32,128]{3,2,1,0:T(8,128)} %vs.7) | copy-start | bytes 4718596
  0.6 8.1 %copy-start.1 = (f32[32,32,128]{2,1,0:T(8,128)S(1)}, f32[32,32,128]{2,1,0:T(8,128)}, u32[]{:S(2)}) copy-start(f32[32,32,128]{2,1,0:T(8,128)} %c.5) | copy-start | bytes 1572868
  2.2 11.3 %copy-start.2 = (s32[1,1024,2]{1,2,0:T(2,128)S(1)}, s32[1,1024,2]{1,2,0:T(2,128)}, u32[]{:S(2)}) copy-start(s32[1,1024,2]{1,2,0:T(2,128)} %param.8) | copy-start | bytes 24580
  2.2 11.3 %copy-start.3 = (f32[1,1024,2]{1,2,0:T(2,128)S(1)}, f32[1,1024,2]{1,2,0:T(2,128)}, u32[]{:S(2)}) copy-start(f32[1,1024,2]{1,2,0:T(2,128)} %param.9) | copy-start | bytes 24580
  2.2 11.3 %copy-start.4 = (s32[1,1024,1]{1,2,0:T(1,128)S(1)}, s32[1,1024,1]{1,2,0:T(1,128)}, u32[]{:S(2)}) copy-start(s32[1,1024,1]{1,2,0:T(1,128)} %param.7) | copy-start | bytes 12292
  2.2 9.4 %collective-permute-start = (f32[416,128]{1,0:T(8,128)S(1)}, f32[416,128]{1,0:T(8,128)S(1)}, u32[]{:S(2)}, u32[]{:S(2)}) collective-permute-start(f32[416,128]{1,0:T(8,128)S(1)} %get-tuple-element.24), channel_id=1, source_target_pairs={{0,16},{1,2},{2,1},{3,4},{4,3},{5,6},{6,5},{7,8},{8,7},{9,10},{10,... | collective-permute-start | bytes 638984 | tf_op jit(solution)/shard_map/ppermute | solution.py:58
  3.8 7.9 %collective-permute-start.1 = (f32[416,128]{1,0:T(8,128)S(1)}, f32[416,128]{1,0:T(8,128)S(1)}, u32[]{:S(2)}, u32[]{:S(2)}) collective-permute-start(f32[416,128]{1,0:T(8,128)S(1)} %get-tuple-element.25), channel_id=1, source_target_pairs={{0,1},{1,0},{2,3},{3,2},{4,5},{5,4},{6,7},{7,6},{8,9},{9,8},{10,11... | collective-permute-start | bytes 638984 | tf_op jit(solution)/shard_map/ppermute | solution.py:59
  5.6 11.6 %collective-permute-start.2 = (f32[13,32,128]{2,1,0:T(8,128)S(1)}, f32[13,32,128]{2,1,0:T(8,128)S(1)}, u32[]{:S(2)}, u32[]{:S(2)}) collective-permute-start(f32[13,32,128]{2,1,0:T(8,128)S(1)} %get-tuple-element.26), channel_id=1, source_target_pairs={{0,112},{1,113},{2,114},{3,115},{4,116},{5,117},{6,118},{7,119},{8... | collective-permute-start | bytes 638984 | tf_op jit(solution)/shard_map/ppermute | solution.py:58
  8.0 9.2 %collective-permute-start.3 = (f32[13,32,128]{2,1,0:T(8,128)S(1)}, f32[13,32,128]{2,1,0:T(8,128)S(1)}, u32[]{:S(2)}, u32[]{:S(2)}) collective-permute-start(f32[13,32,128]{2,1,0:T(8,128)S(1)} %get-tuple-element.27), channel_id=1, source_target_pairs={{0,16},{1,17},{2,18},{3,19},{4,20},{5,21},{6,22},{7,23},{8,24},{9,... | collective-permute-start | bytes 638984 | tf_op jit(solution)/shard_map/ppermute | solution.py:59
  11.7 5.4 %collective-permute-start.4 = (f32[13,8,128]{2,1,0:T(8,128)S(1)}, f32[13,8,128]{2,1,0:T(8,128)S(1)}, u32[]{:S(2)}, u32[]{:S(2)}) collective-permute-start(f32[13,8,128]{2,1,0:T(8,128)S(1)} %get-tuple-element.29), channel_id=1, source_target_pairs={{0,112},{1,113},{2,114},{3,115},{4,116},{5,117},{6,118},{7,119},{8... | collective-permute-start | bytes 159752 | tf_op jit(solution)/shard_map/ppermute | solution.py:58
  13.1 4.1 %collective-permute-start.5 = (f32[13,8,128]{2,1,0:T(8,128)S(1)}, f32[13,8,128]{2,1,0:T(8,128)S(1)}, u32[]{:S(2)}, u32[]{:S(2)}) collective-permute-start(f32[13,8,128]{2,1,0:T(8,128)S(1)} %get-tuple-element.30), channel_id=1, source_target_pairs={{0,16},{1,17},{2,18},{3,19},{4,20},{5,21},{6,22},{7,23},{8,24},{9,... | collective-permute-start | bytes 159752 | tf_op jit(solution)/shard_map/ppermute | solution.py:59
